TPU v7x, 32 devices: a whole 2x2x4 slice. The times are simulated.
32 devices in a mesh: group: 2 (over y), dp: 4 (over z), section: 2 (over x), mp: 2 (over core).
Axes of the slice: x: 2, y: 2, z: 4, core: 2. Of those that a mesh axis runs over, the one named last changes fastest.
Arguments:
- acts: bfloat16 [2, 1024, 8192], P('section', ('group', 'dp'), 'mp'), parts along dimension 1, may hold values from -7 to 7
- cotangent: bfloat16 [1024, 8192], P(('group', 'dp'), 'mp'), parts along dimension 0, may hold values from -7 to 7
- in_weight: bfloat16 [2, 512, 8192], P('section', 'dp', 'mp'), may hold values from -0.25 to 0.25
- out_weight: bfloat16 [2, 512, 8192], P('section', 'dp', 'mp'), may hold values from -0.0625 to 0.0625
- in_factor: bfloat16 [2, 64, 8192], P('section', None, 'mp'), may hold values from -0.0625 to 0.0625
- out_factor: bfloat16 [2, 64, 512], P('section'), may hold values from -0.25 to 0.25
- damping: float32 [2], P('section'), may hold values from 0.25 to 4
- lengths: int32 [8, 4], P(('group', 'dp')), parts along dimension 0, may hold values from 1 to 64, 128 in all within a row
Outputs:
- adjoints: bfloat16 [2, 1024, 8192], P('section', ('group', 'dp'), 'mp'), parts along dimension 1
- leverage: float32 [2, 32], P('section', ('group', 'dp')), parts along dimension 1
There are 2 independent parts, one for each index of `group`. A program takes and returns all parts, laid end to end along the dimension named above; an argument that names none is the same for every part. Nothing has to cross between parts.
Inputs may be any that keep to these rules, and one draw needn't show every extreme that they name: `lengths`: each row sums to 128, and its largest entry is exactly 64.
All inputs are finite; a program needn't handle non-finite values.
Results may differ from a plain program's by a relative error of at most 0.0054.
Values may be sent and summed in bfloat16 or wider, within the bound.
No kernel may reach another device: no remote copies, remote signals or barrier semaphores. Data moves between devices by JAX's collectives and lax.ppermute only.
A program may use at most 64 MiB of HBM per device.

v0:
```python
import jax
import jax.numpy as jnp
from jax import lax
from jax.sharding import PartitionSpec as P


def shifted(shard, axis, by):
    devices = lax.axis_size(axis)
    pairs = [(i, i + by) for i in range(devices) if 0 <= i + by < devices]
    return lax.ppermute(shard, axis, pairs)


def local(acts, cotangent, in_weight, out_weight, in_factor, out_factor, damping, lengths):
    sections = lax.axis_size("section")
    section_index = lax.axis_index("section")
    inputs = acts[0]
    tok_rows = cotangent.shape[0]
    examples = lengths.shape[1]
    columns = in_factor.shape[1] * out_factor.shape[1]
    u_full, v_full = (
        lax.all_gather(in_weight[0], "dp", axis=0, tiled=True),
        lax.all_gather(out_weight[0], "dp", axis=0, tiled=True),
    )
    adjoint_now = cotangent
    kept_rank = jnp.zeros((tok_rows, v_full.shape[0]), jnp.bfloat16)
    kept_adjoint = jnp.zeros_like(cotangent)
    for turn in range(sections):
        partial_rank = lax.dot_general(
            adjoint_now, v_full, (((1,), (1,)), ((), ())), preferred_element_type=jnp.float32
        )
        own_half = lax.psum_scatter(partial_rank, "mp", scatter_dimension=1, tiled=True).astype(
            jnp.bfloat16
        )
        rank_grad = lax.all_gather(own_half, "mp", axis=1, tiled=True)
        new_adjoint = (
            adjoint_now.astype(jnp.float32)
            + jnp.dot(rank_grad, u_full, preferred_element_type=jnp.float32)
        ).astype(jnp.bfloat16)
        active = section_index == sections - 1 - turn
        kept_rank = jnp.where(active, rank_grad, kept_rank)
        kept_adjoint = jnp.where(active, new_adjoint, kept_adjoint)
        if turn + 1 < sections:
            adjoint_now = shifted(new_adjoint, "section", -1)
    out_proj = lax.dot_general(
        kept_rank, out_factor[0], (((1,), (1,)), ((), ())), preferred_element_type=jnp.float32
    )
    in_part = lax.dot_general(
        inputs, in_factor[0], (((1,), (1,)), ((), ())), preferred_element_type=jnp.float32
    )
    in_proj = lax.psum(in_part.astype(jnp.bfloat16), "mp").astype(jnp.float32)
    ends = jnp.cumsum(lengths[0])
    positions = jnp.arange(tok_rows, dtype=jnp.int32)
    doc_index = jnp.sum((positions[:, None] >= ends[None, :]).astype(jnp.int32), axis=1)
    member = (doc_index[:, None] == jnp.arange(examples, dtype=jnp.int32)[None, :]).astype(
        jnp.float32
    )
    local_rows = jnp.einsum(
        "te,to,ti->eoi", member, out_proj, in_proj, precision=lax.Precision.HIGHEST
    ).reshape(examples, columns)
    every_row = lax.all_gather(local_rows.astype(jnp.bfloat16), "dp", axis=0, tiled=True).astype(
        local_rows.dtype
    )
    kernel = jnp.dot(every_row, every_row.T, precision=lax.Precision.HIGHEST)
    docs_all = kernel.shape[0]
    shift_value = damping[0] * (columns * tok_rows / examples)
    factor = jnp.linalg.cholesky(kernel + shift_value * jnp.eye(docs_all, dtype=jnp.float32))
    start = lax.axis_index("dp") * examples
    own_columns = lax.dynamic_slice_in_dim(kernel, start, examples, 1)
    first = lax.linalg.triangular_solve(factor, own_columns, left_side=True, lower=True)
    second = lax.linalg.triangular_solve(
        factor, first, left_side=True, lower=True, transpose_a=True
    )
    own_block = lax.dynamic_slice_in_dim(second, start, examples, 0)
    scores = jnp.diagonal(own_block)
    return (kept_adjoint[None], scores[None])


def solution(mesh):
    return jax.shard_map(
        local,
        mesh=mesh,
        in_specs=(
            P("section", ("group", "dp"), "mp"),
            P(("group", "dp"), "mp"),
            P("section", "dp", "mp"),
            P("section", "dp", "mp"),
            P("section", None, "mp"),
            P("section", None, None),
            P("section"),
            P(("group", "dp"), None),
        ),
        out_specs=(P("section", ("group", "dp"), "mp"), P("section", ("group", "dp"))),
        check_vma=False,
    )
```

profile of v0, /device:TPU:0, one launch (start us, length us, event | category | flops | bytes accessed | tf_op | source)
XLA Modules:
  0.0 259.2 jit_solution(1934195725843426018)
XLA Ops:
  7.2 0.0 copy-start
  7.2 0.0 copy-start.2
  7.2 0.0 all-gather.6.cloned.1.call-start
  7.2 0.7 all-gather.6.cloned.1.call-update
  7.9 0.0 reduce-scatter.3.cloned.1.call-start
  8.0 85.1 %all-gather.6.cloned.1.call-done = bf16[1,512,4096]{2,1,0:T(8,128)(2,1)} async-done(((bf16[1,128,4096]{2,1,0:T(8,128)(2,1)}), bf16[1,512,4096]{2,1,0:T(8,128)(2,1)}) %all-gather.6.cloned.1.call-update) | async-done | bytes 4194320 | tf_op jit(solution)/shard_map/all_gather | solution.py:22
  93.1 4.7 %fusion.6 = f32[128,512]{1,0:T(8,128)} fusion(bf16[128,4096]{1,0:T(8,128)(2,1)} %param.9, bf16[1,512,4096]{2,1,0:T(8,128)(2,1)} %all-gather.6.cloned.1.call-done), kind=kOutput, calls=%fused_computation.8 | convolution fusion | flops 536870912 | bytes 5505024 | tf_op jit(solution)/shard_map/dot_general | solution.py:28
  97.8 0.0 reduce-scatter.3.cloned.1.call-update
  97.9 0.0 all-gather.8.cloned.1.call-start
  97.9 0.7 all-gather.8.cloned.1.call-update
  98.6 0.0 reduce-scatter.5.cloned.1.call-start
  98.6 5.6 %reduce-scatter.3.cloned.1.call-done = f32[128,256]{1,0:T(8,128)} async-done(((f32[128,512]{1,0:T(8,128)}), f32[128,256]{1,0:T(8,128)}) %reduce-scatter.3.cloned.1.call-update) | async-done | bytes 131088 | tf_op jit(solution)/shard_map/reduce_scatter | solution.py:31
  104.2 0.9 convert_element_type.38
  105.1 1.9 all_gather.16
  107.0 80.8 %all-gather.8.cloned.1.call-done = bf16[1,512,4096]{2,1,0:T(8,128)(2,1)} async-done(((bf16[1,128,4096]{2,1,0:T(8,128)(2,1)}), bf16[1,512,4096]{2,1,0:T(8,128)(2,1)}) %all-gather.8.cloned.1.call-update) | async-done | bytes 4194320 | tf_op jit(solution)/shard_map/all_gather | solution.py:21
  187.8 0.0 copy-done.2
  187.8 0.0 copy-start.1
  187.8 3.1 %fusion = bf16[128,4096]{1,0:T(8,128)(2,1)S(1)} fusion(bf16[128,512]{1,0:T(8,128)(2,1)S(1)} %all_gather.16, bf16[1,512,4096]{2,1,0:T(8,128)(2,1)} %all-gather.8.cloned.1.call-done, bf16[128,4096]{1,0:T(8,128)(2,1)S(1)} %copy-done.2), kind=kOutput, calls=%fused_computation.2 | convolution fusion | flops 538443776 | bytes 6422528 | tf_op jit(solution)/shard_map/dot_general | solution.py:37
  190.9 0.0 copy-start.4
  190.9 0.0 copy-start.3
  190.9 1.4 collective-permute-start
  192.3 25.5 %collective-permute-done = bf16[128,4096]{1,0:T(8,128)(2,1)S(1)} collective-permute-done((bf16[128,4096]{1,0:T(8,128)(2,1)S(1)}, bf16[128,4096]{1,0:T(8,128)(2,1)S(1)}, u32[]{:S(2)}, u32[]{:S(2)}) %collective-permute-start) | collective-permute-done | bytes 1048608 | tf_op jit(solution)/shard_map/ppermute | solution.py:10
  217.8 0.0 copy-done.1
  217.9 2.2 fusion.4
  220.1 0.0 reduce-scatter.5.cloned.1.call-update
  220.1 0.0 copy-done
  220.1 1.5 convolution_convert_fusion.1
  221.7 0.0 copy-done.4
  221.7 0.2 reduce-window.8
  222.5 3.4 %psum.7 = bf16[128,64]{0,1:T(8,128)(2,1)S(1)} all-reduce(bf16[128,64]{0,1:T(8,128)(2,1)S(1)} %convolution_convert_fusion.1), channel_id=1, replica_groups=mesh['group'=2,'dp'=4,'section'=2,'mp'=2] {'mp'}, use_global_device_ids=true, to_apply=%region_4.5 | all-reduce | flops 8192 | bytes 32768 | tf_op jit(solution)/shard_map/psum | solution.py:50
  225.9 0.1 convert_reduce_fusion
  226.0 0.0 reduce-scatter.5.cloned.1.call-done
  226.0 0.9 convert_element_type.41
  226.9 1.9 all_gather.18
  228.8 0.0 copy-done.3
  228.8 0.2 fusion.14
  229.0 0.2 fusion.8
  229.2 0.1 reshape.54
  229.3 13.4 %all-gather.2 = bf16[4,4,4096]{2,1,0:T(4,128)(2,1)S(1)} all-gather(bf16[1,4,4096]{2,1,0:T(4,128)(2,1)S(1)} %reshape.54), channel_id=1, replica_groups=mesh['group'=2,'dp'=4,'section'=2,'mp'=2] {'dp'}, dimensions={0}, use_global_device_ids=true | all-gather | bytes 163840 | tf_op jit(solution)/shard_map/all_gather | solution.py:60
  242.8 0.2 fusion.37
  242.9 0.1 copy.13
  243.0 1.5 cholesky.16
  244.5 0.6 compare_reduce_fusion
  245.2 0.6 fusion.24
  245.8 1.2 custom-call.8
  247.1 0.1 fusion.27
  247.2 0.1 fusion.25
  247.4 1.2 gather_fusion
  248.5 4.2 %fusion.10 = bf16[1,128,4096]{2,1,0:T(8,128)(2,1)} fusion(bf16[128,4096]{1,0:T(8,128)(2,1)S(1)} %collective-permute-done, bf16[128,4096]{1,0:T(8,128)(2,1)S(1)} %fusion, pred[]{:T(512)S(6)} %eq.24, pred[]{:T(512)S(6)} %eq.23, bf16[128,512]{1,0:T(8,128)(2,1)S(1)} %all_gather.18, bf16[1,512,4096]{2,1,0:T(8,128)(2,1)} %all-gather.8.cloned.1.call-done), kind=kOutput, calls=%fused_computation.15 | convolution fusion | flops 539492352 | bytes 7471106 | tf_op jit(solution)/shard_map/dot_general | solution.py:37
  (6 shorter events, 0.1 us)
Async XLA Ops:
  7.2 213.0 %copy-start = (bf16[1,128,4096]{2,1,0:T(8,128)(2,1)S(1)}, bf16[1,128,4096]{2,1,0:T(8,128)(2,1)}, u32[]{:S(2)}) copy-start(bf16[1,128,4096]{2,1,0:T(8,128)(2,1)} %param.8) | copy-start | bytes 3145732
  7.2 180.6 %copy-start.2 = (bf16[128,4096]{1,0:T(8,128)(2,1)S(1)}, bf16[128,4096]{1,0:T(8,128)(2,1)}, u32[]{:S(2)}) copy-start(bf16[128,4096]{1,0:T(8,128)(2,1)} %param.9) | copy-start | bytes 3145732
  7.2 85.9 %all-gather.6.cloned.1.call-start = ((), (), s32[]{:S(2)}) async-start(), calls=%async_computation.4 | async-start | bytes 5242880 | tf_op jit(solution)/shard_map/all_gather | solution.py:22
  7.9 96.3 %reduce-scatter.3.cloned.1.call-start = ((), (), s32[]{:S(2)}) async-start(), calls=%async_computation.2 | async-start | bytes 393216 | tf_op jit(solution)/shard_map/reduce_scatter | solution.py:31
  97.9 90.0 %all-gather.8.cloned.1.call-start = ((), (), s32[]{:S(2)}) async-start(), calls=%async_computation.5 | async-start | bytes 5242880 | tf_op jit(solution)/shard_map/all_gather | solution.py:21
  98.6 127.4 %reduce-scatter.5.cloned.1.call-start = ((), (), s32[]{:S(2)}) async-start(), calls=%async_computation.3 | async-start | bytes 393216 | tf_op jit(solution)/shard_map/reduce_scatter | solution.py:31
  187.8 30.0 %copy-start.1 = (bf16[1,512,4096]{2,1,0:T(8,128)(2,1)S(1)}, bf16[1,512,4096]{2,1,0:T(8,128)(2,1)}, u32[]{:S(2)}) copy-start(bf16[1,512,4096]{2,1,0:T(8,128)(2,1)} %all-gather.6.cloned.1.call-done) | copy-start | bytes 12582916
  190.9 30.8 %copy-start.4 = (s32[1,4]{1,0:T(1,128)S(1)}, s32[1,4]{1,0:T(1,128)}, u32[]{:S(2)}) copy-start(s32[1,4]{1,0:T(1,128)} %param.15) | copy-start | bytes 52
  190.9 37.9 %copy-start.3 = (bf16[1,64,512]{2,1,0:T(8,128)(2,1)S(1)}, bf16[1,64,512]{2,1,0:T(8,128)(2,1)}, u32[]{:S(2)}) copy-start(bf16[1,64,512]{2,1,0:T(8,128)(2,1)} %param.13) | copy-start | bytes 196612
  190.9 26.9 %collective-permute-start = (bf16[128,4096]{1,0:T(8,128)(2,1)S(1)}, bf16[128,4096]{1,0:T(8,128)(2,1)S(1)}, u32[]{:S(2)}, u32[]{:S(2)}) collective-permute-start(bf16[128,4096]{1,0:T(8,128)(2,1)S(1)} %fusion), channel_id=1, source_target_pairs={{2,0},{3,1},{6,4},{7,5},{10,8},{11,9},{14,12},{15,13},{18,16},{19,... | collective-permute-start | bytes 3145736 | tf_op jit(solution)/shard_map/ppermute | solution.py:10
Sparse Core Ops, SparseCore 0:
  9.6 83.4 all-gather.5
  98.0 6.1 reduce-scatter.2
  105.9 81.9 all-gather.7
  220.2 5.3 reduce-scatter.4
where the time goes:
time: 260 us; the launch traced here: 259 us
  waiting for transfers between devices  198 us (76%)
  blocking collectives  20.6 us (8%)
  matrix products  16.5 us (6%)
  between operations  14.6 us (6%)
  other arithmetic  6.15 us (2%)
    all_gather x1, waiting for transfers between devices, local(): lax.all_gather(out_weight[0], 'dp', axis=0, tiled=True)  85.1 us
    all_gather x1, waiting for transfers between devices, local(): lax.all_gather(in_weight[0], 'dp', axis=0, tiled=True)  80.8 us
    ppermute x1, waiting for transfers between devices, shifted(): return lax.ppermute(shard, axis, pairs)  25.5 us
    all_gather x1, blocking collectives, local(): lax.all_gather(local_rows.astype(jnp.bfloat16), 'dp', axis=0, tiled=True)  13.4 us
    dot_general x2, matrix products, local(): jnp.dot(rank_grad, u_full, preferred_element_type=jnp.float32)  7.22 us
    dot_general x2, matrix products, local(): lax.dot_general(adjoint_now, v_full, (((1,), (1,)), ((), ())), preferred_...  6.98 us
    reduce_scatter x2, waiting for transfers between devices, local(): lax.psum_scatter(partial_rank, 'mp', scatter_dimension=1, tiled=True)  5.58 us
  transfers between devices with their start and end apart: 5, of which 4 were waited for; matrix products, arithmetic and copies ran while one was open for 1% of the time, Pallas kernels for 0%

commit v1 on v0

v1 whole, which is shorter than its diff:
```python
import jax
import jax.numpy as jnp
from jax import lax
from jax.sharding import PartitionSpec as P

F32 = jnp.float32
BF16 = jnp.bfloat16
STEP = ((0, 1), (1, 0), (2, 3), (3, 2))
MIDDLE = ((1, 2), (2, 1))
TWO = ((0, 2), (2, 0), (1, 3), (3, 1))
ENDS = ((1, 0), (2, 3))
ACROSS = ((0, 3), (3, 0), (1, 2), (2, 1))
PAIR = ((0, 1), (1, 0))


def dot_t(a, b, **kw):
    return lax.dot_general(a, b, (((1,), (1,)), ((), ())), preferred_element_type=F32, **kw)


def after(x, *first):
    return lax.optimization_barrier((x, *first))[0]


def shifted(shard, axis, by):
    devices = lax.axis_size(axis)
    pairs = [(i, i + by) for i in range(devices) if 0 <= i + by < devices]
    return lax.ppermute(shard, axis, pairs)


def member_of(lengths, tok_rows):
    examples = lengths.shape[0]
    upto = jnp.arange(examples)[:, None] <= jnp.arange(examples)[None, :]
    ends = jnp.sum(jnp.where(upto, lengths[:, None], 0), axis=0)
    positions = jnp.arange(tok_rows, dtype=jnp.int32)
    doc_index = jnp.sum((positions[:, None] >= ends[None, :]).astype(jnp.int32), axis=1)
    return (doc_index[:, None] == jnp.arange(examples, dtype=jnp.int32)[None, :]).astype(F32)


def own_rows(out_proj, in_proj, lengths):
    member = member_of(lengths, out_proj.shape[0])
    rows = jnp.einsum("te,to,ti->eoi", member, out_proj, in_proj, precision=lax.Precision.HIGHEST)
    return rows.reshape(lengths.shape[0], -1).astype(BF16)


def scores_of(every_row, damping, start, examples, tok_rows):
    columns = every_row.shape[1]
    kernel = dot_t(every_row, every_row)
    shift_value = damping * (columns * tok_rows / examples)
    factor = jnp.linalg.cholesky(kernel + shift_value * jnp.eye(kernel.shape[0], dtype=F32))
    own_columns = lax.dynamic_slice_in_dim(kernel, start, examples, 1)
    first = lax.linalg.triangular_solve(factor, own_columns, left_side=True, lower=True)
    second = lax.linalg.triangular_solve(factor, first, left_side=True, lower=True, transpose_a=True)
    own_block = lax.dynamic_slice_in_dim(second, start, examples, 0)
    return jnp.sum(own_block * jnp.eye(examples, dtype=F32), axis=1)


def relay(acts, cotangent, in_weight, out_weight, in_factor, out_factor, damping, lengths):
    sections = lax.axis_size("section")
    section_index = lax.axis_index("section")
    tok_rows = cotangent.shape[0]
    examples = lengths.shape[1]
    u_full = lax.all_gather(in_weight[0], "dp", axis=0, tiled=True)
    v_full = lax.all_gather(out_weight[0], "dp", axis=0, tiled=True)
    adjoint_now = cotangent
    kept_rank = jnp.zeros((tok_rows, v_full.shape[0]), BF16)
    kept_adjoint = jnp.zeros_like(cotangent)
    for turn in range(sections):
        partial_rank = dot_t(adjoint_now, v_full)
        own_half = lax.psum_scatter(partial_rank, "mp", scatter_dimension=1, tiled=True).astype(BF16)
        rank_grad = lax.all_gather(own_half, "mp", axis=1, tiled=True)
        new_adjoint = (
            adjoint_now.astype(F32) + jnp.dot(rank_grad, u_full, preferred_element_type=F32)
        ).astype(BF16)
        active = section_index == sections - 1 - turn
        kept_rank = jnp.where(active, rank_grad, kept_rank)
        kept_adjoint = jnp.where(active, new_adjoint, kept_adjoint)
        if turn + 1 < sections:
            adjoint_now = shifted(new_adjoint, "section", -1)
    out_proj = dot_t(kept_rank, out_factor[0])
    in_proj = lax.psum(dot_t(acts[0], in_factor[0]), "mp")
    rows = own_rows(out_proj, in_proj, lengths[0])
    every_row = lax.all_gather(rows, "dp", axis=0, tiled=True)
    start = lax.axis_index("dp") * examples
    scores = scores_of(every_row, damping[0], start, examples, tok_rows)
    return (kept_adjoint[None], scores[None])


def gathered(w, *first):
    z = lax.axis_index("dp")
    w = after(w, *first)
    two = lax.ppermute(w, "dp", TWO)
    one = lax.ppermute(w, "dp", STEP)
    ends = lax.ppermute(two, "dp", ENDS)
    middle = lax.ppermute(after(w, two), "dp", MIDDLE)
    far = jnp.where((z == 0) | (z == 3), ends, middle)
    return [w, one, two, far]


def plane(axis):
    return (axis, PAIR) if axis != "both" else (("group", "section"), ACROSS)


def summed(part):
    core = lax.axis_index("mp")
    half = part.shape[1] // 2
    keep = lax.dynamic_slice_in_dim(part, core * half, half, 1)
    send = lax.dynamic_slice_in_dim(part, (1 - core) * half, half, 1)
    own = (keep + lax.ppermute(send, "mp", PAIR)).astype(BF16)
    others = [lax.ppermute(own, *plane(a)) for a in ("both", "section", "group")]
    total = own.astype(F32)
    for other in others:
        total = total + other.astype(F32)
    total = total.astype(BF16)
    other = lax.ppermute(total, "mp", PAIR)
    return jnp.where(core == 0, jnp.concatenate([total, other], 1), jnp.concatenate([other, total], 1))


def spread(acts, cotangent, in_weight, out_weight, in_factor, out_factor, damping, lengths):
    x, y, z = lax.axis_index("section"), lax.axis_index("group"), lax.axis_index("dp")
    tok_rows, width = cotangent.shape
    examples = lengths.shape[1]
    slice_width = width // 4

    def piece(a, px, py):
        return lax.dynamic_slice_in_dim(a, (px * 2 + py) * slice_width, slice_width, 1)

    v_own, u_own = out_weight[0], in_weight[0]
    v_keep, u_keep = piece(v_own, x, y), piece(u_own, x, y)
    v_other = lax.ppermute(piece(v_own, 1 - x, y), "section", PAIR)
    u_other = lax.ppermute(piece(u_own, 1 - x, y), "section", PAIR)
    last = x == 1
    v1, v0 = jnp.where(last, v_keep, v_other), jnp.where(last, v_other, v_keep)
    u1, u0 = jnp.where(last, u_keep, u_other), jnp.where(last, u_other, u_keep)
    g_own = piece(cotangent, x, y)
    g_other = lax.ppermute(piece(cotangent, x, 1 - y), "group", PAIR)
    g = jnp.where(y == 0, jnp.concatenate([g_own, g_other], 0), jnp.concatenate([g_other, g_own], 0))

    v1s = gathered(v1)
    u1s = gathered(u1, v1s[2])
    v0s = gathered(v0, u1s[2])
    u0s = gathered(u0, v0s[2])

    def step(adjoint, vs, us):
        part = jnp.concatenate([dot_t(adjoint, v) for v in vs], 1)
        rank = summed(part)
        block = rank.shape[1] // 4
        total = adjoint.astype(F32)
        for k, u in enumerate(us):
            total = total + jnp.dot(rank[:, k * block : (k + 1) * block], u, preferred_element_type=F32)
        return rank, total.astype(BF16)

    rank1, adjoint1 = step(g, v1s, u1s)
    rank0, adjoint0 = step(adjoint1, v0s, u0s)

    def of_group(a, who):
        return lax.dynamic_slice_in_dim(a, who * tok_rows, tok_rows, 0)

    mine, theirs = jnp.where(last, adjoint1, adjoint0), jnp.where(last, adjoint0, adjoint1)
    here = of_group(mine, y)
    from_x = lax.ppermute(of_group(theirs, y), *plane("section"))
    from_xy = lax.ppermute(of_group(theirs, 1 - y), *plane("both"))
    from_y = lax.ppermute(of_group(mine, 1 - y), *plane("group"))
    adjoint = jnp.zeros_like(cotangent)
    for value, px, py in ((here, x, y), (from_y, x, 1 - y), (from_x, 1 - x, y), (from_xy, 1 - x, 1 - y)):
        adjoint = lax.dynamic_update_slice_in_dim(adjoint, value, (px * 2 + py) * slice_width, 1)

    rank = of_group(jnp.where(last, rank1, rank0), y)
    block = out_factor.shape[2] // 4
    factor = jnp.concatenate(
        [lax.dynamic_slice_in_dim(out_factor[0], jnp.bitwise_xor(z, k) * block, block, 1) for k in range(4)], 1
    )
    out_proj = dot_t(rank, factor)
    in_part = dot_t(acts[0], in_factor[0])
    in_proj = in_part + lax.ppermute(in_part, "mp", PAIR)
    rows = own_rows(out_proj, in_proj, lengths[0])
    every_row = jnp.concatenate([rows] + [lax.ppermute(rows, "dp", p) for p in (STEP, TWO, ACROSS)], 0)
    scores = scores_of(every_row, damping[0], 0, examples, tok_rows)
    return (adjoint[None], scores[None])


def solution(mesh):
    sizes = (mesh.shape["group"], mesh.shape["dp"], mesh.shape["section"], mesh.shape["mp"])
    return jax.shard_map(
        spread if sizes == (2, 4, 2, 2) else relay,
        mesh=mesh,
        in_specs=(
            P("section", ("group", "dp"), "mp"),
            P(("group", "dp"), "mp"),
            P("section", "dp", "mp"),
            P("section", "dp", "mp"),
            P("section", None, "mp"),
            P("section", None, None),
            P("section"),
            P(("group", "dp"), None),
        ),
        out_specs=(P("section", ("group", "dp"), "mp"), P("section", ("group", "dp"))),
        check_vma=False,
    )
```

time: 260 us -> 139 us (0.53)
  waiting for transfers between devices: 198 us -> 72.3 us
  starting transfers between devices: 1.58 us -> 37.3 us
  blocking collectives: 20.6 us -> 0 us
  between operations: 14.6 us -> 1.85 us
  matrix products: 16.5 us -> 9.47 us
  local copies, waits for them, and re-layouts: 1.42 us -> 7.97 us
  other arithmetic: 6.15 us -> 9.06 us
    all_gather x2 -> x0, waiting for transfers between devices: 166 us -> none  [the longest x1 85.1 us: local(): lax.all_gather(out_weight[0], 'dp', axis=0, tiled=True)]
    ppermute x1 -> x36, waiting for transfers between devices: 25.5 us -> 72.3 us  [the longest x4 37.2 us: gathered(): two = lax.ppermute(w, 'dp', TWO)]
    ppermute x1 -> x36, starting transfers between devices: 1.42 us -> 37.3 us  [the longest x6 7.11 us: summed(): lax.ppermute(own, *plane(a))]
    all_gather x3 -> x0, blocking collectives: 17.2 us -> none  [the longest x1 13.4 us: local(): lax.all_gather(local_rows.astype(jnp.bfloat16), 'dp', axis=0, tiled=True)]
    dot_general x8 -> x20, matrix products: 16.2 us -> 8.52 us  [the longest x11 4.83 us: dot_t(): lax.dot_general(a, b, (((1,), (1,)), ((), ())), preferred_element_type=F3...]
    reduce_scatter x2 -> x0, waiting for transfers between devices: 5.58 us -> none  [local(): lax.psum_scatter(partial_rank, 'mp', scatter_dimension=1, tiled=True)]
    select_n x0 -> x5, other arithmetic: none -> 3.62 us  [the longest x1 1.27 us: spread(): jnp.where(last, v_other, v_keep)]
    psum x1 -> x0, blocking collectives: 3.36 us -> none  [local(): in_proj = lax.psum(in_part.astype(jnp.bfloat16), 'mp').astype(jnp.float32)]
  transfers between devices with their start and end apart: 5 -> 36, of which waited for: 4 -> 14; matrix products, arithmetic and copies ran while one was open for 1% -> 14% of each run, Pallas kernels for 0% -> 0%
where the time goes in v1:
time: 139 us; the launch traced here: 138 us
  waiting for transfers between devices  72.3 us (52%)
  starting transfers between devices  37.3 us (27%)
  matrix products  9.47 us (7%)
  other arithmetic  9.06 us (7%)
  local copies, waits for them, and re-layouts  7.97 us (6%)
  between operations  1.85 us (1%)
    ppermute x4, waiting for transfers between devices, gathered(): two = lax.ppermute(w, 'dp', TWO)  37.2 us
    ppermute x4, waiting for transfers between devices, gathered(): ends = lax.ppermute(two, 'dp', ENDS)  18.8 us
    ppermute x6, starting transfers between devices, summed(): lax.ppermute(own, *plane(a))  7.11 us
    ppermute x1, waiting for transfers between devices, spread(): v_other = lax.ppermute(piece(v_own, 1 - x, y), 'section', PAIR)  6.31 us
    ppermute x6, waiting for transfers between devices, summed(): lax.ppermute(own, *plane(a))  5.82 us
    ppermute x4, starting transfers between devices, gathered(): ends = lax.ppermute(two, 'dp', ENDS)  5.16 us
    ppermute x3, starting transfers between devices, spread(): lax.ppermute(rows, 'dp', p)  5.08 us
    dot_general x11, matrix products, dot_t(): lax.dot_general(a, b, (((1,), (1,)), ((), ())), preferred_element_type=F3...  4.83 us
  transfers between devices with their start and end apart: 36, of which 14 were waited for; matrix products, arithmetic and copies ran while one was open for 14% of the time, Pallas kernels for 0%

profile of v1, /device:TPU:0, one launch (start us, length us, event | category | flops | bytes accessed | tf_op | source)
XLA Modules:
  0.0 137.9 jit_solution(12881576624109218349)
XLA Ops:
  0.7 1.1 dynamic-slice_bitcast_fusion.1
  1.7 3.0 %collective-permute-start.1 = (bf16[128,1024]{1,0:T(8,128)(2,1)S(1)}, bf16[128,1024]{1,0:T(8,128)(2,1)S(1)}, u32[]{:S(2)}, u32[]{:S(2)}) collective-permute-start(bf16[128,1024]{1,0:T(8,128)(2,1)S(1)} %dynamic-slice_bitcast_fusion.1), channel_id=1, source_target_pairs={{0,2},{2,0},{1,3},{3,1},{4,6},{6,4},{5,7},{7,5},{8,10},{10,8},{9,1... | collective-permute-start | bytes 786440 | tf_op jit(solution)/shard_map/ppermute | solution.py:129
  4.7 6.3 %collective-permute-done.1 = bf16[128,1024]{1,0:T(8,128)(2,1)S(1)} collective-permute-done((bf16[128,1024]{1,0:T(8,128)(2,1)S(1)}, bf16[128,1024]{1,0:T(8,128)(2,1)S(1)}, u32[]{:S(2)}, u32[]{:S(2)}) %collective-permute-start.1) | collective-permute-done | bytes 262176 | tf_op jit(solution)/shard_map/ppermute | solution.py:129
  11.0 1.3 bitcast_select_fusion.2
  12.3 1.8 %collective-permute-start = (bf16[128,1024]{1,0:T(8,128)(2,1)S(1)}, bf16[128,1024]{1,0:T(8,128)(2,1)S(1)}, u32[]{:S(2)}, u32[]{:S(2)}) collective-permute-start(bf16[128,1024]{1,0:T(8,128)(2,1)S(1)} %get-tuple-element.30), channel_id=1, source_target_pairs={{0,16},{16,0},{1,17},{17,1},{2,18},{18,2},{3,19},{19,3},{4,20},{20... | collective-permute-start | bytes 786440 | tf_op jit(solution)/shard_map/ppermute | solution.py:135
  14.1 1.7 %dynamic-slice_bitcast_fusion = bf16[128,1024]{1,0:T(8,128)(2,1)} fusion(bf16[1,128,4096]{2,1,0:T(8,128)(2,1)} %param.10, s32[]{:T(128)S(6)} %select_n.136), kind=kLoop, calls=%fused_computation.32 | loop fusion | bytes 524292 | tf_op jit(solution)/shard_map/dynamic_slice | solution.py:125
  15.8 1.5 %collective-permute-start.11 = (bf16[128,1024]{1,0:T(8,128)(2,1)}, bf16[128,1024]{1,0:T(8,128)(2,1)S(1)}, u32[]{:S(2)}, u32[]{:S(2)}) collective-permute-start(bf16[128,1024]{1,0:T(8,128)(2,1)} %dynamic-slice_bitcast_fusion), channel_id=1, source_target_pairs={{0,2},{2,0},{1,3},{3,1},{4,6},{6,4},{5,7},{7,5},{8,10},{10,8},{9,1... | collective-permute-start | bytes 786440 | tf_op jit(solution)/shard_map/ppermute | solution.py:130
  17.3 1.6 %collective-permute-start.2 = (bf16[128,1024]{1,0:T(8,128)(2,1)S(1)}, bf16[128,1024]{1,0:T(8,128)(2,1)S(1)}, u32[]{:S(2)}, u32[]{:S(2)}) collective-permute-start(bf16[128,1024]{1,0:T(8,128)(2,1)S(1)} %get-tuple-element.9), channel_id=1, source_target_pairs={{0,4},{4,0},{8,12},{12,8},{1,5},{5,1},{9,13},{13,9},{2,6},{6,2},{1... | collective-permute-start | bytes 786440 | tf_op jit(solution)/shard_map/ppermute | solution.py:92
  18.9 2.6 %collective-permute-start.3 = (bf16[128,1024]{1,0:T(8,128)(2,1)S(1)}, bf16[128,1024]{1,0:T(8,128)(2,1)S(1)}, u32[]{:S(2)}, u32[]{:S(2)}) collective-permute-start(bf16[128,1024]{1,0:T(8,128)(2,1)S(1)} %get-tuple-element.9), channel_id=1, source_target_pairs={{0,8},{8,0},{4,12},{12,4},{1,9},{9,1},{5,13},{13,5},{2,10},{10,2},... | collective-permute-start | bytes 786440 | tf_op jit(solution)/shard_map/ppermute | solution.py:91
  21.9 9.8 %collective-permute-done.3 = bf16[128,1024]{1,0:T(8,128)(2,1)S(1)} collective-permute-done((bf16[128,1024]{1,0:T(8,128)(2,1)S(1)}, bf16[128,1024]{1,0:T(8,128)(2,1)S(1)}, u32[]{:S(2)}, u32[]{:S(2)}) %collective-permute-start.3) | collective-permute-done | bytes 262176 | tf_op jit(solution)/shard_map/ppermute | solution.py:91
  31.8 0.7 collective-permute-start.5
  32.4 1.3 collective-permute-start.4
  34.4 6.3 %collective-permute-done.4 = bf16[128,1024]{1,0:T(8,128)(2,1)S(1)} collective-permute-done((bf16[128,1024]{1,0:T(8,128)(2,1)S(1)}, bf16[128,1024]{1,0:T(8,128)(2,1)S(1)}, u32[]{:S(2)}, u32[]{:S(2)}) %collective-permute-start.4) | collective-permute-done | bytes 262176 | tf_op jit(solution)/shard_map/ppermute | solution.py:93
  41.2 1.1 bitcast_select_fusion
  42.3 0.6 collective-permute-start.13
  42.9 1.0 add_convert_fusion.3
  43.9 0.5 collective-permute-start.7
  44.4 1.5 %collective-permute-start.8 = (bf16[256,256]{0,1:T(8,128)(2,1)S(1)}, bf16[256,256]{0,1:T(8,128)(2,1)S(1)}, u32[]{:S(2)}, u32[]{:S(2)}) collective-permute-start(bf16[256,256]{0,1:T(8,128)(2,1)S(1)} %add_convert_fusion.3), channel_id=1, source_target_pairs={{0,2},{2,0},{1,3},{3,1},{4,6},{6,4},{5,7},{7,5},{8,10},{10,8},{9,1... | collective-permute-start | bytes 393224 | tf_op jit(solution)/shard_map/ppermute | solution.py:109
  45.9 1.5 %collective-permute-start.9 = (bf16[256,256]{0,1:T(8,128)(2,1)S(1)}, bf16[256,256]{0,1:T(8,128)(2,1)S(1)}, u32[]{:S(2)}, u32[]{:S(2)}) collective-permute-start(bf16[256,256]{0,1:T(8,128)(2,1)S(1)} %add_convert_fusion.3), channel_id=1, source_target_pairs={{0,16},{16,0},{1,17},{17,1},{2,18},{18,2},{3,19},{19,3},{4,20},{20... | collective-permute-start | bytes 393224 | tf_op jit(solution)/shard_map/ppermute | solution.py:109
  47.4 10.0 %collective-permute-done.13 = bf16[128,1024]{1,0:T(8,128)(2,1)S(1)} collective-permute-done((bf16[128,1024]{1,0:T(8,128)(2,1)S(1)}, bf16[128,1024]{1,0:T(8,128)(2,1)S(1)}, u32[]{:S(2)}, u32[]{:S(2)}) %collective-permute-start.13) | collective-permute-done | bytes 262176 | tf_op jit(solution)/shard_map/ppermute | solution.py:91
  57.5 0.6 copy-done.3
  58.2 1.7 %collective-permute-start.12 = (bf16[128,1024]{1,0:T(8,128)(2,1)S(1)}, bf16[128,1024]{1,0:T(8,128)(2,1)S(1)}, u32[]{:S(2)}, u32[]{:S(2)}) collective-permute-start(bf16[128,1024]{1,0:T(8,128)(2,1)S(1)} %get-tuple-element.11), channel_id=1, source_target_pairs={{0,4},{4,0},{8,12},{12,8},{1,5},{5,1},{9,13},{13,9},{2,6},{6,2},{1... | collective-permute-start | bytes 786440 | tf_op jit(solution)/shard_map/ppermute | solution.py:92
  59.8 0.4 collective-permute-start.16
  60.2 0.7 collective-permute-start.15
  60.9 10.4 %collective-permute-done.17 = bf16[128,1024]{1,0:T(8,128)(2,1)S(1)} collective-permute-done((bf16[128,1024]{1,0:T(8,128)(2,1)S(1)}, bf16[128,1024]{1,0:T(8,128)(2,1)S(1)}, u32[]{:S(2)}, u32[]{:S(2)}) %collective-permute-start.17) | collective-permute-done | bytes 262176 | tf_op jit(solution)/shard_map/ppermute | solution.py:91
  71.3 1.3 collective-permute-start.14
  72.6 0.7 collective-permute-start.19
  73.4 0.3 fusion.41
  73.7 0.6 copy-done.4
  74.7 1.3 collective-permute-start.18
  76.3 7.8 %collective-permute-done.14 = bf16[128,1024]{1,0:T(8,128)(2,1)S(1)} collective-permute-done((bf16[128,1024]{1,0:T(8,128)(2,1)}, bf16[128,1024]{1,0:T(8,128)(2,1)S(1)}, u32[]{:S(2)}, u32[]{:S(2)}) %collective-permute-start.14) | collective-permute-done | bytes 262176 | tf_op jit(solution)/shard_map/ppermute | solution.py:93
  84.1 0.3 fusion
  85.4 3.9 %collective-permute-done.18 = bf16[128,1024]{1,0:T(8,128)(2,1)S(1)} collective-permute-done((bf16[128,1024]{1,0:T(8,128)(2,1)S(1)}, bf16[128,1024]{1,0:T(8,128)(2,1)S(1)}, u32[]{:S(2)}, u32[]{:S(2)}) %collective-permute-start.18) | collective-permute-done | bytes 262176 | tf_op jit(solution)/shard_map/ppermute | solution.py:93
  89.8 0.9 copy-done.2
  90.7 1.1 fusion.4
  91.9 0.5 collective-permute-start.21
  92.4 1.5 %collective-permute-start.22 = (bf16[256,256]{0,1:T(8,128)(2,1)S(1)}, bf16[256,256]{0,1:T(8,128)(2,1)S(1)}, u32[]{:S(2)}, u32[]{:S(2)}) collective-permute-start(bf16[256,256]{0,1:T(8,128)(2,1)S(1)} %add_convert_fusion.1), channel_id=1, source_target_pairs={{0,2},{2,0},{1,3},{3,1},{4,6},{6,4},{5,7},{7,5},{8,10},{10,8},{9,1... | collective-permute-start | bytes 393224 | tf_op jit(solution)/shard_map/ppermute | solution.py:109
  93.9 1.5 %collective-permute-start.23 = (bf16[256,256]{0,1:T(8,128)(2,1)S(1)}, bf16[256,256]{0,1:T(8,128)(2,1)S(1)}, u32[]{:S(2)}, u32[]{:S(2)}) collective-permute-start(bf16[256,256]{0,1:T(8,128)(2,1)S(1)} %add_convert_fusion.1), channel_id=1, source_target_pairs={{0,16},{16,0},{1,17},{17,1},{2,18},{18,2},{3,19},{19,3},{4,20},{20... | collective-permute-start | bytes 393224 | tf_op jit(solution)/shard_map/ppermute | solution.py:109
  95.7 3.4 %collective-permute-done.21 = bf16[256,256]{0,1:T(8,128)(2,1)S(1)} collective-permute-done((bf16[256,256]{0,1:T(8,128)(2,1)S(1)}, bf16[256,256]{0,1:T(8,128)(2,1)S(1)}, u32[]{:S(2)}, u32[]{:S(2)}) %collective-permute-start.21) | collective-permute-done | bytes 131104 | tf_op jit(solution)/shard_map/ppermute | solution.py:109
  99.2 1.4 %collective-permute-done.22 = bf16[256,256]{0,1:T(8,128)(2,1)S(1)} collective-permute-done((bf16[256,256]{0,1:T(8,128)(2,1)S(1)}, bf16[256,256]{0,1:T(8,128)(2,1)S(1)}, u32[]{:S(2)}, u32[]{:S(2)}) %collective-permute-start.22) | collective-permute-done | bytes 131104 | tf_op jit(solution)/shard_map/ppermute | solution.py:109
  100.6 1.0 collective-permute-done.23
  102.5 7.0 %collective-permute-done.26 = bf16[128,1024]{1,0:T(8,128)(2,1)S(1)} collective-permute-done((bf16[128,1024]{1,0:T(8,128)(2,1)S(1)}, bf16[128,1024]{1,0:T(8,128)(2,1)S(1)}, u32[]{:S(2)}, u32[]{:S(2)}) %collective-permute-start.26) | collective-permute-done | bytes 262176 | tf_op jit(solution)/shard_map/ppermute | solution.py:91
  109.5 0.7 collective-permute-start.28
  110.2 1.3 collective-permute-start.27
  111.5 1.1 maximum_select_fusion.2
  112.7 1.0 fusion.2
  113.8 0.7 convert_element_type.82
  114.5 2.6 %collective-permute-start.33 = (bf16[4,4096]{1,0:T(4,128)(2,1)}, bf16[4,4096]{1,0:T(4,128)(2,1)S(1)}, u32[]{:S(2)}, u32[]{:S(2)}) collective-permute-start(bf16[4,4096]{1,0:T(4,128)(2,1)} %convert_element_type.82), channel_id=1, source_target_pairs={{0,4},{4,0},{8,12},{12,8},{1,5},{5,1},{9,13},{13,9},{2,6},{6,2},{1... | collective-permute-start | bytes 98312 | tf_op jit(solution)/shard_map/ppermute | solution.py:176
  117.5 0.3 fusion.34
  118.1 2.1 %collective-permute-start.35 = (bf16[4,4096]{1,0:T(4,128)(2,1)}, bf16[4,4096]{1,0:T(4,128)(2,1)S(1)}, u32[]{:S(2)}, u32[]{:S(2)}) collective-permute-start(bf16[4,4096]{1,0:T(4,128)(2,1)} %convert_element_type.82), channel_id=1, source_target_pairs={{0,12},{12,0},{4,8},{8,4},{1,13},{13,1},{5,9},{9,5},{2,14},{14,2},... | collective-permute-start | bytes 98312 | tf_op jit(solution)/shard_map/ppermute | solution.py:176
  120.6 0.8 collective-permute-done.27
  121.3 0.5 broadcast_select_fusion
  122.0 0.6 collective-permute-start.29
  122.6 0.6 collective-permute-start.30
  123.2 2.5 %collective-permute-start.31 = (bf16[128,1024]{1,0:T(8,128)(2,1)S(1)}, bf16[128,1024]{1,0:T(8,128)(2,1)}, u32[]{:S(2)}, u32[]{:S(2)}) collective-permute-start(bf16[128,1024]{1,0:T(8,128)(2,1)S(1)} %get-tuple-element.24), channel_id=1, source_target_pairs={{0,18},{18,0},{2,16},{16,2},{1,19},{19,1},{3,17},{17,3},{4,22},{22... | collective-permute-start | bytes 786440 | tf_op jit(solution)/shard_map/ppermute | solution.py:161
  125.6 1.0 fusion.19
  126.8 1.5 %cholesky.16 = f32[16,16]{1,0:T(8,128)S(1)} custom-call(f32[16,16]{1,0:T(8,128)S(1)} %fusion.56), custom_call_target="Cholesky" | custom-call | tf_op jit(solution)/shard_map/jit(cholesky)/cholesky | solution.py:49
  128.3 0.6 compare_reduce_fusion
  128.9 0.6 fusion.54
  129.6 1.2 custom-call.8
  131.0 0.7 fusion.3
  131.9 4.1 %collective-permute-done.31 = bf16[128,1024]{1,0:T(8,128)(2,1)} collective-permute-done((bf16[128,1024]{1,0:T(8,128)(2,1)S(1)}, bf16[128,1024]{1,0:T(8,128)(2,1)}, u32[]{:S(2)}, u32[]{:S(2)}) %collective-permute-start.31) | collective-permute-done | bytes 262176 | tf_op jit(solution)/shard_map/ppermute | solution.py:161
  136.0 1.0 bitcast_dynamic-update-slice_fusion
  137.0 1.0 copy-done.1
  (78 shorter events, 6.3 us)
Async XLA Ops:
  0.6 89.1 %copy-start = (bf16[1,128,4096]{2,1,0:T(8,128)(2,1)S(1)}, bf16[1,128,4096]{2,1,0:T(8,128)(2,1)}, u32[]{:S(2)}) copy-start(bf16[1,128,4096]{2,1,0:T(8,128)(2,1)} %param.8) | copy-start | bytes 3145732
  1.7 9.3 %collective-permute-start.1 = (bf16[128,1024]{1,0:T(8,128)(2,1)S(1)}, bf16[128,1024]{1,0:T(8,128)(2,1)S(1)}, u32[]{:S(2)}, u32[]{:S(2)}) collective-permute-start(bf16[128,1024]{1,0:T(8,128)(2,1)S(1)} %dynamic-slice_bitcast_fusion.1), channel_id=1, source_target_pairs={{0,2},{2,0},{1,3},{3,1},{4,6},{6,4},{5,7},{7,5},{8,10},{10,8},{9,1... | collective-permute-start | bytes 786440 | tf_op jit(solution)/shard_map/ppermute | solution.py:129
  12.3 9.2 %collective-permute-start = (bf16[128,1024]{1,0:T(8,128)(2,1)S(1)}, bf16[128,1024]{1,0:T(8,128)(2,1)S(1)}, u32[]{:S(2)}, u32[]{:S(2)}) collective-permute-start(bf16[128,1024]{1,0:T(8,128)(2,1)S(1)} %get-tuple-element.30), channel_id=1, source_target_pairs={{0,16},{16,0},{1,17},{17,1},{2,18},{18,2},{3,19},{19,3},{4,20},{20... | collective-permute-start | bytes 786440 | tf_op jit(solution)/shard_map/ppermute | solution.py:135
  15.8 25.4 %collective-permute-start.11 = (bf16[128,1024]{1,0:T(8,128)(2,1)}, bf16[128,1024]{1,0:T(8,128)(2,1)S(1)}, u32[]{:S(2)}, u32[]{:S(2)}) collective-permute-start(bf16[128,1024]{1,0:T(8,128)(2,1)} %dynamic-slice_bitcast_fusion), channel_id=1, source_target_pairs={{0,2},{2,0},{1,3},{3,1},{4,6},{6,4},{5,7},{7,5},{8,10},{10,8},{9,1... | collective-permute-start | bytes 786440 | tf_op jit(solution)/shard_map/ppermute | solution.py:130
  17.3 16.8 %collective-permute-start.2 = (bf16[128,1024]{1,0:T(8,128)(2,1)S(1)}, bf16[128,1024]{1,0:T(8,128)(2,1)S(1)}, u32[]{:S(2)}, u32[]{:S(2)}) collective-permute-start(bf16[128,1024]{1,0:T(8,128)(2,1)S(1)} %get-tuple-element.9), channel_id=1, source_target_pairs={{0,4},{4,0},{8,12},{12,8},{1,5},{5,1},{9,13},{13,9},{2,6},{6,2},{1... | collective-permute-start | bytes 786440 | tf_op jit(solution)/shard_map/ppermute | solution.py:92
  18.9 12.9 %collective-permute-start.3 = (bf16[128,1024]{1,0:T(8,128)(2,1)S(1)}, bf16[128,1024]{1,0:T(8,128)(2,1)S(1)}, u32[]{:S(2)}, u32[]{:S(2)}) collective-permute-start(bf16[128,1024]{1,0:T(8,128)(2,1)S(1)} %get-tuple-element.9), channel_id=1, source_target_pairs={{0,8},{8,0},{4,12},{12,4},{1,9},{9,1},{5,13},{13,5},{2,10},{10,2},... | collective-permute-start | bytes 786440 | tf_op jit(solution)/shard_map/ppermute | solution.py:91
  31.8 2.6 %collective-permute-start.5 = (bf16[128,1024]{1,0:T(8,128)(2,1)S(1)}, bf16[128,1024]{1,0:T(8,128)(2,1)S(1)}, u32[]{:S(2)}, u32[]{:S(2)}) collective-permute-start(bf16[128,1024]{1,0:T(8,128)(2,1)S(1)} %get-tuple-element.9), channel_id=1, source_target_pairs={{4,8},{8,4},{5,9},{9,5},{6,10},{10,6},{7,11},{11,7},{20,24},{24,20... | collective-permute-start | bytes 786440 | tf_op jit(solution)/shard_map/ppermute | solution.py:94
  32.4 8.3 %collective-permute-start.4 = (bf16[128,1024]{1,0:T(8,128)(2,1)S(1)}, bf16[128,1024]{1,0:T(8,128)(2,1)S(1)}, u32[]{:S(2)}, u32[]{:S(2)}) collective-permute-start(bf16[128,1024]{1,0:T(8,128)(2,1)S(1)} %collective-permute-done.3), channel_id=1, source_target_pairs={{4,0},{8,12},{5,1},{9,13},{6,2},{10,14},{7,3},{11,15},{20,16},{24,... | collective-permute-start | bytes 786440 | tf_op jit(solution)/shard_map/ppermute | solution.py:93
  41.1 1.8 %collective-permute-start.6 = (f32[256,256]{0,1:T(8,128)S(1)}, f32[256,256]{0,1:T(8,128)}, u32[]{:S(2)}, u32[]{:S(2)}) collective-permute-start(f32[256,256]{0,1:T(8,128)S(1)} %constant_dynamic-slice_fusion.4), channel_id=1, source_target_pairs={{0,1},{1,0},{2,3},{3,2},{4,5},{5,4},{6,7},{7,6},{8,9},{9,8},{10,11... | collective-permute-start | bytes 786440 | tf_op jit(solution)/shard_map/ppermute | solution.py:108
  42.3 15.1 %collective-permute-start.13 = (bf16[128,1024]{1,0:T(8,128)(2,1)S(1)}, bf16[128,1024]{1,0:T(8,128)(2,1)S(1)}, u32[]{:S(2)}, u32[]{:S(2)}) collective-permute-start(bf16[128,1024]{1,0:T(8,128)(2,1)S(1)} %get-tuple-element.11), channel_id=1, source_target_pairs={{0,8},{8,0},{4,12},{12,4},{1,9},{9,1},{5,13},{13,5},{2,10},{10,2},... | collective-permute-start | bytes 786440 | tf_op jit(solution)/shard_map/ppermute | solution.py:91
  43.9 13.5 %collective-permute-start.7 = (bf16[256,256]{0,1:T(8,128)(2,1)S(1)}, bf16[256,256]{0,1:T(8,128)(2,1)S(1)}, u32[]{:S(2)}, u32[]{:S(2)}) collective-permute-start(bf16[256,256]{0,1:T(8,128)(2,1)S(1)} %add_convert_fusion.3), channel_id=1, source_target_pairs={{0,18},{18,0},{2,16},{16,2},{1,19},{19,1},{3,17},{17,3},{4,22},{22... | collective-permute-start | bytes 393224 | tf_op jit(solution)/shard_map/ppermute | solution.py:109
  44.4 13.0 %collective-permute-start.8 = (bf16[256,256]{0,1:T(8,128)(2,1)S(1)}, bf16[256,256]{0,1:T(8,128)(2,1)S(1)}, u32[]{:S(2)}, u32[]{:S(2)}) collective-permute-start(bf16[256,256]{0,1:T(8,128)(2,1)S(1)} %add_convert_fusion.3), channel_id=1, source_target_pairs={{0,2},{2,0},{1,3},{3,1},{4,6},{6,4},{5,7},{7,5},{8,10},{10,8},{9,1... | collective-permute-start | bytes 393224 | tf_op jit(solution)/shard_map/ppermute | solution.py:109
  45.9 11.5 %collective-permute-start.9 = (bf16[256,256]{0,1:T(8,128)(2,1)S(1)}, bf16[256,256]{0,1:T(8,128)(2,1)S(1)}, u32[]{:S(2)}, u32[]{:S(2)}) collective-permute-start(bf16[256,256]{0,1:T(8,128)(2,1)S(1)} %add_convert_fusion.3), channel_id=1, source_target_pairs={{0,16},{16,0},{1,17},{17,1},{2,18},{18,2},{3,19},{19,3},{4,20},{20... | collective-permute-start | bytes 393224 | tf_op jit(solution)/shard_map/ppermute | solution.py:109
  57.4 0.7 copy-start.3
  57.4 13.9 %collective-permute-start.17 = (bf16[128,1024]{1,0:T(8,128)(2,1)S(1)}, bf16[128,1024]{1,0:T(8,128)(2,1)S(1)}, u32[]{:S(2)}, u32[]{:S(2)}) collective-permute-start(bf16[128,1024]{1,0:T(8,128)(2,1)S(1)} %get-tuple-element.13), channel_id=1, source_target_pairs={{0,8},{8,0},{4,12},{12,4},{1,9},{9,1},{5,13},{13,5},{2,10},{10,2},... | collective-permute-start | bytes 786440 | tf_op jit(solution)/shard_map/ppermute | solution.py:91
  58.1 14.5 %collective-permute-start.10 = (bf16[256,256]{0,1:T(8,128)(2,1)S(1)}, bf16[256,256]{0,1:T(8,128)(2,1)S(1)}, u32[]{:S(2)}, u32[]{:S(2)}) collective-permute-start(bf16[256,256]{0,1:T(8,128)(2,1)S(1)} %add_convert_fusion.2), channel_id=1, source_target_pairs={{0,1},{1,0},{2,3},{3,2},{4,5},{5,4},{6,7},{7,6},{8,9},{9,8},{10,11... | collective-permute-start | bytes 393224 | tf_op jit(solution)/shard_map/ppermute | solution.py:114
  58.2 16.5 %collective-permute-start.12 = (bf16[128,1024]{1,0:T(8,128)(2,1)S(1)}, bf16[128,1024]{1,0:T(8,128)(2,1)S(1)}, u32[]{:S(2)}, u32[]{:S(2)}) collective-permute-start(bf16[128,1024]{1,0:T(8,128)(2,1)S(1)} %get-tuple-element.11), channel_id=1, source_target_pairs={{0,4},{4,0},{8,12},{12,8},{1,5},{5,1},{9,13},{13,9},{2,6},{6,2},{1... | collective-permute-start | bytes 786440 | tf_op jit(solution)/shard_map/ppermute | solution.py:92
  59.8 25.2 %collective-permute-start.16 = (bf16[128,1024]{1,0:T(8,128)(2,1)S(1)}, bf16[128,1024]{1,0:T(8,128)(2,1)S(1)}, u32[]{:S(2)}, u32[]{:S(2)}) collective-permute-start(bf16[128,1024]{1,0:T(8,128)(2,1)S(1)} %get-tuple-element.13), channel_id=1, source_target_pairs={{0,4},{4,0},{8,12},{12,8},{1,5},{5,1},{9,13},{13,9},{2,6},{6,2},{1... | collective-permute-start | bytes 786440 | tf_op jit(solution)/shard_map/ppermute | solution.py:92
  60.2 16.1 %collective-permute-start.15 = (bf16[128,1024]{1,0:T(8,128)(2,1)S(1)}, bf16[128,1024]{1,0:T(8,128)(2,1)S(1)}, u32[]{:S(2)}, u32[]{:S(2)}) collective-permute-start(bf16[128,1024]{1,0:T(8,128)(2,1)S(1)} %get-tuple-element.11), channel_id=1, source_target_pairs={{4,8},{8,4},{5,9},{9,5},{6,10},{10,6},{7,11},{11,7},{20,24},{24,20... | collective-permute-start | bytes 786440 | tf_op jit(solution)/shard_map/ppermute | solution.py:94
  71.3 12.8 %collective-permute-start.14 = (bf16[128,1024]{1,0:T(8,128)(2,1)}, bf16[128,1024]{1,0:T(8,128)(2,1)S(1)}, u32[]{:S(2)}, u32[]{:S(2)}) collective-permute-start(bf16[128,1024]{1,0:T(8,128)(2,1)} %copy-done.3), channel_id=1, source_target_pairs={{4,0},{8,12},{5,1},{9,13},{6,2},{10,14},{7,3},{11,15},{20,16},{24,... | collective-permute-start | bytes 786440 | tf_op jit(solution)/shard_map/ppermute | solution.py:93
  72.6 12.8 %collective-permute-start.19 = (bf16[128,1024]{1,0:T(8,128)(2,1)S(1)}, bf16[128,1024]{1,0:T(8,128)(2,1)S(1)}, u32[]{:S(2)}, u32[]{:S(2)}) collective-permute-start(bf16[128,1024]{1,0:T(8,128)(2,1)S(1)} %get-tuple-element.13), channel_id=1, source_target_pairs={{4,8},{8,4},{5,9},{9,5},{6,10},{10,6},{7,11},{11,7},{20,24},{24,20... | collective-permute-start | bytes 786440 | tf_op jit(solution)/shard_map/ppermute | solution.py:94
  73.4 1.0 copy-start.4
  74.7 14.6 %collective-permute-start.18 = (bf16[128,1024]{1,0:T(8,128)(2,1)S(1)}, bf16[128,1024]{1,0:T(8,128)(2,1)S(1)}, u32[]{:S(2)}, u32[]{:S(2)}) collective-permute-start(bf16[128,1024]{1,0:T(8,128)(2,1)S(1)} %collective-permute-done.17), channel_id=1, source_target_pairs={{4,0},{8,12},{5,1},{9,13},{6,2},{10,14},{7,3},{11,15},{20,16},{24,... | collective-permute-start | bytes 786440 | tf_op jit(solution)/shard_map/ppermute | solution.py:93
  89.6 1.0 copy-start.2
  89.7 2.1 %collective-permute-start.20 = (f32[256,256]{0,1:T(8,128)S(1)}, f32[256,256]{0,1:T(8,128)S(1)}, u32[]{:S(2)}, u32[]{:S(2)}) collective-permute-start(f32[256,256]{0,1:T(8,128)S(1)} %constant_dynamic-slice_fusion.3), channel_id=1, source_target_pairs={{0,1},{1,0},{2,3},{3,2},{4,5},{5,4},{6,7},{7,6},{8,9},{9,8},{10,11... | collective-permute-start | bytes 786440 | tf_op jit(solution)/shard_map/ppermute | solution.py:108
  91.8 20.9 %collective-permute-start.32 = (f32[128,64]{0,1:T(8,128)}, f32[128,64]{0,1:T(8,128)}, u32[]{:S(2)}, u32[]{:S(2)}) collective-permute-start(f32[128,64]{0,1:T(8,128)} %fusion.4), channel_id=1, source_target_pairs={{0,1},{1,0},{2,3},{3,2},{4,5},{5,4},{6,7},{7,6},{8,9},{9,8},{10,11... | collective-permute-start | bytes 98312 | tf_op jit(solution)/shard_map/ppermute | solution.py:174
  91.8 3.6 %copy-start.6 = (s32[1,4]{1,0:T(1,128)S(1)}, s32[1,4]{1,0:T(1,128)}, u32[]{:S(2)}) copy-start(s32[1,4]{1,0:T(1,128)} %param.15) | copy-start | bytes 52
  91.9 7.3 %collective-permute-start.21 = (bf16[256,256]{0,1:T(8,128)(2,1)S(1)}, bf16[256,256]{0,1:T(8,128)(2,1)S(1)}, u32[]{:S(2)}, u32[]{:S(2)}) collective-permute-start(bf16[256,256]{0,1:T(8,128)(2,1)S(1)} %add_convert_fusion.1), channel_id=1, source_target_pairs={{0,18},{18,0},{2,16},{16,2},{1,19},{19,1},{3,17},{17,3},{4,22},{22... | collective-permute-start | bytes 393224 | tf_op jit(solution)/shard_map/ppermute | solution.py:109
  92.4 8.2 %collective-permute-start.22 = (bf16[256,256]{0,1:T(8,128)(2,1)S(1)}, bf16[256,256]{0,1:T(8,128)(2,1)S(1)}, u32[]{:S(2)}, u32[]{:S(2)}) collective-permute-start(bf16[256,256]{0,1:T(8,128)(2,1)S(1)} %add_convert_fusion.1), channel_id=1, source_target_pairs={{0,2},{2,0},{1,3},{3,1},{4,6},{6,4},{5,7},{7,5},{8,10},{10,8},{9,1... | collective-permute-start | bytes 393224 | tf_op jit(solution)/shard_map/ppermute | solution.py:109
  93.9 7.6 %collective-permute-start.23 = (bf16[256,256]{0,1:T(8,128)(2,1)S(1)}, bf16[256,256]{0,1:T(8,128)(2,1)S(1)}, u32[]{:S(2)}, u32[]{:S(2)}) collective-permute-start(bf16[256,256]{0,1:T(8,128)(2,1)S(1)} %add_convert_fusion.1), channel_id=1, source_target_pairs={{0,16},{16,0},{1,17},{17,1},{2,18},{18,2},{3,19},{19,3},{4,20},{20... | collective-permute-start | bytes 393224 | tf_op jit(solution)/shard_map/ppermute | solution.py:109
  95.6 13.9 %collective-permute-start.26 = (bf16[128,1024]{1,0:T(8,128)(2,1)S(1)}, bf16[128,1024]{1,0:T(8,128)(2,1)S(1)}, u32[]{:S(2)}, u32[]{:S(2)}) collective-permute-start(bf16[128,1024]{1,0:T(8,128)(2,1)S(1)} %get-tuple-element.15), channel_id=1, source_target_pairs={{0,8},{8,0},{4,12},{12,4},{1,9},{9,1},{5,13},{13,5},{2,10},{10,2},... | collective-permute-start | bytes 786440 | tf_op jit(solution)/shard_map/ppermute | solution.py:91
  101.6 0.8 copy-start.5
  101.6 9.9 %collective-permute-start.24 = (bf16[256,256]{0,1:T(8,128)(2,1)S(1)}, bf16[256,256]{0,1:T(8,128)(2,1)}, u32[]{:S(2)}, u32[]{:S(2)}) collective-permute-start(bf16[256,256]{0,1:T(8,128)(2,1)S(1)} %add_convert_fusion), channel_id=1, source_target_pairs={{0,1},{1,0},{2,3},{3,2},{4,5},{5,4},{6,7},{7,6},{8,9},{9,8},{10,11... | collective-permute-start | bytes 393224 | tf_op jit(solution)/shard_map/ppermute | solution.py:114
  102.5 15.6 %collective-permute-start.25 = (bf16[128,1024]{1,0:T(8,128)(2,1)S(1)}, bf16[128,1024]{1,0:T(8,128)(2,1)S(1)}, u32[]{:S(2)}, u32[]{:S(2)}) collective-permute-start(bf16[128,1024]{1,0:T(8,128)(2,1)S(1)} %get-tuple-element.15), channel_id=1, source_target_pairs={{0,4},{4,0},{8,12},{12,8},{1,5},{5,1},{9,13},{13,9},{2,6},{6,2},{1... | collective-permute-start | bytes 786440 | tf_op jit(solution)/shard_map/ppermute | solution.py:92
  109.5 11.0 %collective-permute-start.28 = (bf16[128,1024]{1,0:T(8,128)(2,1)S(1)}, bf16[128,1024]{1,0:T(8,128)(2,1)S(1)}, u32[]{:S(2)}, u32[]{:S(2)}) collective-permute-start(bf16[128,1024]{1,0:T(8,128)(2,1)S(1)} %get-tuple-element.15), channel_id=1, source_target_pairs={{4,8},{8,4},{5,9},{9,5},{6,10},{10,6},{7,11},{11,7},{20,24},{24,20... | collective-permute-start | bytes 786440 | tf_op jit(solution)/shard_map/ppermute | solution.py:94
  110.2 11.2 %collective-permute-start.27 = (bf16[128,1024]{1,0:T(8,128)(2,1)S(1)}, bf16[128,1024]{1,0:T(8,128)(2,1)S(1)}, u32[]{:S(2)}, u32[]{:S(2)}) collective-permute-start(bf16[128,1024]{1,0:T(8,128)(2,1)S(1)} %collective-permute-done.26), channel_id=1, source_target_pairs={{4,0},{8,12},{5,1},{9,13},{6,2},{10,14},{7,3},{11,15},{20,16},{24,... | collective-permute-start | bytes 786440 | tf_op jit(solution)/shard_map/ppermute | solution.py:93
  114.5 8.7 %collective-permute-start.33 = (bf16[4,4096]{1,0:T(4,128)(2,1)}, bf16[4,4096]{1,0:T(4,128)(2,1)S(1)}, u32[]{:S(2)}, u32[]{:S(2)}) collective-permute-start(bf16[4,4096]{1,0:T(4,128)(2,1)} %convert_element_type.82), channel_id=1, source_target_pairs={{0,4},{4,0},{8,12},{12,8},{1,5},{5,1},{9,13},{13,9},{2,6},{6,2},{1... | collective-permute-start | bytes 98312 | tf_op jit(solution)/shard_map/ppermute | solution.py:176
  117.2 8.5 %collective-permute-start.34 = (bf16[4,4096]{1,0:T(4,128)(2,1)}, bf16[4,4096]{1,0:T(4,128)(2,1)S(1)}, u32[]{:S(2)}, u32[]{:S(2)}) collective-permute-start(bf16[4,4096]{1,0:T(4,128)(2,1)} %convert_element_type.82), channel_id=1, source_target_pairs={{0,8},{8,0},{4,12},{12,4},{1,9},{9,1},{5,13},{13,5},{2,10},{10,2},... | collective-permute-start | bytes 98312 | tf_op jit(solution)/shard_map/ppermute | solution.py:176
  118.1 7.5 %collective-permute-start.35 = (bf16[4,4096]{1,0:T(4,128)(2,1)}, bf16[4,4096]{1,0:T(4,128)(2,1)S(1)}, u32[]{:S(2)}, u32[]{:S(2)}) collective-permute-start(bf16[4,4096]{1,0:T(4,128)(2,1)} %convert_element_type.82), channel_id=1, source_target_pairs={{0,12},{12,0},{4,8},{8,4},{1,13},{13,1},{5,9},{9,5},{2,14},{14,2},... | collective-permute-start | bytes 98312 | tf_op jit(solution)/shard_map/ppermute | solution.py:176
  122.0 9.8 %collective-permute-start.29 = (bf16[128,1024]{1,0:T(8,128)(2,1)S(1)}, bf16[128,1024]{1,0:T(8,128)(2,1)S(1)}, u32[]{:S(2)}, u32[]{:S(2)}) collective-permute-start(bf16[128,1024]{1,0:T(8,128)(2,1)S(1)} %constant_dynamic-slice_fusion.2), channel_id=1, source_target_pairs={{0,16},{16,0},{1,17},{17,1},{2,18},{18,2},{3,19},{19,3},{4,20},{20... | collective-permute-start | bytes 786440 | tf_op jit(solution)/shard_map/ppermute | solution.py:162
  122.6 9.3 %collective-permute-start.30 = (bf16[128,1024]{1,0:T(8,128)(2,1)S(1)}, bf16[128,1024]{1,0:T(8,128)(2,1)S(1)}, u32[]{:S(2)}, u32[]{:S(2)}) collective-permute-start(bf16[128,1024]{1,0:T(8,128)(2,1)S(1)} %get-tuple-element.25), channel_id=1, source_target_pairs={{0,2},{2,0},{1,3},{3,1},{4,6},{6,4},{5,7},{7,5},{8,10},{10,8},{9,1... | collective-permute-start | bytes 786440 | tf_op jit(solution)/shard_map/ppermute | solution.py:160
  123.2 12.8 %collective-permute-start.31 = (bf16[128,1024]{1,0:T(8,128)(2,1)S(1)}, bf16[128,1024]{1,0:T(8,128)(2,1)}, u32[]{:S(2)}, u32[]{:S(2)}) collective-permute-start(bf16[128,1024]{1,0:T(8,128)(2,1)S(1)} %get-tuple-element.24), channel_id=1, source_target_pairs={{0,18},{18,0},{2,16},{16,2},{1,19},{19,1},{3,17},{17,3},{4,22},{22... | collective-permute-start | bytes 786440 | tf_op jit(solution)/shard_map/ppermute | solution.py:161
  137.0 1.0 copy-start.1

commit v2 on v1

--- a/solution.py
+++ b/solution.py
@@ -1,14 +1,15 @@
 import jax
 import jax.numpy as jnp
 from jax import lax
+from jax.experimental import pallas as pl
+from jax.experimental.pallas import tpu as pltpu
 from jax.sharding import PartitionSpec as P
 
 F32 = jnp.float32
 BF16 = jnp.bfloat16
-STEP = ((0, 1), (1, 0), (2, 3), (3, 2))
-MIDDLE = ((1, 2), (2, 1))
-TWO = ((0, 2), (2, 0), (1, 3), (3, 1))
-ENDS = ((1, 0), (2, 3))
+UP = ((0, 1), (1, 2), (2, 3), (3, 0))
+DOWN = ((1, 0), (2, 1), (3, 2), (0, 3))
+OPPOSITE = ((0, 2), (2, 0), (1, 3), (3, 1))
 ACROSS = ((0, 3), (3, 0), (1, 2), (2, 1))
 PAIR = ((0, 1), (1, 0))
 
@@ -19,6 +20,10 @@
 
 def after(x, *first):
     return lax.optimization_barrier((x, *first))[0]
+
+
+def after2(xs, *first):
+    return lax.optimization_barrier((*xs, *first))[: len(xs)]
 
 
 def shifted(shard, axis, by):
@@ -85,34 +90,153 @@
     return (kept_adjoint[None], scores[None])
 
 
-def gathered(w, *first):
-    z = lax.axis_index("dp")
-    w = after(w, *first)
-    two = lax.ppermute(w, "dp", TWO)
-    one = lax.ppermute(w, "dp", STEP)
-    ends = lax.ppermute(two, "dp", ENDS)
-    middle = lax.ppermute(after(w, two), "dp", MIDDLE)
-    far = jnp.where((z == 0) | (z == 3), ends, middle)
-    return [w, one, two, far]
+def gathered(w, name):
+    half = w.shape[0] // 2
+    with jax.named_scope(name):
+        below, above = lax.ppermute(w, "dp", UP), lax.ppermute(w, "dp", DOWN)
+        upper, lower = lax.ppermute(below[:half], "dp", UP), lax.ppermute(above[half:], "dp", DOWN)
+    return [w, below, above, upper, lower]
 
 
 def plane(axis):
     return (axis, PAIR) if axis != "both" else (("group", "section"), ACROSS)
 
 
-def summed(part):
-    core = lax.axis_index("mp")
-    half = part.shape[1] // 2
-    keep = lax.dynamic_slice_in_dim(part, core * half, half, 1)
-    send = lax.dynamic_slice_in_dim(part, (1 - core) * half, half, 1)
-    own = (keep + lax.ppermute(send, "mp", PAIR)).astype(BF16)
+def summed(keep, send, gate1, gate2):
+    own = after((keep + lax.ppermute(send, "mp", PAIR)).astype(BF16), *gate1)
     others = [lax.ppermute(own, *plane(a)) for a in ("both", "section", "group")]
     total = own.astype(F32)
     for other in others:
         total = total + other.astype(F32)
-    total = total.astype(BF16)
-    other = lax.ppermute(total, "mp", PAIR)
-    return jnp.where(core == 0, jnp.concatenate([total, other], 1), jnp.concatenate([other, total], 1))
+    total = after(total.astype(BF16), *gate2)
+    return total, lax.ppermute(total, "mp", PAIR)
+
+
+class Copies:
+    def __init__(self, sems):
+        self.sems, self.used, self.waits = sems, 0, []
+
+    def start(self, pairs):
+        for src, dst in pairs:
+            copy = pltpu.make_async_copy(src, dst, self.sems.at[self.used])
+            copy.start()
+            self.waits.append(copy)
+            self.used += 1
+
+    def start_either(self, which, ifs, elses):
+        first = self.used
+        for holds, pairs in ((which, ifs), (jnp.logical_not(which), elses)):
+
+            @pl.when(holds)
+            def _():
+                for k, (src, dst) in enumerate(pairs):
+                    pltpu.make_async_copy(src, dst, self.sems.at[first + k]).start()
+
+        for k, (src, dst) in enumerate(ifs):
+            self.waits.append(pltpu.make_async_copy(src, dst, self.sems.at[first + k]))
+        self.used += len(ifs)
+
+    def wait(self):
+        for copy in self.waits:
+            copy.wait()
+        self.waits = []
+
+
+def rows_into(slot, dst, which=0):
+    n, starts = dst.shape[0] // 8, []
+    for ref in slot[:3]:
+        starts += [(ref, which * n), (ref, ref.shape[0] // 2 + which * n)]
+    starts += [(ref, which * n) for ref in slot[3:]]
+    return [(ref.at[pl.ds(at, n)], dst.at[pl.ds(k * n, n)]) for k, (ref, at) in enumerate(starts)]
+
+
+def halves_into(mine, other, dst, core):
+    half = mine.shape[1]
+    return [
+        (mine, dst.at[:, pl.ds(pl.multiple_of(core * half, half), half)]),
+        (other, dst.at[:, pl.ds(pl.multiple_of((1 - core) * half, half), half)]),
+    ]
+
+
+def groups_into(own, other, dst, y):
+    n = own.shape[0]
+    return [
+        (own, dst.at[pl.ds(pl.multiple_of(y * n, n), n)]),
+        (other, dst.at[pl.ds(pl.multiple_of((1 - y) * n, n), n)]),
+    ]
+
+
+def write_part(adjoint, vs, keep, send, part, core):
+    half = keep.shape[1]
+    for k in range(2):
+        part[k] = dot_t(adjoint[...], vs[k * half : (k + 1) * half, :])
+    keep[...] = part[core]
+    send[...] = part[1 - core]
+
+
+def add_ranked(adjoint, rank, us, out, step):
+    for at in range(0, adjoint.shape[1], step):
+        columns = slice(at, at + step)
+        delta = jnp.dot(rank[...], us[:, columns], preferred_element_type=F32)
+        out[:, columns] = (adjoint[:, columns].astype(F32) + delta).astype(BF16)
+
+
+def first_kernel(flags, g_own, g_other, *refs):
+    slot1, slot2, (keep, send, g, vs, part, sems) = refs[:5], refs[5:10], refs[10:]
+    last, y, core = flags[0] == 1, flags[1], flags[2]
+    copies = Copies(sems)
+    copies.start(groups_into(g_own, g_other, g, y))
+    copies.start_either(last, rows_into(slot1, vs), rows_into(slot2, vs))
+    copies.wait()
+    write_part(g, vs, keep, send, part, core)
+
+
+def middle_kernel(flags, g_own, g_other, mine, other, *refs):
+    slot1, slot2, rest = refs[:5], refs[5:10], refs[10:15]
+    adjoint, keep, send, g, rank, us, vs, part, sems = refs[15:]
+    last, y, core = flags[0] == 1, flags[1], flags[2]
+    copies = Copies(sems)
+    copies.start(groups_into(g_own, g_other, g, y) + halves_into(mine, other, rank, core))
+    copies.start_either(last, rows_into(slot2, us), rows_into(rest, us))
+    copies.start_either(last, rows_into(rest, vs), rows_into(slot1, vs))
+    copies.wait()
+    add_ranked(g, rank, us, adjoint, 256)
+    write_part(adjoint, vs, keep, send, part, core)
+
+
+def last_kernel(flags, adjoint1, mine, other, *refs):
+    rest, (here, to_x, to_xy, to_y, kept, rank, us, adjoint0, sems) = refs[:5], refs[5:]
+    last, y, core = flags[0] == 1, flags[1], flags[2]
+    n = here.shape[0]
+    copies = Copies(sems)
+    copies.start([(adjoint1, kept)] + halves_into(mine, other, rank, core))
+    copies.start(rows_into(rest, us, 1))
+    copies.wait()
+    add_ranked(kept, rank, us, adjoint0, 256)
+
+    def sends(own, others):
+        return [
+            (others.at[pl.ds(pl.multiple_of(y * n, n), n)], to_x),
+            (others.at[pl.ds(pl.multiple_of((1 - y) * n, n), n)], to_xy),
+            (own.at[pl.ds(pl.multiple_of((1 - y) * n, n), n)], to_y),
+            (own.at[pl.ds(pl.multiple_of(y * n, n), n)], here),
+        ]
+
+    copies.start_either(last, sends(kept, adjoint0), sends(adjoint0, kept))
+    copies.wait()
+
+
+def kernel_call(body, name, outs, scratch, copies, flags, *args):
+    anywhere = pl.BlockSpec(memory_space=pltpu.HBM)
+    return pl.pallas_call(
+        body,
+        name=name,
+        out_shape=[o for o, _ in outs],
+        in_specs=[pl.BlockSpec(memory_space=pltpu.SMEM)] + [anywhere] * len(args),
+        out_specs=[anywhere if far else pl.BlockSpec(memory_space=pltpu.VMEM) for _, far in outs],
+        scratch_shapes=[pltpu.VMEM(*shape) for shape in scratch] + [pltpu.SemaphoreType.DMA((copies,))],
+        compiler_params=pltpu.CompilerParams(vmem_limit_bytes=16 << 20),
+    )(flags, *[pltpu.with_memory_space_constraint(a, pltpu.HBM) for a in args])
 
 
 def spread(acts, cotangent, in_weight, out_weight, in_factor, out_factor, damping, lengths):
@@ -125,55 +249,67 @@
         return lax.dynamic_slice_in_dim(a, (px * 2 + py) * slice_width, slice_width, 1)
 
     v_own, u_own = out_weight[0], in_weight[0]
+    last = x == 1
+
+    n = v_own.shape[0]
     v_keep, u_keep = piece(v_own, x, y), piece(u_own, x, y)
+    slot1 = gathered(v_keep, "slot1")
     v_other = lax.ppermute(piece(v_own, 1 - x, y), "section", PAIR)
     u_other = lax.ppermute(piece(u_own, 1 - x, y), "section", PAIR)
-    last = x == 1
-    v1, v0 = jnp.where(last, v_keep, v_other), jnp.where(last, v_other, v_keep)
-    u1, u0 = jnp.where(last, u_keep, u_other), jnp.where(last, u_other, u_keep)
     g_own = piece(cotangent, x, y)
     g_other = lax.ppermute(piece(cotangent, x, 1 - y), "group", PAIR)
-    g = jnp.where(y == 0, jnp.concatenate([g_own, g_other], 0), jnp.concatenate([g_other, g_own], 0))
-
-    v1s = gathered(v1)
-    u1s = gathered(u1, v1s[2])
-    v0s = gathered(v0, u1s[2])
-    u0s = gathered(u0, v0s[2])
-
-    def step(adjoint, vs, us):
-        part = jnp.concatenate([dot_t(adjoint, v) for v in vs], 1)
-        rank = summed(part)
-        block = rank.shape[1] // 4
-        total = adjoint.astype(F32)
-        for k, u in enumerate(us):
-            total = total + jnp.dot(rank[:, k * block : (k + 1) * block], u, preferred_element_type=F32)
-        return rank, total.astype(BF16)
-
-    rank1, adjoint1 = step(g, v1s, u1s)
-    rank0, adjoint0 = step(adjoint1, v0s, u0s)
+    slot2 = gathered(jnp.where(last, u_keep, v_other), "slot2")
+    u_keep, v_other, u_other = after2((u_keep, v_other, u_other), slot1[1])
+    h = n // 2
+    third, fourth = jnp.where(last, v_other, u_other), jnp.where(last, u_other, u_keep)
+    rest = gathered(jnp.concatenate([third[:h], fourth[:h], third[h:], fourth[h:]], 0), "slot34")
+
+    flags = jnp.stack([x, y, lax.axis_index("mp")]).astype(jnp.int32)
+    groups = lax.axis_size("group")
+    ranks = 4 * n
+    tokens = groups * tok_rows
+    half_part = jax.ShapeDtypeStruct((tokens, ranks // 2), F32)
+    shape_of = jax.ShapeDtypeStruct((tokens, slice_width), BF16)
+    send_of = jax.ShapeDtypeStruct((tok_rows, slice_width), BF16)
+    wide, rank_of = ((tokens, slice_width), BF16), ((tokens, ranks), BF16)
+    weight, part_of = ((ranks, slice_width), BF16), ((2, tokens, ranks // 2), F32)
+
+    keep, send = kernel_call(
+        first_kernel, "first", [(half_part, False)] * 2, [wide, weight, part_of], 10, flags, g_own, g_other, *slot1, *slot2
+    )
+    mine1, other1 = summed(keep, send, rest[1:2], rest[3:])
+    adjoint1, keep, send = kernel_call(
+        middle_kernel, "middle", [(shape_of, False), (half_part, False), (half_part, False)],
+        [wide, rank_of, weight, weight, part_of], 20, flags, g_own, g_other, mine1, other1, *slot1, *slot2, *rest,
+    )
+    mine0, other0 = summed(keep, send, (), ())
+    here, to_x, to_xy, to_y = kernel_call(
+        last_kernel, "last", [(send_of, True)] * 4, [wide, rank_of, weight, wide], 15, flags, adjoint1, mine0, other0, *rest
+    )
+    from_xy = lax.ppermute(to_xy, *plane("both"))
+    from_x = lax.ppermute(to_x, *plane("section"))
+    from_y = lax.ppermute(to_y, *plane("group"))
 
     def of_group(a, who):
         return lax.dynamic_slice_in_dim(a, who * tok_rows, tok_rows, 0)
 
-    mine, theirs = jnp.where(last, adjoint1, adjoint0), jnp.where(last, adjoint0, adjoint1)
-    here = of_group(mine, y)
-    from_x = lax.ppermute(of_group(theirs, y), *plane("section"))
-    from_xy = lax.ppermute(of_group(theirs, 1 - y), *plane("both"))
-    from_y = lax.ppermute(of_group(mine, 1 - y), *plane("group"))
     adjoint = jnp.zeros_like(cotangent)
     for value, px, py in ((here, x, y), (from_y, x, 1 - y), (from_x, 1 - x, y), (from_xy, 1 - x, 1 - y)):
         adjoint = lax.dynamic_update_slice_in_dim(adjoint, value, (px * 2 + py) * slice_width, 1)
 
-    rank = of_group(jnp.where(last, rank1, rank0), y)
+    core = lax.axis_index("mp")
+    mine, other = of_group(jnp.where(last, mine1, mine0), y), of_group(jnp.where(last, other1, other0), y)
+    rank = jnp.where(core == 0, jnp.concatenate([mine, other], 1), jnp.concatenate([other, mine], 1))
     block = out_factor.shape[2] // 4
     factor = jnp.concatenate(
-        [lax.dynamic_slice_in_dim(out_factor[0], jnp.bitwise_xor(z, k) * block, block, 1) for k in range(4)], 1
+        [lax.dynamic_slice_in_dim(out_factor[0], lax.rem(z + k, 4) * block, block, 1) for k in (0, 3, 1, 2)], 1
     )
     out_proj = dot_t(rank, factor)
     in_part = dot_t(acts[0], in_factor[0])
     in_proj = in_part + lax.ppermute(in_part, "mp", PAIR)
     rows = own_rows(out_proj, in_proj, lengths[0])
-    every_row = jnp.concatenate([rows] + [lax.ppermute(rows, "dp", p) for p in (STEP, TWO, ACROSS)], 0)
+    every_row = jnp.concatenate([rows] + [lax.ppermute(rows, "dp", p) for p in (UP, DOWN, OPPOSITE)], 0)
+    every_row = after(every_row, from_x, from_y)
     scores = scores_of(every_row, damping[0], 0, examples, tok_rows)
     return (adjoint[None], scores[None])
 

time: 139 us -> 120 us (0.86)
  waiting for transfers between devices: 72.3 us -> 54.5 us
  Pallas kernels: 0 us -> 8.28 us
  matrix products: 9.47 us -> 1.99 us
  other arithmetic: 9.06 us -> 5.74 us
  starting transfers between devices: 37.3 us -> 39.2 us
    ppermute x23 -> x19, waiting for transfers between devices: 60.2 us -> 48.6 us  [the longest x6 24 us: gathered(): below, above = (lax.ppermute(w, 'dp', UP), lax.ppermute(w, 'dp', DOWN))]
    pallas_call x0 -> x3, Pallas kernels: none -> 8.28 us  [kernel_call(): pl.pallas_call(body, name=name, out_shape=[o for o, _ in outs], in_specs=...]
    ppermute x1, waiting for transfers between devices: 6.31 us -> 0.01 us  [spread(): v_other = lax.ppermute(piece(v_own, 1 - x, y), 'section', PAIR)]
    ppermute x23 -> x19, starting transfers between devices: 18.8 us -> 22.8 us  [the longest x6 12.7 us: gathered(): below, above = (lax.ppermute(w, 'dp', UP), lax.ppermute(w, 'dp', DOWN))]
    dot_general x11 -> x3, matrix products: 4.83 us -> 0.81 us  [dot_t(): lax.dot_general(a, b, (((1,), (1,)), ((), ())), preferred_element_type=F3...]
    dot_general x8 -> x0, matrix products: 2.66 us -> none  [step(): jnp.dot(rank[:, k * block:(k + 1) * block], u, preferred_element_type=F32)]
    select_n x5 -> x4, other arithmetic: 3.62 us -> 1.12 us  [the longest x1 1.02 us: spread(): slot2 = gathered(jnp.where(last, u_keep, v_other), 'slot2')]
    dynamic_slice x2 -> x3, local copies, waits for them, and re-layouts: 2.73 us -> 3.87 us  [piece(): lax.dynamic_slice_in_dim(a, (px * 2 + py) * slice_width, slice_width, 1)]
  transfers between devices with their start and end apart: 36 -> 32, of which waited for: 14 -> 18; matrix products, arithmetic and copies ran while one was open for 14% -> 9% of each run, Pallas kernels for 0% -> 4%
where the time goes in v2:
time: 120 us
  waiting for transfers between devices  54.5 us (45%)
  starting transfers between devices  39.2 us (33%)
  Pallas kernels  8.28 us (7%)
  local copies, waits for them, and re-layouts  8.09 us (7%)
  other arithmetic  5.74 us (5%)
  matrix products  1.99 us (2%)
  between operations  1.81 us (2%)
    ppermute x6, waiting for transfers between devices, gathered(): below, above = (lax.ppermute(w, 'dp', UP), lax.ppermute(w, 'dp', DOWN))  24 us
    ppermute x6, starting transfers between devices, gathered(): below, above = (lax.ppermute(w, 'dp', UP), lax.ppermute(w, 'dp', DOWN))  12.7 us
    pallas_call x3, Pallas kernels, kernel_call(): pl.pallas_call(body, name=name, out_shape=[o for o, _ in outs], in_specs=...  8.28 us
    ppermute x3, waiting for transfers between devices, gathered(): lax.ppermute(above[half:], 'dp', DOWN)  8.1 us
    ppermute x3, waiting for transfers between devices, gathered(): lax.ppermute(below[:half], 'dp', UP)  7.87 us
    ppermute x6, starting transfers between devices, summed(): lax.ppermute(own, *plane(a))  7.04 us
    ppermute x3, starting transfers between devices, gathered(): lax.ppermute(above[half:], 'dp', DOWN)  5.94 us
    ppermute x6, waiting for transfers between devices, summed(): lax.ppermute(own, *plane(a))  5.86 us
  transfers between devices with their start and end apart: 32, of which 18 were waited for; matrix products, arithmetic and copies ran while one was open for 9% of the time, Pallas kernels for 4%

profile of v2, /device:TPU:0, one launch (start us, length us, event | category | flops | bytes accessed | tf_op | source)
XLA Modules:
  0.0 119.6 jit_solution(9405263929766204470)
XLA Ops:
  0.7 1.2 dynamic-slice_bitcast_fusion.1
  1.8 3.0 %collective-permute-start.5 = (bf16[128,1024]{1,0:T(8,128)(2,1)S(1)}, bf16[128,1024]{1,0:T(8,128)(2,1)S(1)}, u32[]{:S(2)}, u32[]{:S(2)}) collective-permute-start(bf16[128,1024]{1,0:T(8,128)(2,1)S(1)} %get-tuple-element.34), channel_id=1, source_target_pairs={{0,2},{2,0},{1,3},{3,1},{4,6},{6,4},{5,7},{7,5},{8,10},{10,8},{9,1... | collective-permute-start | bytes 786440 | tf_op jit(solution)/shard_map/ppermute | solution.py:257
  4.8 1.6 %collective-permute-start.1 = (bf16[128,1024]{1,0:T(8,128)(2,1)S(1)}, bf16[128,1024]{1,0:T(8,128)(2,1)S(1)}, u32[]{:S(2)}, u32[]{:S(2)}) collective-permute-start(bf16[128,1024]{1,0:T(8,128)(2,1)S(1)} %get-tuple-element.35.refs_0_), channel_id=1, source_target_pairs={{0,4},{4,8},{8,12},{12,0},{1,5},{5,9},{9,13},{13,1},{2,6},{6,10},{... | collective-permute-start | bytes 786440 | tf_op jit(solution)/shard_map/slot1/ppermute | solution.py:96
  6.4 2.2 %collective-permute-start.2 = (bf16[128,1024]{1,0:T(8,128)(2,1)S(1)}, bf16[128,1024]{1,0:T(8,128)(2,1)S(1)}, u32[]{:S(2)}, u32[]{:S(2)}) collective-permute-start(bf16[128,1024]{1,0:T(8,128)(2,1)S(1)} %get-tuple-element.35.refs_0_), channel_id=1, source_target_pairs={{4,0},{8,4},{12,8},{0,12},{5,1},{9,5},{13,9},{1,13},{6,2},{10,6},{... | collective-permute-start | bytes 786440 | tf_op jit(solution)/shard_map/slot1/ppermute | solution.py:96
  8.7 1.0 dynamic-slice_bitcast_fusion
  9.6 0.4 collective-permute-start.11
  10.0 1.8 %constant_dynamic-slice_fusion = (bf16[128,1024]{1,0:T(8,128)(2,1)S(1)}, bf16[128,1024]{1,0:T(8,128)(2,1)}) fusion(bf16[128,4096]{1,0:T(8,128)(2,1)} %param.9, s32[]{:T(128)S(6)} %select_n.79, s32[]{:T(128)S(6)} %select_n.78), kind=kLoop, calls=%fused_computation.59 | loop fusion | bytes 1048584 | tf_op jit(solution)/shard_map/dynamic_slice | solution.py:249
  11.8 1.7 %collective-permute-start = (bf16[128,1024]{1,0:T(8,128)(2,1)S(1)}, bf16[128,1024]{1,0:T(8,128)(2,1)}, u32[]{:S(2)}, u32[]{:S(2)}) collective-permute-start(bf16[128,1024]{1,0:T(8,128)(2,1)S(1)} %get-tuple-element.36), channel_id=1, source_target_pairs={{0,16},{16,0},{1,17},{17,1},{2,18},{18,2},{3,19},{19,3},{4,20},{20... | collective-permute-start | bytes 786440 | tf_op jit(solution)/shard_map/ppermute | solution.py:260
  13.5 1.0 broadcast_select_fusion.2
  14.5 0.6 collective-permute-start.6
  15.2 0.7 collective-permute-done.1.refs_1_
  15.9 4.7 %collective-permute-start.7 = (bf16[128,1024]{1,0:T(8,128)(2,1)S(1)}, bf16[128,1024]{1,0:T(8,128)(2,1)S(1)}, u32[]{:S(2)}, u32[]{:S(2)}) collective-permute-start(bf16[128,1024]{1,0:T(8,128)(2,1)S(1)} %get-tuple-element.32.refs_5_), channel_id=1, source_target_pairs={{4,0},{8,4},{12,8},{0,12},{5,1},{9,5},{13,9},{1,13},{6,2},{10,6},{... | collective-permute-start | bytes 786440 | tf_op jit(solution)/shard_map/slot2/ppermute | solution.py:96
  20.7 1.2 collective-permute-done.2.refs_2_
  21.9 2.7 %collective-permute-start.4 = (bf16[64,1024]{1,0:T(8,128)(2,1)S(1)}, bf16[64,1024]{1,0:T(8,128)(2,1)S(1)}, u32[]{:S(2)}, u32[]{:S(2)}) collective-permute-start(bf16[64,1024]{1,0:T(8,128)(2,1)S(1)} %slice.57), channel_id=1, source_target_pairs={{4,0},{8,4},{12,8},{0,12},{5,1},{9,5},{13,9},{1,13},{6,2},{10,6},{... | collective-permute-start | bytes 393224 | tf_op jit(solution)/shard_map/slot1/ppermute | solution.py:97
  24.7 2.5 %collective-permute-done.6.refs_6_ = bf16[128,1024]{1,0:T(8,128)(2,1)S(1)} collective-permute-done((bf16[128,1024]{1,0:T(8,128)(2,1)S(1)}, bf16[128,1024]{1,0:T(8,128)(2,1)S(1)}, u32[]{:S(2)}, u32[]{:S(2)}) %collective-permute-start.6) | collective-permute-done | bytes 262176 | tf_op jit(solution)/shard_map/slot2/ppermute | solution.py:96
  27.3 5.6 %collective-permute-done.7.refs_7_ = bf16[128,1024]{1,0:T(8,128)(2,1)S(1)} collective-permute-done((bf16[128,1024]{1,0:T(8,128)(2,1)S(1)}, bf16[128,1024]{1,0:T(8,128)(2,1)S(1)}, u32[]{:S(2)}, u32[]{:S(2)}) %collective-permute-start.7) | collective-permute-done | bytes 262176 | tf_op jit(solution)/shard_map/slot2/ppermute | solution.py:96
  32.9 1.6 %collective-permute-start.9 = (bf16[64,1024]{1,0:T(8,128)(2,1)S(1)}, bf16[64,1024]{1,0:T(8,128)(2,1)S(1)}, u32[]{:S(2)}, u32[]{:S(2)}) collective-permute-start(bf16[64,1024]{1,0:T(8,128)(2,1)S(1)} %slice.59), channel_id=1, source_target_pairs={{4,0},{8,4},{12,8},{0,12},{5,1},{9,5},{13,9},{1,13},{6,2},{10,6},{... | collective-permute-start | bytes 393224 | tf_op jit(solution)/shard_map/slot2/ppermute | solution.py:97
  34.5 0.6 collective-permute-start.12
  35.2 0.4 collective-permute-done.3.refs_3_
  35.6 3.0 %collective-permute-done.4.refs_4_ = bf16[64,1024]{1,0:T(8,128)(2,1)S(1)} collective-permute-done((bf16[64,1024]{1,0:T(8,128)(2,1)S(1)}, bf16[64,1024]{1,0:T(8,128)(2,1)S(1)}, u32[]{:S(2)}, u32[]{:S(2)}) %collective-permute-start.4) | collective-permute-done | bytes 131104 | tf_op jit(solution)/shard_map/slot1/ppermute | solution.py:97
  38.6 2.6 %collective-permute-done.8.refs_8_ = bf16[64,1024]{1,0:T(8,128)(2,1)S(1)} collective-permute-done((bf16[64,1024]{1,0:T(8,128)(2,1)S(1)}, bf16[64,1024]{1,0:T(8,128)(2,1)S(1)}, u32[]{:S(2)}, u32[]{:S(2)}) %collective-permute-start.8) | collective-permute-done | bytes 131104 | tf_op jit(solution)/shard_map/slot2/ppermute | solution.py:97
  41.2 1.5 %collective-permute-done.9.refs_9_ = bf16[64,1024]{1,0:T(8,128)(2,1)S(1)} collective-permute-done((bf16[64,1024]{1,0:T(8,128)(2,1)S(1)}, bf16[64,1024]{1,0:T(8,128)(2,1)S(1)}, u32[]{:S(2)}, u32[]{:S(2)}) %collective-permute-start.9) | collective-permute-done | bytes 131104 | tf_op jit(solution)/shard_map/slot2/ppermute | solution.py:97
  42.7 0.6 copy-done.21
  43.4 2.5 %first.1 = (f32[256,256]{1,0:T(8,128)S(1)}, f32[256,256]{1,0:T(8,128)S(1)}) custom-call(s32[3]{0:T(128)S(1)} %pad_add_fusion.flags, bf16[128,1024]{1,0:T(8,128)(2,1)} %get-tuple-element.37.g_own, bf16[128,1024]{1,0:T(8,128)(2,1)} %collective-permute-done.g_other, bf16[128,1024]{1,0:T(8,128)(2,1)} %copy-done.5, bf16[128,1024]{1,0:T(8,128)(2,1)} %copy-done.7, ...), custom_call_target="tpu_custom_call" | custom-call | tf_op jit(solution)/shard_map/first/pallas_call | solution.py:231
  45.9 2.9 %collective-permute-start.17 = (bf16[256,1024]{1,0:T(8,128)(2,1)S(1)}, bf16[256,1024]{1,0:T(8,128)(2,1)S(1)}, u32[]{:S(2)}, u32[]{:S(2)}) collective-permute-start(bf16[256,1024]{1,0:T(8,128)(2,1)S(1)} %pad_maximum_fusion.refs_10_.refs_0_), channel_id=1, source_target_pairs={{4,0},{8,4},{12,8},{0,12},{5,1},{9,5},{13,9},{1,13},{6,2},{10,6},{... | collective-permute-start | bytes 1572872 | tf_op jit(solution)/shard_map/slot34/ppermute | solution.py:96
  48.9 6.3 %collective-permute-done.12.refs_11_.refs_1_ = bf16[256,1024]{1,0:T(8,128)(2,1)S(1)} collective-permute-done((bf16[256,1024]{1,0:T(8,128)(2,1)S(1)}, bf16[256,1024]{1,0:T(8,128)(2,1)S(1)}, u32[]{:S(2)}, u32[]{:S(2)}) %collective-permute-start.12) | collective-permute-done | bytes 524320 | tf_op jit(solution)/shard_map/slot34/ppermute | solution.py:96
  55.3 1.5 %collective-permute-start.13 = (bf16[256,256]{1,0:T(8,128)(2,1)S(1)}, bf16[256,256]{1,0:T(8,128)(2,1)S(1)}, u32[]{:S(2)}, u32[]{:S(2)}) collective-permute-start(bf16[256,256]{1,0:T(8,128)(2,1)S(1)} %add_convert_fusion.3), channel_id=1, source_target_pairs={{0,18},{18,0},{2,16},{16,2},{1,19},{19,1},{3,17},{17,3},{4,22},{22... | collective-permute-start | bytes 393224 | tf_op jit(solution)/shard_map/ppermute | solution.py:107
  56.8 1.5 %collective-permute-start.14 = (bf16[256,256]{1,0:T(8,128)(2,1)S(1)}, bf16[256,256]{1,0:T(8,128)(2,1)S(1)}, u32[]{:S(2)}, u32[]{:S(2)}) collective-permute-start(bf16[256,256]{1,0:T(8,128)(2,1)S(1)} %add_convert_fusion.3), channel_id=1, source_target_pairs={{0,2},{2,0},{1,3},{3,1},{4,6},{6,4},{5,7},{7,5},{8,10},{10,8},{9,1... | collective-permute-start | bytes 393224 | tf_op jit(solution)/shard_map/ppermute | solution.py:107
  58.3 0.5 collective-permute-start.15
  58.8 7.7 %collective-permute-done.17.refs_12_.refs_2_ = bf16[256,1024]{1,0:T(8,128)(2,1)S(1)} collective-permute-done((bf16[256,1024]{1,0:T(8,128)(2,1)S(1)}, bf16[256,1024]{1,0:T(8,128)(2,1)S(1)}, u32[]{:S(2)}, u32[]{:S(2)}) %collective-permute-start.17) | collective-permute-done | bytes 524320 | tf_op jit(solution)/shard_map/slot34/ppermute | solution.py:96
  66.5 1.7 %collective-permute-start.18 = (bf16[128,1024]{1,0:T(8,128)(2,1)S(1)}, bf16[128,1024]{1,0:T(8,128)(2,1)S(1)}, u32[]{:S(2)}, u32[]{:S(2)}) collective-permute-start(bf16[128,1024]{1,0:T(8,128)(2,1)S(1)} %slice.65), channel_id=1, source_target_pairs={{4,0},{8,4},{12,8},{0,12},{5,1},{9,5},{13,9},{1,13},{6,2},{10,6},{... | collective-permute-start | bytes 786440 | tf_op jit(solution)/shard_map/slot34/ppermute | solution.py:97
  68.4 4.8 %collective-permute-done.16.refs_13_.refs_3_ = bf16[128,1024]{1,0:T(8,128)(2,1)S(1)} collective-permute-done((bf16[128,1024]{1,0:T(8,128)(2,1)S(1)}, bf16[128,1024]{1,0:T(8,128)(2,1)S(1)}, u32[]{:S(2)}, u32[]{:S(2)}) %collective-permute-start.16) | collective-permute-done | bytes 262176 | tf_op jit(solution)/shard_map/slot34/ppermute | solution.py:97
  73.2 3.6 %collective-permute-done.18.refs_14_.refs_4_ = bf16[128,1024]{1,0:T(8,128)(2,1)S(1)} collective-permute-done((bf16[128,1024]{1,0:T(8,128)(2,1)S(1)}, bf16[128,1024]{1,0:T(8,128)(2,1)S(1)}, u32[]{:S(2)}, u32[]{:S(2)}) %collective-permute-start.18) | collective-permute-done | bytes 262176 | tf_op jit(solution)/shard_map/slot34/ppermute | solution.py:97
  76.8 1.3 %collective-permute-done.19.other = bf16[256,256]{1,0:T(8,128)(2,1)S(1)} collective-permute-done((bf16[256,256]{1,0:T(8,128)(2,1)S(1)}, bf16[256,256]{1,0:T(8,128)(2,1)S(1)}, u32[]{:S(2)}, u32[]{:S(2)}) %collective-permute-start.19) | collective-permute-done | bytes 131104 | tf_op jit(solution)/shard_map/ppermute | solution.py:112
  78.2 0.7 copy-done.22
  78.8 3.2 %middle.1 = (bf16[256,1024]{1,0:T(8,128)(2,1)S(1)}, f32[256,256]{1,0:T(8,128)S(1)}, f32[256,256]{1,0:T(8,128)S(1)}) custom-call(s32[3]{0:T(128)S(1)} %pad_add_fusion.flags, bf16[128,1024]{1,0:T(8,128)(2,1)} %get-tuple-element.37.g_own, bf16[128,1024]{1,0:T(8,128)(2,1)} %collective-permute-done.g_other, bf16[256,256]{1,0:T(8,128)(2,1)} %copy-done.14, ...), custom_call_target="tpu_custom_call" | custom-call | tf_op jit(solution)/shard_map/middle/pallas_call | solution.py:231
  82.1 0.2 collective-permute-start.20
  82.3 0.5 fusion.2
  82.9 0.3 collective-permute-start.28
  83.2 0.7 copy-done.26
  84.1 1.4 %collective-permute-start.21 = (bf16[256,256]{1,0:T(8,128)(2,1)S(1)}, bf16[256,256]{1,0:T(8,128)(2,1)S(1)}, u32[]{:S(2)}, u32[]{:S(2)}) collective-permute-start(bf16[256,256]{1,0:T(8,128)(2,1)S(1)} %add_convert_fusion.1), channel_id=1, source_target_pairs={{0,18},{18,0},{2,16},{16,2},{1,19},{19,1},{3,17},{17,3},{4,22},{22... | collective-permute-start | bytes 393224 | tf_op jit(solution)/shard_map/ppermute | solution.py:107
  85.5 1.6 %collective-permute-start.22 = (bf16[256,256]{1,0:T(8,128)(2,1)S(1)}, bf16[256,256]{1,0:T(8,128)(2,1)S(1)}, u32[]{:S(2)}, u32[]{:S(2)}) collective-permute-start(bf16[256,256]{1,0:T(8,128)(2,1)S(1)} %add_convert_fusion.1), channel_id=1, source_target_pairs={{0,2},{2,0},{1,3},{3,1},{4,6},{6,4},{5,7},{7,5},{8,10},{10,8},{9,1... | collective-permute-start | bytes 393224 | tf_op jit(solution)/shard_map/ppermute | solution.py:107
  87.1 0.5 collective-permute-start.23
  87.6 3.7 %collective-permute-done.21 = bf16[256,256]{1,0:T(8,128)(2,1)S(1)} collective-permute-done((bf16[256,256]{1,0:T(8,128)(2,1)S(1)}, bf16[256,256]{1,0:T(8,128)(2,1)S(1)}, u32[]{:S(2)}, u32[]{:S(2)}) %collective-permute-start.21) | collective-permute-done | bytes 131104 | tf_op jit(solution)/shard_map/ppermute | solution.py:107
  91.4 2.1 %collective-permute-done.22 = bf16[256,256]{1,0:T(8,128)(2,1)S(1)} collective-permute-done((bf16[256,256]{1,0:T(8,128)(2,1)S(1)}, bf16[256,256]{1,0:T(8,128)(2,1)S(1)}, u32[]{:S(2)}, u32[]{:S(2)}) %collective-permute-start.22) | collective-permute-done | bytes 131104 | tf_op jit(solution)/shard_map/ppermute | solution.py:107
  94.6 0.4 collective-permute-done.24.other
  95.0 0.2 fusion.5
  95.2 0.5 copy-done.24
  95.7 0.3 fusion
  96.0 0.6 collective-permute-start.29
  96.7 3.3 %collective-permute-start.30 = (bf16[4,4096]{1,0:T(4,128)(2,1)S(1)}, bf16[4,4096]{1,0:T(4,128)(2,1)S(1)}, u32[]{:S(2)}, u32[]{:S(2)}) collective-permute-start(bf16[4,4096]{1,0:T(4,128)(2,1)S(1)} %convert_element_type.66), channel_id=1, source_target_pairs={{4,0},{8,4},{12,8},{0,12},{5,1},{9,5},{13,9},{1,13},{6,2},{10,6},{... | collective-permute-start | bytes 98312 | tf_op jit(solution)/shard_map/ppermute | solution.py:311
  99.9 2.6 %last.1 = (bf16[128,1024]{1,0:T(8,128)(2,1)S(1)}, bf16[128,1024]{1,0:T(8,128)(2,1)S(1)}, bf16[128,1024]{1,0:T(8,128)(2,1)S(1)}, bf16[128,1024]{1,0:T(8,128)(2,1)S(1)}) custom-call(s32[3]{0:T(128)S(1)} %pad_add_fusion.flags, bf16[256,1024]{1,0:T(8,128)(2,1)} %copy-done.1, bf16[256,256]{1,0:T(8,128)(2,1)} %copy-done.16, bf16[256,256]{1,0:T(8,128)(2,1)} %copy-done.24, ...), custom_call_target="tpu_custom_call" | custom-call | tf_op jit(solution)/shard_map/last/pallas_call | solution.py:231
  102.5 1.5 %collective-permute-start.25 = (bf16[128,1024]{1,0:T(8,128)(2,1)S(1)}, bf16[128,1024]{1,0:T(8,128)(2,1)S(1)}, u32[]{:S(2)}, u32[]{:S(2)}) collective-permute-start(bf16[128,1024]{1,0:T(8,128)(2,1)S(1)} %get-tuple-element.28), channel_id=1, source_target_pairs={{0,16},{16,0},{1,17},{17,1},{2,18},{18,2},{3,19},{19,3},{4,20},{20... | collective-permute-start | bytes 786440 | tf_op jit(solution)/shard_map/ppermute | solution.py:291
  104.1 0.4 collective-permute-start.26
  104.6 1.7 %collective-permute-start.27 = (bf16[128,1024]{1,0:T(8,128)(2,1)S(1)}, bf16[128,1024]{1,0:T(8,128)(2,1)S(1)}, u32[]{:S(2)}, u32[]{:S(2)}) collective-permute-start(bf16[128,1024]{1,0:T(8,128)(2,1)S(1)} %get-tuple-element.30), channel_id=1, source_target_pairs={{0,18},{18,0},{2,16},{16,2},{1,19},{19,1},{3,17},{17,3},{4,22},{22... | collective-permute-start | bytes 786440 | tf_op jit(solution)/shard_map/ppermute | solution.py:289
  106.4 4.5 %collective-permute-done.25 = bf16[128,1024]{1,0:T(8,128)(2,1)S(1)} collective-permute-done((bf16[128,1024]{1,0:T(8,128)(2,1)S(1)}, bf16[128,1024]{1,0:T(8,128)(2,1)S(1)}, u32[]{:S(2)}, u32[]{:S(2)}) %collective-permute-start.25) | collective-permute-done | bytes 262176 | tf_op jit(solution)/shard_map/ppermute | solution.py:291
  110.9 2.4 %collective-permute-done.26 = bf16[128,1024]{1,0:T(8,128)(2,1)S(1)} collective-permute-done((bf16[128,1024]{1,0:T(8,128)(2,1)S(1)}, bf16[128,1024]{1,0:T(8,128)(2,1)S(1)}, u32[]{:S(2)}, u32[]{:S(2)}) %collective-permute-start.26) | collective-permute-done | bytes 262176 | tf_op jit(solution)/shard_map/ppermute | solution.py:290
  113.5 1.5 %cholesky.16 = f32[16,16]{1,0:T(8,128)S(1)} custom-call(f32[16,16]{1,0:T(8,128)S(1)} %fusion.26), custom_call_target="Cholesky" | custom-call | tf_op jit(solution)/shard_map/jit(cholesky)/cholesky | solution.py:54
  115.0 0.6 compare_reduce_fusion
  115.7 0.6 fusion.24
  116.4 1.2 %custom-call.8 = f32[1,16,16]{1,2,0:T(8,128)S(1)} custom-call(f32[1,16,16]{2,1,0:T(8,128)S(1)} %fusion.24), custom_call_target="InvertDiagBlocksLowerTriangular" | custom-call | tf_op jit(solution)/shard_map/triangular_solve | solution.py:57
  117.6 0.2 fusion.27
  117.8 0.7 fusion.1
  118.6 1.0 copy-done.13
  (101 shorter events, 2.1 us)
Async XLA Ops:
  0.6 81.6 %copy-start = (bf16[1,128,4096]{2,1,0:T(8,128)(2,1)S(1)}, bf16[1,128,4096]{2,1,0:T(8,128)(2,1)}, u32[]{:S(2)}) copy-start(bf16[1,128,4096]{2,1,0:T(8,128)(2,1)} %param.8) | copy-start | bytes 3145732
  1.8 7.8 %copy-start.5 = (bf16[128,1024]{1,0:T(8,128)(2,1)}, bf16[128,1024]{1,0:T(8,128)(2,1)S(1)}, u32[]{:S(2)}) copy-start(bf16[128,1024]{1,0:T(8,128)(2,1)S(1)} %get-tuple-element.35.refs_0_) | copy-start | bytes 786436
  1.8 11.7 %collective-permute-start.5 = (bf16[128,1024]{1,0:T(8,128)(2,1)S(1)}, bf16[128,1024]{1,0:T(8,128)(2,1)S(1)}, u32[]{:S(2)}, u32[]{:S(2)}) collective-permute-start(bf16[128,1024]{1,0:T(8,128)(2,1)S(1)} %get-tuple-element.34), channel_id=1, source_target_pairs={{0,2},{2,0},{1,3},{3,1},{4,6},{6,4},{5,7},{7,5},{8,10},{10,8},{9,1... | collective-permute-start | bytes 786440 | tf_op jit(solution)/shard_map/ppermute | solution.py:257
  4.8 11.1 %collective-permute-start.1 = (bf16[128,1024]{1,0:T(8,128)(2,1)S(1)}, bf16[128,1024]{1,0:T(8,128)(2,1)S(1)}, u32[]{:S(2)}, u32[]{:S(2)}) collective-permute-start(bf16[128,1024]{1,0:T(8,128)(2,1)S(1)} %get-tuple-element.35.refs_0_), channel_id=1, source_target_pairs={{0,4},{4,8},{8,12},{12,0},{1,5},{5,9},{9,13},{13,1},{2,6},{6,10},{... | collective-permute-start | bytes 786440 | tf_op jit(solution)/shard_map/slot1/ppermute | solution.py:96
  6.4 15.5 %collective-permute-start.2 = (bf16[128,1024]{1,0:T(8,128)(2,1)S(1)}, bf16[128,1024]{1,0:T(8,128)(2,1)S(1)}, u32[]{:S(2)}, u32[]{:S(2)}) collective-permute-start(bf16[128,1024]{1,0:T(8,128)(2,1)S(1)} %get-tuple-element.35.refs_0_), channel_id=1, source_target_pairs={{4,0},{8,4},{12,8},{0,12},{5,1},{9,5},{13,9},{1,13},{6,2},{10,6},{... | collective-permute-start | bytes 786440 | tf_op jit(solution)/shard_map/slot1/ppermute | solution.py:96
  9.6 11.0 %collective-permute-start.11 = (bf16[128,1024]{1,0:T(8,128)(2,1)S(1)}, bf16[128,1024]{1,0:T(8,128)(2,1)S(1)}, u32[]{:S(2)}, u32[]{:S(2)}) collective-permute-start(bf16[128,1024]{1,0:T(8,128)(2,1)S(1)} %dynamic-slice_bitcast_fusion), channel_id=1, source_target_pairs={{0,2},{2,0},{1,3},{3,1},{4,6},{6,4},{5,7},{7,5},{8,10},{10,8},{9,1... | collective-permute-start | bytes 786440 | tf_op jit(solution)/shard_map/ppermute | solution.py:258
  11.8 22.8 %collective-permute-start = (bf16[128,1024]{1,0:T(8,128)(2,1)S(1)}, bf16[128,1024]{1,0:T(8,128)(2,1)}, u32[]{:S(2)}, u32[]{:S(2)}) collective-permute-start(bf16[128,1024]{1,0:T(8,128)(2,1)S(1)} %get-tuple-element.36), channel_id=1, source_target_pairs={{0,16},{16,0},{1,17},{17,1},{2,18},{18,2},{3,19},{19,3},{4,20},{20... | collective-permute-start | bytes 786440 | tf_op jit(solution)/shard_map/ppermute | solution.py:260
  14.5 7.4 %copy-start.6 = (bf16[128,1024]{1,0:T(8,128)(2,1)}, bf16[128,1024]{1,0:T(8,128)(2,1)S(1)}, u32[]{:S(2)}) copy-start(bf16[128,1024]{1,0:T(8,128)(2,1)S(1)} %get-tuple-element.32.refs_5_) | copy-start | bytes 786436
  14.5 12.6 %collective-permute-start.6 = (bf16[128,1024]{1,0:T(8,128)(2,1)S(1)}, bf16[128,1024]{1,0:T(8,128)(2,1)S(1)}, u32[]{:S(2)}, u32[]{:S(2)}) collective-permute-start(bf16[128,1024]{1,0:T(8,128)(2,1)S(1)} %get-tuple-element.32.refs_5_), channel_id=1, source_target_pairs={{0,4},{4,8},{8,12},{12,0},{1,5},{5,9},{9,13},{13,1},{2,6},{6,10},{... | collective-permute-start | bytes 786440 | tf_op jit(solution)/shard_map/slot2/ppermute | solution.py:96
  15.9 6.0 %copy-start.7 = (bf16[128,1024]{1,0:T(8,128)(2,1)}, bf16[128,1024]{1,0:T(8,128)(2,1)S(1)}, u32[]{:S(2)}) copy-start(bf16[128,1024]{1,0:T(8,128)(2,1)S(1)} %collective-permute-done.1.refs_1_) | copy-start | bytes 786436
  15.9 17.0 %collective-permute-start.7 = (bf16[128,1024]{1,0:T(8,128)(2,1)S(1)}, bf16[128,1024]{1,0:T(8,128)(2,1)S(1)}, u32[]{:S(2)}, u32[]{:S(2)}) collective-permute-start(bf16[128,1024]{1,0:T(8,128)(2,1)S(1)} %get-tuple-element.32.refs_5_), channel_id=1, source_target_pairs={{4,0},{8,4},{12,8},{0,12},{5,1},{9,5},{13,9},{1,13},{6,2},{10,6},{... | collective-permute-start | bytes 786440 | tf_op jit(solution)/shard_map/slot2/ppermute | solution.py:96
  20.6 15.0 %collective-permute-start.3 = (bf16[64,1024]{1,0:T(8,128)(2,1)S(1)}, bf16[64,1024]{1,0:T(8,128)(2,1)S(1)}, u32[]{:S(2)}, u32[]{:S(2)}) collective-permute-start(bf16[64,1024]{1,0:T(8,128)(2,1)S(1)} %slice.56), channel_id=1, source_target_pairs={{0,4},{4,8},{8,12},{12,0},{1,5},{5,9},{9,13},{13,1},{2,6},{6,10},{... | collective-permute-start | bytes 393224 | tf_op jit(solution)/shard_map/slot1/ppermute | solution.py:97
  21.9 2.8 %copy-start.8 = (bf16[128,1024]{1,0:T(8,128)(2,1)}, bf16[128,1024]{1,0:T(8,128)(2,1)S(1)}, u32[]{:S(2)}) copy-start(bf16[128,1024]{1,0:T(8,128)(2,1)S(1)} %collective-permute-done.2.refs_2_) | copy-start | bytes 786436
  21.9 16.7 %collective-permute-start.4 = (bf16[64,1024]{1,0:T(8,128)(2,1)S(1)}, bf16[64,1024]{1,0:T(8,128)(2,1)S(1)}, u32[]{:S(2)}, u32[]{:S(2)}) collective-permute-start(bf16[64,1024]{1,0:T(8,128)(2,1)S(1)} %slice.57), channel_id=1, source_target_pairs={{4,0},{8,4},{12,8},{0,12},{5,1},{9,5},{13,9},{1,13},{6,2},{10,6},{... | collective-permute-start | bytes 393224 | tf_op jit(solution)/shard_map/slot1/ppermute | solution.py:97
  27.2 7.3 %copy-start.9 = (bf16[128,1024]{1,0:T(8,128)(2,1)}, bf16[128,1024]{1,0:T(8,128)(2,1)S(1)}, u32[]{:S(2)}) copy-start(bf16[128,1024]{1,0:T(8,128)(2,1)S(1)} %collective-permute-done.6.refs_6_) | copy-start | bytes 786436
  27.2 14.0 %collective-permute-start.8 = (bf16[64,1024]{1,0:T(8,128)(2,1)S(1)}, bf16[64,1024]{1,0:T(8,128)(2,1)S(1)}, u32[]{:S(2)}, u32[]{:S(2)}) collective-permute-start(bf16[64,1024]{1,0:T(8,128)(2,1)S(1)} %slice.58), channel_id=1, source_target_pairs={{0,4},{4,8},{8,12},{12,0},{1,5},{5,9},{9,13},{13,1},{2,6},{6,10},{... | collective-permute-start | bytes 393224 | tf_op jit(solution)/shard_map/slot2/ppermute | solution.py:97
  32.9 1.6 %copy-start.10 = (bf16[128,1024]{1,0:T(8,128)(2,1)}, bf16[128,1024]{1,0:T(8,128)(2,1)S(1)}, u32[]{:S(2)}) copy-start(bf16[128,1024]{1,0:T(8,128)(2,1)S(1)} %collective-permute-done.7.refs_7_) | copy-start | bytes 786436
  32.9 9.8 %collective-permute-start.9 = (bf16[64,1024]{1,0:T(8,128)(2,1)S(1)}, bf16[64,1024]{1,0:T(8,128)(2,1)S(1)}, u32[]{:S(2)}, u32[]{:S(2)}) collective-permute-start(bf16[64,1024]{1,0:T(8,128)(2,1)S(1)} %slice.59), channel_id=1, source_target_pairs={{4,0},{8,4},{12,8},{0,12},{5,1},{9,5},{13,9},{1,13},{6,2},{10,6},{... | collective-permute-start | bytes 393224 | tf_op jit(solution)/shard_map/slot2/ppermute | solution.py:97
  34.5 11.4 %copy-start.2 = (bf16[256,1024]{1,0:T(8,128)(2,1)}, bf16[256,1024]{1,0:T(8,128)(2,1)S(1)}, u32[]{:S(2)}) copy-start(bf16[256,1024]{1,0:T(8,128)(2,1)S(1)} %pad_maximum_fusion.refs_10_.refs_0_) | copy-start | bytes 1572868
  34.5 20.7 %collective-permute-start.12 = (bf16[256,1024]{1,0:T(8,128)(2,1)S(1)}, bf16[256,1024]{1,0:T(8,128)(2,1)S(1)}, u32[]{:S(2)}, u32[]{:S(2)}) collective-permute-start(bf16[256,1024]{1,0:T(8,128)(2,1)S(1)} %pad_maximum_fusion.refs_10_.refs_0_), channel_id=1, source_target_pairs={{0,4},{4,8},{8,12},{12,0},{1,5},{5,9},{9,13},{13,1},{2,6},{6,10},{... | collective-permute-start | bytes 1572872 | tf_op jit(solution)/shard_map/slot34/ppermute | solution.py:96
  35.6 7.1 %copy-start.18 = (bf16[64,1024]{1,0:T(8,128)(2,1)}, bf16[64,1024]{1,0:T(8,128)(2,1)S(1)}, u32[]{:S(2)}) copy-start(bf16[64,1024]{1,0:T(8,128)(2,1)S(1)} %collective-permute-done.3.refs_3_) | copy-start | bytes 393220
  38.6 4.1 %copy-start.19 = (bf16[64,1024]{1,0:T(8,128)(2,1)}, bf16[64,1024]{1,0:T(8,128)(2,1)S(1)}, u32[]{:S(2)}) copy-start(bf16[64,1024]{1,0:T(8,128)(2,1)S(1)} %collective-permute-done.4.refs_4_) | copy-start | bytes 393220
  41.2 1.5 %copy-start.20 = (bf16[64,1024]{1,0:T(8,128)(2,1)}, bf16[64,1024]{1,0:T(8,128)(2,1)S(1)}, u32[]{:S(2)}) copy-start(bf16[64,1024]{1,0:T(8,128)(2,1)S(1)} %collective-permute-done.8.refs_8_) | copy-start | bytes 393220
  42.7 0.6 copy-start.21
  45.9 3.0 %collective-permute-start.10 = (f32[256,256]{1,0:T(8,128)S(1)}, f32[256,256]{1,0:T(8,128)S(1)}, u32[]{:S(2)}, u32[]{:S(2)}) collective-permute-start(f32[256,256]{1,0:T(8,128)S(1)} %get-tuple-element.18), channel_id=1, source_target_pairs={{0,1},{1,0},{2,3},{3,2},{4,5},{5,4},{6,7},{7,6},{8,9},{9,8},{10,11... | collective-permute-start | bytes 786440 | tf_op jit(solution)/shard_map/ppermute | solution.py:106
  45.9 20.6 %collective-permute-start.17 = (bf16[256,1024]{1,0:T(8,128)(2,1)S(1)}, bf16[256,1024]{1,0:T(8,128)(2,1)S(1)}, u32[]{:S(2)}, u32[]{:S(2)}) collective-permute-start(bf16[256,1024]{1,0:T(8,128)(2,1)S(1)} %pad_maximum_fusion.refs_10_.refs_0_), channel_id=1, source_target_pairs={{4,0},{8,4},{12,8},{0,12},{5,1},{9,5},{13,9},{1,13},{6,2},{10,6},{... | collective-permute-start | bytes 1572872 | tf_op jit(solution)/shard_map/slot34/ppermute | solution.py:96
  55.3 11.3 %copy-start.3 = (bf16[256,1024]{1,0:T(8,128)(2,1)}, bf16[256,1024]{1,0:T(8,128)(2,1)S(1)}, u32[]{:S(2)}) copy-start(bf16[256,1024]{1,0:T(8,128)(2,1)S(1)} %collective-permute-done.12.refs_11_.refs_1_) | copy-start | bytes 1572868
  55.3 13.0 %collective-permute-start.13 = (bf16[256,256]{1,0:T(8,128)(2,1)S(1)}, bf16[256,256]{1,0:T(8,128)(2,1)S(1)}, u32[]{:S(2)}, u32[]{:S(2)}) collective-permute-start(bf16[256,256]{1,0:T(8,128)(2,1)S(1)} %add_convert_fusion.3), channel_id=1, source_target_pairs={{0,18},{18,0},{2,16},{16,2},{1,19},{19,1},{3,17},{17,3},{4,22},{22... | collective-permute-start | bytes 393224 | tf_op jit(solution)/shard_map/ppermute | solution.py:107
  56.8 11.5 %collective-permute-start.14 = (bf16[256,256]{1,0:T(8,128)(2,1)S(1)}, bf16[256,256]{1,0:T(8,128)(2,1)S(1)}, u32[]{:S(2)}, u32[]{:S(2)}) collective-permute-start(bf16[256,256]{1,0:T(8,128)(2,1)S(1)} %add_convert_fusion.3), channel_id=1, source_target_pairs={{0,2},{2,0},{1,3},{3,1},{4,6},{6,4},{5,7},{7,5},{8,10},{10,8},{9,1... | collective-permute-start | bytes 393224 | tf_op jit(solution)/shard_map/ppermute | solution.py:107
  58.3 10.0 %collective-permute-start.15 = (bf16[256,256]{1,0:T(8,128)(2,1)S(1)}, bf16[256,256]{1,0:T(8,128)(2,1)S(1)}, u32[]{:S(2)}, u32[]{:S(2)}) collective-permute-start(bf16[256,256]{1,0:T(8,128)(2,1)S(1)} %add_convert_fusion.3), channel_id=1, source_target_pairs={{0,16},{16,0},{1,17},{17,1},{2,18},{18,2},{3,19},{19,3},{4,20},{20... | collective-permute-start | bytes 393224 | tf_op jit(solution)/shard_map/ppermute | solution.py:107
  58.8 14.4 %collective-permute-start.16 = (bf16[128,1024]{1,0:T(8,128)(2,1)S(1)}, bf16[128,1024]{1,0:T(8,128)(2,1)S(1)}, u32[]{:S(2)}, u32[]{:S(2)}) collective-permute-start(bf16[128,1024]{1,0:T(8,128)(2,1)S(1)} %slice.64), channel_id=1, source_target_pairs={{0,4},{4,8},{8,12},{12,0},{1,5},{5,9},{9,13},{13,1},{2,6},{6,10},{... | collective-permute-start | bytes 786440 | tf_op jit(solution)/shard_map/slot34/ppermute | solution.py:97
  66.5 1.8 %copy-start.4 = (bf16[256,1024]{1,0:T(8,128)(2,1)}, bf16[256,1024]{1,0:T(8,128)(2,1)S(1)}, u32[]{:S(2)}) copy-start(bf16[256,1024]{1,0:T(8,128)(2,1)S(1)} %collective-permute-done.17.refs_12_.refs_2_) | copy-start | bytes 1572868
  66.5 10.3 %collective-permute-start.18 = (bf16[128,1024]{1,0:T(8,128)(2,1)S(1)}, bf16[128,1024]{1,0:T(8,128)(2,1)S(1)}, u32[]{:S(2)}, u32[]{:S(2)}) collective-permute-start(bf16[128,1024]{1,0:T(8,128)(2,1)S(1)} %slice.65), channel_id=1, source_target_pairs={{4,0},{8,4},{12,8},{0,12},{5,1},{9,5},{13,9},{1,13},{6,2},{10,6},{... | collective-permute-start | bytes 786440 | tf_op jit(solution)/shard_map/slot34/ppermute | solution.py:97
  68.3 9.8 %copy-start.14 = (bf16[256,256]{1,0:T(8,128)(2,1)}, bf16[256,256]{1,0:T(8,128)(2,1)S(1)}, u32[]{:S(2)}) copy-start(bf16[256,256]{1,0:T(8,128)(2,1)S(1)} %add_convert_fusion.2.mine) | copy-start | bytes 393220
  68.4 13.9 %copy-start.17 = (bf16[1,64,4096]{2,1,0:T(8,128)(2,1)S(1)}, bf16[1,64,4096]{2,1,0:T(8,128)(2,1)}, u32[]{:S(2)}) copy-start(bf16[1,64,4096]{2,1,0:T(8,128)(2,1)} %param.12) | copy-start | bytes 1572868
  73.2 5.0 %copy-start.11 = (bf16[128,1024]{1,0:T(8,128)(2,1)}, bf16[128,1024]{1,0:T(8,128)(2,1)S(1)}, u32[]{:S(2)}) copy-start(bf16[128,1024]{1,0:T(8,128)(2,1)S(1)} %collective-permute-done.16.refs_13_.refs_3_) | copy-start | bytes 786436
  76.8 1.4 %copy-start.12 = (bf16[128,1024]{1,0:T(8,128)(2,1)}, bf16[128,1024]{1,0:T(8,128)(2,1)S(1)}, u32[]{:S(2)}) copy-start(bf16[128,1024]{1,0:T(8,128)(2,1)S(1)} %collective-permute-done.18.refs_14_.refs_4_) | copy-start | bytes 786436
  76.8 1.3 %collective-permute-start.19 = (bf16[256,256]{1,0:T(8,128)(2,1)S(1)}, bf16[256,256]{1,0:T(8,128)(2,1)S(1)}, u32[]{:S(2)}, u32[]{:S(2)}) collective-permute-start(bf16[256,256]{1,0:T(8,128)(2,1)S(1)} %add_convert_fusion.2.mine), channel_id=1, source_target_pairs={{0,1},{1,0},{2,3},{3,2},{4,5},{5,4},{6,7},{7,6},{8,9},{9,8},{10,11... | collective-permute-start | bytes 393224 | tf_op jit(solution)/shard_map/ppermute | solution.py:112
  78.2 0.7 copy-start.22
  82.0 0.8 copy-start.1
  82.1 2.0 %collective-permute-start.20 = (f32[256,256]{1,0:T(8,128)S(1)}, f32[256,256]{1,0:T(8,128)S(1)}, u32[]{:S(2)}, u32[]{:S(2)}) collective-permute-start(f32[256,256]{1,0:T(8,128)S(1)} %get-tuple-element.26), channel_id=1, source_target_pairs={{0,1},{1,0},{2,3},{3,2},{4,5},{5,4},{6,7},{7,6},{8,9},{9,8},{10,11... | collective-permute-start | bytes 786440 | tf_op jit(solution)/shard_map/ppermute | solution.py:106
  82.9 12.8 %collective-permute-start.28 = (f32[128,64]{0,1:T(8,128)S(1)}, f32[128,64]{0,1:T(8,128)S(1)}, u32[]{:S(2)}, u32[]{:S(2)}) collective-permute-start(f32[128,64]{0,1:T(8,128)S(1)} %fusion.2), channel_id=1, source_target_pairs={{0,1},{1,0},{2,3},{3,2},{4,5},{5,4},{6,7},{7,6},{8,9},{9,8},{10,11... | collective-permute-start | bytes 98312 | tf_op jit(solution)/shard_map/ppermute | solution.py:309
  83.2 0.7 copy-start.26
  84.1 7.3 %collective-permute-start.21 = (bf16[256,256]{1,0:T(8,128)(2,1)S(1)}, bf16[256,256]{1,0:T(8,128)(2,1)S(1)}, u32[]{:S(2)}, u32[]{:S(2)}) collective-permute-start(bf16[256,256]{1,0:T(8,128)(2,1)S(1)} %add_convert_fusion.1), channel_id=1, source_target_pairs={{0,18},{18,0},{2,16},{16,2},{1,19},{19,1},{3,17},{17,3},{4,22},{22... | collective-permute-start | bytes 393224 | tf_op jit(solution)/shard_map/ppermute | solution.py:107
  85.5 8.0 %collective-permute-start.22 = (bf16[256,256]{1,0:T(8,128)(2,1)S(1)}, bf16[256,256]{1,0:T(8,128)(2,1)S(1)}, u32[]{:S(2)}, u32[]{:S(2)}) collective-permute-start(bf16[256,256]{1,0:T(8,128)(2,1)S(1)} %add_convert_fusion.1), channel_id=1, source_target_pairs={{0,2},{2,0},{1,3},{3,1},{4,6},{6,4},{5,7},{7,5},{8,10},{10,8},{9,1... | collective-permute-start | bytes 393224 | tf_op jit(solution)/shard_map/ppermute | solution.py:107
  87.1 6.4 %collective-permute-start.23 = (bf16[256,256]{1,0:T(8,128)(2,1)S(1)}, bf16[256,256]{1,0:T(8,128)(2,1)S(1)}, u32[]{:S(2)}, u32[]{:S(2)}) collective-permute-start(bf16[256,256]{1,0:T(8,128)(2,1)S(1)} %add_convert_fusion.1), channel_id=1, source_target_pairs={{0,16},{16,0},{1,17},{17,1},{2,18},{18,2},{3,19},{19,3},{4,20},{20... | collective-permute-start | bytes 393224 | tf_op jit(solution)/shard_map/ppermute | solution.py:107
  87.6 6.0 %copy-start.25 = (bf16[1,64,512]{2,1,0:T(8,128)(2,1)S(1)}, bf16[1,64,512]{2,1,0:T(8,128)(2,1)}, u32[]{:S(2)}) copy-start(bf16[1,64,512]{2,1,0:T(8,128)(2,1)} %param.13) | copy-start | bytes 196612
  93.6 1.0 copy-start.16
  93.6 1.0 copy-start.15
  93.6 1.4 %collective-permute-start.24 = (bf16[256,256]{1,0:T(8,128)(2,1)S(1)}, bf16[256,256]{1,0:T(8,128)(2,1)S(1)}, u32[]{:S(2)}, u32[]{:S(2)}) collective-permute-start(bf16[256,256]{1,0:T(8,128)(2,1)S(1)} %add_convert_fusion.mine), channel_id=1, source_target_pairs={{0,1},{1,0},{2,3},{3,2},{4,5},{5,4},{6,7},{7,6},{8,9},{9,8},{10,11... | collective-permute-start | bytes 393224 | tf_op jit(solution)/shard_map/ppermute | solution.py:112
  93.7 1.3 %copy-start.23 = (bf16[256,256]{1,0:T(8,128)(2,1)S(1)}, bf16[256,256]{1,0:T(8,128)(2,1)}, u32[]{:S(2)}) copy-start(bf16[256,256]{1,0:T(8,128)(2,1)} %copy-done.22) | copy-start | bytes 393220
  95.0 0.7 copy-start.24
  96.0 8.6 %collective-permute-start.29 = (bf16[4,4096]{1,0:T(4,128)(2,1)S(1)}, bf16[4,4096]{1,0:T(4,128)(2,1)S(1)}, u32[]{:S(2)}, u32[]{:S(2)}) collective-permute-start(bf16[4,4096]{1,0:T(4,128)(2,1)S(1)} %convert_element_type.66), channel_id=1, source_target_pairs={{0,4},{4,8},{8,12},{12,0},{1,5},{5,9},{9,13},{13,1},{2,6},{6,10},{... | collective-permute-start | bytes 98312 | tf_op jit(solution)/shard_map/ppermute | solution.py:311
  96.7 9.7 %collective-permute-start.30 = (bf16[4,4096]{1,0:T(4,128)(2,1)S(1)}, bf16[4,4096]{1,0:T(4,128)(2,1)S(1)}, u32[]{:S(2)}, u32[]{:S(2)}) collective-permute-start(bf16[4,4096]{1,0:T(4,128)(2,1)S(1)} %convert_element_type.66), channel_id=1, source_target_pairs={{4,0},{8,4},{12,8},{0,12},{5,1},{9,5},{13,9},{1,13},{6,2},{10,6},{... | collective-permute-start | bytes 98312 | tf_op jit(solution)/shard_map/ppermute | solution.py:311
  99.9 6.4 %collective-permute-start.31 = (bf16[4,4096]{1,0:T(4,128)(2,1)S(1)}, bf16[4,4096]{1,0:T(4,128)(2,1)S(1)}, u32[]{:S(2)}, u32[]{:S(2)}) collective-permute-start(bf16[4,4096]{1,0:T(4,128)(2,1)S(1)} %convert_element_type.66), channel_id=1, source_target_pairs={{0,8},{8,0},{4,12},{12,4},{1,9},{9,1},{5,13},{13,5},{2,10},{10,2},... | collective-permute-start | bytes 98312 | tf_op jit(solution)/shard_map/ppermute | solution.py:311
  102.5 8.4 %collective-permute-start.25 = (bf16[128,1024]{1,0:T(8,128)(2,1)S(1)}, bf16[128,1024]{1,0:T(8,128)(2,1)S(1)}, u32[]{:S(2)}, u32[]{:S(2)}) collective-permute-start(bf16[128,1024]{1,0:T(8,128)(2,1)S(1)} %get-tuple-element.28), channel_id=1, source_target_pairs={{0,16},{16,0},{1,17},{17,1},{2,18},{18,2},{3,19},{19,3},{4,20},{20... | collective-permute-start | bytes 786440 | tf_op jit(solution)/shard_map/ppermute | solution.py:291
  104.1 9.2 %collective-permute-start.26 = (bf16[128,1024]{1,0:T(8,128)(2,1)S(1)}, bf16[128,1024]{1,0:T(8,128)(2,1)S(1)}, u32[]{:S(2)}, u32[]{:S(2)}) collective-permute-start(bf16[128,1024]{1,0:T(8,128)(2,1)S(1)} %get-tuple-element.29), channel_id=1, source_target_pairs={{0,2},{2,0},{1,3},{3,1},{4,6},{6,4},{5,7},{7,5},{8,10},{10,8},{9,1... | collective-permute-start | bytes 786440 | tf_op jit(solution)/shard_map/ppermute | solution.py:290
  104.6 14.0 %collective-permute-start.27 = (bf16[128,1024]{1,0:T(8,128)(2,1)S(1)}, bf16[128,1024]{1,0:T(8,128)(2,1)S(1)}, u32[]{:S(2)}, u32[]{:S(2)}) collective-permute-start(bf16[128,1024]{1,0:T(8,128)(2,1)S(1)} %get-tuple-element.30), channel_id=1, source_target_pairs={{0,18},{18,0},{2,16},{16,2},{1,19},{19,1},{3,17},{17,3},{4,22},{22... | collective-permute-start | bytes 786440 | tf_op jit(solution)/shard_map/ppermute | solution.py:289
  118.6 1.0 copy-start.13

commit v3 on v2

--- a/solution.py
+++ b/solution.py
@@ -146,7 +146,7 @@
     n, starts = dst.shape[0] // 8, []
     for ref in slot[:3]:
         starts += [(ref, which * n), (ref, ref.shape[0] // 2 + which * n)]
-    starts += [(ref, which * n) for ref in slot[3:]]
+    starts += [(ref, 0) for ref in slot[3:]]
     return [(ref.at[pl.ds(at, n)], dst.at[pl.ds(k * n, n)]) for k, (ref, at) in enumerate(starts)]
 
 
@@ -226,8 +226,42 @@
     copies.wait()
 
 
+def score_kernel(shift, *refs):
+    rows, (out, stacked) = refs[:-2], refs[-2:]
+    n = rows[0].shape[0]
+    for k, ref in enumerate(rows):
+        stacked[k * n : (k + 1) * n, :] = ref[...].astype(F32)
+    every = stacked[...].astype(BF16)
+    kernel = dot_t(every, every)
+    order = kernel.shape[0]
+    row = lax.broadcasted_iota(jnp.int32, (order, order), 0)
+    column = lax.broadcasted_iota(jnp.int32, (order, order), 1)
+    left = kernel + jnp.where(row == column, shift[0], 0.0)
+    right = kernel
+    for k in range(order):
+        inverse = 1.0 / left[k : k + 1, k : k + 1]
+        left_row, right_row = left[k : k + 1, :] * inverse, right[k : k + 1, :] * inverse
+        factor = left[:, k : k + 1]
+        left = jnp.where(row == k, left_row, left - factor * left_row)
+        right = jnp.where(row == k, right_row, right - factor * right_row)
+    out[...] = jnp.sum(jnp.where(row == column, right, 0.0), axis=0, keepdims=True)
+
+
+def scores_by_kernel(blocks, shift):
+    order = len(blocks) * blocks[0].shape[0]
+    return pl.pallas_call(
+        score_kernel,
+        name="scores",
+        out_shape=jax.ShapeDtypeStruct((1, order), F32),
+        in_specs=[pl.BlockSpec(memory_space=pltpu.SMEM)] + [pl.BlockSpec(memory_space=pltpu.VMEM)] * len(blocks),
+        out_specs=pl.BlockSpec(memory_space=pltpu.VMEM),
+        scratch_shapes=[pltpu.VMEM((order, blocks[0].shape[1]), F32)],
+        compiler_params=pltpu.CompilerParams(vmem_limit_bytes=8 << 20),
+    )(shift, *blocks)
+
+
 def kernel_call(body, name, outs, scratch, copies, flags, *args):
-    anywhere = pl.BlockSpec(memory_space=pltpu.HBM)
+    anywhere = pl.BlockSpec(memory_space=pl.ANY)
     return pl.pallas_call(
         body,
         name=name,
@@ -236,7 +270,7 @@
         out_specs=[anywhere if far else pl.BlockSpec(memory_space=pltpu.VMEM) for _, far in outs],
         scratch_shapes=[pltpu.VMEM(*shape) for shape in scratch] + [pltpu.SemaphoreType.DMA((copies,))],
         compiler_params=pltpu.CompilerParams(vmem_limit_bytes=16 << 20),
-    )(flags, *[pltpu.with_memory_space_constraint(a, pltpu.HBM) for a in args])
+    )(flags, *[pltpu.with_memory_space_constraint(a, pltpu.HBM) if a.shape[1] > 512 else a for a in args])
 
 
 def spread(acts, cotangent, in_weight, out_weight, in_factor, out_factor, damping, lengths):
@@ -259,10 +293,18 @@
     g_own = piece(cotangent, x, y)
     g_other = lax.ppermute(piece(cotangent, x, 1 - y), "group", PAIR)
     slot2 = gathered(jnp.where(last, u_keep, v_other), "slot2")
-    u_keep, v_other, u_other = after2((u_keep, v_other, u_other), slot1[1])
+    u_keep, v_other, u_other = after2((u_keep, v_other, u_other), *slot2[1:3])
     h = n // 2
     third, fourth = jnp.where(last, v_other, u_other), jnp.where(last, u_other, u_keep)
-    rest = gathered(jnp.concatenate([third[:h], fourth[:h], third[h:], fourth[h:]], 0), "slot34")
+    both = jnp.concatenate([third[:h], fourth[:h], third[h:], fourth[h:]], 0)
+    with jax.named_scope("slot34"):
+        below, above = lax.ppermute(both, "dp", UP), lax.ppermute(both, "dp", DOWN)
+    with jax.named_scope("slot3"):
+        far3 = [lax.ppermute(below[:h], "dp", UP), lax.ppermute(above[n : n + h], "dp", DOWN)]
+    with jax.named_scope("slot4"):
+        ready = after2((below[h:n], above[n + h :]), *far3[:1])
+        far4 = [lax.ppermute(ready[0], "dp", UP), lax.ppermute(ready[1], "dp", DOWN)]
+    slot3, slot4 = [both, below, above, *far3], [both, below, above, *far4]
 
     flags = jnp.stack([x, y, lax.axis_index("mp")]).astype(jnp.int32)
     groups = lax.axis_size("group")
@@ -277,14 +319,14 @@
     keep, send = kernel_call(
         first_kernel, "first", [(half_part, False)] * 2, [wide, weight, part_of], 10, flags, g_own, g_other, *slot1, *slot2
     )
-    mine1, other1 = summed(keep, send, rest[1:2], rest[3:])
+    mine1, other1 = summed(keep, send, slot3[1:2], slot3[3:])
     adjoint1, keep, send = kernel_call(
         middle_kernel, "middle", [(shape_of, False), (half_part, False), (half_part, False)],
-        [wide, rank_of, weight, weight, part_of], 20, flags, g_own, g_other, mine1, other1, *slot1, *slot2, *rest,
-    )
-    mine0, other0 = summed(keep, send, (), ())
+        [wide, rank_of, weight, weight, part_of], 20, flags, g_own, g_other, mine1, other1, *slot1, *slot2, *slot3,
+    )
+    mine0, other0 = summed(keep, send, (), slot4[3:])
     here, to_x, to_xy, to_y = kernel_call(
-        last_kernel, "last", [(send_of, True)] * 4, [wide, rank_of, weight, wide], 15, flags, adjoint1, mine0, other0, *rest
+        last_kernel, "last", [(send_of, True)] * 4, [wide, rank_of, weight, wide], 15, flags, adjoint1, mine0, other0, *slot4
     )
     from_xy = lax.ppermute(to_xy, *plane("both"))
     from_x = lax.ppermute(to_x, *plane("section"))
@@ -308,10 +350,11 @@
     in_part = dot_t(acts[0], in_factor[0])
     in_proj = in_part + lax.ppermute(in_part, "mp", PAIR)
     rows = own_rows(out_proj, in_proj, lengths[0])
-    every_row = jnp.concatenate([rows] + [lax.ppermute(rows, "dp", p) for p in (UP, DOWN, OPPOSITE)], 0)
-    every_row = after(every_row, from_x, from_y)
-    scores = scores_of(every_row, damping[0], 0, examples, tok_rows)
-    return (adjoint[None], scores[None])
+    rows = after(rows, from_x)
+    blocks = [rows] + [lax.ppermute(rows, "dp", p) for p in (UP, DOWN, OPPOSITE)]
+    columns = rows.shape[1]
+    scores = scores_by_kernel(blocks, damping * (columns * tok_rows / examples))[:, :examples]
+    return (adjoint[None], scores)
 
 
 def solution(mesh):

time: 120 us -> 116 us (0.967)
  starting transfers between devices: 39.2 us -> 43.9 us
  waiting for transfers between devices: 54.5 us -> 50.2 us
  other arithmetic: 5.74 us -> 1.61 us
  Pallas kernels: 8.28 us -> 10.2 us
  local copies, waits for them, and re-layouts: 8.09 us -> 6.61 us
    ppermute x0 -> x6, waiting for transfers between devices: none -> 21.5 us  [the longest x1 7.66 us: spread(): lax.ppermute(both, 'dp', DOWN)]
    ppermute x6 -> x4, waiting for transfers between devices: 24 us -> 8.48 us  [gathered(): below, above = (lax.ppermute(w, 'dp', UP), lax.ppermute(w, 'dp', DOWN))]
    ppermute x0 -> x6, starting transfers between devices: none -> 6.95 us  [the longest x1 2.55 us: spread(): lax.ppermute(ready[1], 'dp', DOWN)]
    ppermute x3 -> x2, waiting for transfers between devices: 7.87 us -> 2.64 us  [gathered(): lax.ppermute(below[:half], 'dp', UP)]
    ppermute x3 -> x2, waiting for transfers between devices: 8.1 us -> 2.88 us  [gathered(): lax.ppermute(above[half:], 'dp', DOWN)]
    ppermute x1, waiting for transfers between devices: 4.55 us -> 0.01 us  [spread(): from_y = lax.ppermute(to_y, *plane('group'))]
    another operation x6 -> x1, other arithmetic: 4.04 us -> 0.01 us  [the longest x3 2.16 us: scores_of(): jnp.linalg.cholesky(kernel + shift_value * jnp.eye(kernel.shape[0], dtype...]
    ppermute x6 -> x4, starting transfers between devices: 12.7 us -> 8.78 us  [gathered(): below, above = (lax.ppermute(w, 'dp', UP), lax.ppermute(w, 'dp', DOWN))]
  transfers between devices with their start and end apart: 32 -> 34, of which waited for: 18 -> 19; matrix products, arithmetic and copies ran while one was open for 9% -> 6% of each run, Pallas kernels for 4% -> 4%
where the time goes in v3:
time: 116 us; the launch traced here: 115 us
  waiting for transfers between devices  50.2 us (43%)
  starting transfers between devices  43.9 us (38%)
  Pallas kernels  10.2 us (9%)
  local copies, waits for them, and re-layouts  6.61 us (6%)
  between operations  1.74 us (2%)
  other arithmetic  1.61 us (1%)
    ppermute x4, starting transfers between devices, gathered(): below, above = (lax.ppermute(w, 'dp', UP), lax.ppermute(w, 'dp', DOWN))  8.78 us
    ppermute x4, waiting for transfers between devices, gathered(): below, above = (lax.ppermute(w, 'dp', UP), lax.ppermute(w, 'dp', DOWN))  8.48 us
    pallas_call x3, Pallas kernels, kernel_call(): pl.pallas_call(body, name=name, out_shape=[o for o, _ in outs], in_specs=...  8.14 us
    ppermute x1, waiting for transfers between devices, spread(): lax.ppermute(both, 'dp', DOWN)  7.66 us
    ppermute x6, starting transfers between devices, summed(): lax.ppermute(own, *plane(a))  7.04 us
    ppermute x2, starting transfers between devices, gathered(): lax.ppermute(above[half:], 'dp', DOWN)  6.91 us
    ppermute x1, waiting for transfers between devices, spread(): lax.ppermute(both, 'dp', UP)  6.8 us
    ppermute x1, waiting for transfers between devices, spread(): from_x = lax.ppermute(to_x, *plane('section'))  4.86 us
  transfers between devices with their start and end apart: 34, of which 19 were waited for; matrix products, arithmetic and copies ran while one was open for 6% of the time, Pallas kernels for 4%

profile of v3, /device:TPU:0, one launch (start us, length us, event | category | flops | bytes accessed | tf_op | source)
XLA Modules:
  0.0 115.2 jit_solution(6222058130856013245)
XLA Ops:
  0.7 1.2 %dynamic-slice_bitcast_fusion.1 = (bf16[128,1024]{1,0:T(8,128)(2,1)S(1)}, bf16[128,1024]{1,0:T(8,128)(2,1)S(1)}) fusion(bf16[1,128,4096]{2,1,0:T(8,128)(2,1)} %param.11, s32[]{:T(128)S(6)} %select_n.77, s32[]{:T(128)S(6)} %select_n.74), kind=kLoop, calls=%fused_computation.15 | loop fusion | bytes 1048584 | tf_op jit(solution)/shard_map/dynamic_slice | solution.py:283
  1.8 3.0 %collective-permute-start.5 = (bf16[128,1024]{1,0:T(8,128)(2,1)S(1)}, bf16[128,1024]{1,0:T(8,128)(2,1)S(1)}, u32[]{:S(2)}, u32[]{:S(2)}) collective-permute-start(bf16[128,1024]{1,0:T(8,128)(2,1)S(1)} %get-tuple-element.40), channel_id=1, source_target_pairs={{0,2},{2,0},{1,3},{3,1},{4,6},{6,4},{5,7},{7,5},{8,10},{10,8},{9,1... | collective-permute-start | bytes 786440 | tf_op jit(solution)/shard_map/ppermute | solution.py:291
  4.8 1.6 %collective-permute-start.1 = (bf16[128,1024]{1,0:T(8,128)(2,1)S(1)}, bf16[128,1024]{1,0:T(8,128)(2,1)S(1)}, u32[]{:S(2)}, u32[]{:S(2)}) collective-permute-start(bf16[128,1024]{1,0:T(8,128)(2,1)S(1)} %get-tuple-element.41.refs_0_), channel_id=1, source_target_pairs={{0,4},{4,8},{8,12},{12,0},{1,5},{5,9},{9,13},{13,1},{2,6},{6,10},{... | collective-permute-start | bytes 786440 | tf_op jit(solution)/shard_map/slot1/ppermute | solution.py:96
  6.4 2.2 %collective-permute-start.2 = (bf16[128,1024]{1,0:T(8,128)(2,1)S(1)}, bf16[128,1024]{1,0:T(8,128)(2,1)S(1)}, u32[]{:S(2)}, u32[]{:S(2)}) collective-permute-start(bf16[128,1024]{1,0:T(8,128)(2,1)S(1)} %get-tuple-element.41.refs_0_), channel_id=1, source_target_pairs={{4,0},{8,4},{12,8},{0,12},{5,1},{9,5},{13,9},{1,13},{6,2},{10,6},{... | collective-permute-start | bytes 786440 | tf_op jit(solution)/shard_map/slot1/ppermute | solution.py:96
  8.7 1.7 %dynamic-slice_bitcast_fusion = bf16[128,1024]{1,0:T(8,128)(2,1)} fusion(bf16[1,128,4096]{2,1,0:T(8,128)(2,1)} %param.10, s32[]{:T(128)S(6)} %select_n.77), kind=kLoop, calls=%fused_computation.13 | loop fusion | bytes 524292 | tf_op jit(solution)/shard_map/dynamic_slice | solution.py:283
  10.3 0.3 collective-permute-start.11
  10.6 0.5 collective-permute-done.5
  11.1 1.0 broadcast_select_fusion.2
  12.2 2.9 %collective-permute-start.6 = (bf16[128,1024]{1,0:T(8,128)(2,1)S(1)}, bf16[128,1024]{1,0:T(8,128)(2,1)S(1)}, u32[]{:S(2)}, u32[]{:S(2)}) collective-permute-start(bf16[128,1024]{1,0:T(8,128)(2,1)S(1)} %get-tuple-element.38.refs_5_), channel_id=1, source_target_pairs={{0,4},{4,8},{8,12},{12,0},{1,5},{5,9},{9,13},{13,1},{2,6},{6,10},{... | collective-permute-start | bytes 786440 | tf_op jit(solution)/shard_map/slot2/ppermute | solution.py:96
  15.0 2.1 %collective-permute-start.7 = (bf16[128,1024]{1,0:T(8,128)(2,1)S(1)}, bf16[128,1024]{1,0:T(8,128)(2,1)S(1)}, u32[]{:S(2)}, u32[]{:S(2)}) collective-permute-start(bf16[128,1024]{1,0:T(8,128)(2,1)S(1)} %get-tuple-element.38.refs_5_), channel_id=1, source_target_pairs={{4,0},{8,4},{12,8},{0,12},{5,1},{9,5},{13,9},{1,13},{6,2},{10,6},{... | collective-permute-start | bytes 786440 | tf_op jit(solution)/shard_map/slot2/ppermute | solution.py:96
  17.1 1.8 %constant_dynamic-slice_fusion = (bf16[128,1024]{1,0:T(8,128)(2,1)S(1)}, bf16[128,1024]{1,0:T(8,128)(2,1)}) fusion(bf16[128,4096]{1,0:T(8,128)(2,1)} %param.9, s32[]{:T(128)S(6)} %select_n.75, s32[]{:T(128)S(6)} %select_n.74), kind=kLoop, calls=%fused_computation.47 | loop fusion | bytes 1048584 | tf_op jit(solution)/shard_map/dynamic_slice | solution.py:283
  18.9 1.6 %collective-permute-start = (bf16[128,1024]{1,0:T(8,128)(2,1)S(1)}, bf16[128,1024]{1,0:T(8,128)(2,1)S(1)}, u32[]{:S(2)}, u32[]{:S(2)}) collective-permute-start(bf16[128,1024]{1,0:T(8,128)(2,1)S(1)} %get-tuple-element.42), channel_id=1, source_target_pairs={{0,16},{16,0},{1,17},{17,1},{2,18},{18,2},{3,19},{19,3},{4,20},{20... | collective-permute-start | bytes 786440 | tf_op jit(solution)/shard_map/ppermute | solution.py:294
  20.5 1.4 %collective-permute-done.2.refs_2_ = bf16[128,1024]{1,0:T(8,128)(2,1)S(1)} collective-permute-done((bf16[128,1024]{1,0:T(8,128)(2,1)S(1)}, bf16[128,1024]{1,0:T(8,128)(2,1)S(1)}, u32[]{:S(2)}, u32[]{:S(2)}) %collective-permute-start.2) | collective-permute-done | bytes 262176 | tf_op jit(solution)/shard_map/slot1/ppermute | solution.py:96
  21.9 0.2 collective-permute-start.3
  22.2 3.6 %collective-permute-start.4 = (bf16[64,1024]{1,0:T(8,128)(2,1)S(1)}, bf16[64,1024]{1,0:T(8,128)(2,1)S(1)}, u32[]{:S(2)}, u32[]{:S(2)}) collective-permute-start(bf16[64,1024]{1,0:T(8,128)(2,1)S(1)} %slice.53), channel_id=1, source_target_pairs={{4,0},{8,4},{12,8},{0,12},{5,1},{9,5},{13,9},{1,13},{6,2},{10,6},{... | collective-permute-start | bytes 393224 | tf_op jit(solution)/shard_map/slot1/ppermute | solution.py:97
  25.8 1.4 %collective-permute-done.6.refs_6_ = bf16[128,1024]{1,0:T(8,128)(2,1)S(1)} collective-permute-done((bf16[128,1024]{1,0:T(8,128)(2,1)S(1)}, bf16[128,1024]{1,0:T(8,128)(2,1)S(1)}, u32[]{:S(2)}, u32[]{:S(2)}) %collective-permute-start.6) | collective-permute-done | bytes 262176 | tf_op jit(solution)/shard_map/slot2/ppermute | solution.py:96
  27.2 5.7 %collective-permute-done.7.refs_7_ = bf16[128,1024]{1,0:T(8,128)(2,1)S(1)} collective-permute-done((bf16[128,1024]{1,0:T(8,128)(2,1)S(1)}, bf16[128,1024]{1,0:T(8,128)(2,1)S(1)}, u32[]{:S(2)}, u32[]{:S(2)}) %collective-permute-start.7) | collective-permute-done | bytes 262176 | tf_op jit(solution)/shard_map/slot2/ppermute | solution.py:96
  32.9 0.5 collective-permute-start.8
  33.5 0.1 copy-done.10
  33.6 3.3 %collective-permute-start.9 = (bf16[64,1024]{1,0:T(8,128)(2,1)S(1)}, bf16[64,1024]{1,0:T(8,128)(2,1)S(1)}, u32[]{:S(2)}, u32[]{:S(2)}) collective-permute-start(bf16[64,1024]{1,0:T(8,128)(2,1)S(1)} %slice.55), channel_id=1, source_target_pairs={{4,0},{8,4},{12,8},{0,12},{5,1},{9,5},{13,9},{1,13},{6,2},{10,6},{... | collective-permute-start | bytes 393224 | tf_op jit(solution)/shard_map/slot2/ppermute | solution.py:97
  37.2 1.4 %collective-permute-done.4.refs_4_ = bf16[64,1024]{1,0:T(8,128)(2,1)S(1)} collective-permute-done((bf16[64,1024]{1,0:T(8,128)(2,1)S(1)}, bf16[64,1024]{1,0:T(8,128)(2,1)S(1)}, u32[]{:S(2)}, u32[]{:S(2)}) %collective-permute-start.4) | collective-permute-done | bytes 131104 | tf_op jit(solution)/shard_map/slot1/ppermute | solution.py:97
  38.6 2.6 %collective-permute-done.8.refs_8_ = bf16[64,1024]{1,0:T(8,128)(2,1)S(1)} collective-permute-done((bf16[64,1024]{1,0:T(8,128)(2,1)S(1)}, bf16[64,1024]{1,0:T(8,128)(2,1)S(1)}, u32[]{:S(2)}, u32[]{:S(2)}) %collective-permute-start.8) | collective-permute-done | bytes 131104 | tf_op jit(solution)/shard_map/slot2/ppermute | solution.py:97
  41.2 1.5 %collective-permute-done.9.refs_9_ = bf16[64,1024]{1,0:T(8,128)(2,1)S(1)} collective-permute-done((bf16[64,1024]{1,0:T(8,128)(2,1)S(1)}, bf16[64,1024]{1,0:T(8,128)(2,1)S(1)}, u32[]{:S(2)}, u32[]{:S(2)}) %collective-permute-start.9) | collective-permute-done | bytes 131104 | tf_op jit(solution)/shard_map/slot2/ppermute | solution.py:97
  42.8 0.6 copy-done.17
  43.4 2.5 %first.1 = (f32[256,256]{1,0:T(8,128)S(1)}, f32[256,256]{1,0:T(8,128)S(1)}) custom-call(s32[3]{0:T(128)S(1)} %pad_add_fusion.flags, bf16[128,1024]{1,0:T(8,128)(2,1)} %get-tuple-element.43.g_own, bf16[128,1024]{1,0:T(8,128)(2,1)} %copy-done.12, bf16[128,1024]{1,0:T(8,128)(2,1)} %copy-done.5, bf16[128,1024]{1,0:T(8,128)(2,1)} %copy-done.7, ...), custom_call_target="tpu_custom_call" | custom-call | tf_op jit(solution)/shard_map/first/pallas_call | solution.py:265
  46.0 2.5 %collective-permute-start.17 = (bf16[256,1024]{1,0:T(8,128)(2,1)S(1)}, bf16[256,1024]{1,0:T(8,128)(2,1)S(1)}, u32[]{:S(2)}, u32[]{:S(2)}) collective-permute-start(bf16[256,1024]{1,0:T(8,128)(2,1)S(1)} %pad_maximum_fusion.refs_10_.refs_0_), channel_id=1, source_target_pairs={{4,0},{8,4},{12,8},{0,12},{5,1},{9,5},{13,9},{1,13},{6,2},{10,6},{... | collective-permute-start | bytes 1572872 | tf_op jit(solution)/shard_map/slot34/ppermute | solution.py:301
  48.5 6.8 %collective-permute-done.12.refs_11_.refs_1_ = bf16[256,1024]{1,0:T(8,128)(2,1)S(1)} collective-permute-done((bf16[256,1024]{1,0:T(8,128)(2,1)S(1)}, bf16[256,1024]{1,0:T(8,128)(2,1)S(1)}, u32[]{:S(2)}, u32[]{:S(2)}) %collective-permute-start.12) | collective-permute-done | bytes 524320 | tf_op jit(solution)/shard_map/slot34/ppermute | solution.py:301
  55.3 1.5 %collective-permute-start.13 = (bf16[256,256]{1,0:T(8,128)(2,1)S(1)}, bf16[256,256]{1,0:T(8,128)(2,1)S(1)}, u32[]{:S(2)}, u32[]{:S(2)}) collective-permute-start(bf16[256,256]{1,0:T(8,128)(2,1)S(1)} %add_convert_fusion.3), channel_id=1, source_target_pairs={{0,18},{18,0},{2,16},{16,2},{1,19},{19,1},{3,17},{17,3},{4,22},{22... | collective-permute-start | bytes 393224 | tf_op jit(solution)/shard_map/ppermute | solution.py:107
  56.8 1.5 %collective-permute-start.14 = (bf16[256,256]{1,0:T(8,128)(2,1)S(1)}, bf16[256,256]{1,0:T(8,128)(2,1)S(1)}, u32[]{:S(2)}, u32[]{:S(2)}) collective-permute-start(bf16[256,256]{1,0:T(8,128)(2,1)S(1)} %add_convert_fusion.3), channel_id=1, source_target_pairs={{0,2},{2,0},{1,3},{3,1},{4,6},{6,4},{5,7},{7,5},{8,10},{10,8},{9,1... | collective-permute-start | bytes 393224 | tf_op jit(solution)/shard_map/ppermute | solution.py:107
  58.3 0.5 collective-permute-start.15
  58.8 7.7 %collective-permute-done.17.refs_12_.refs_2_ = bf16[256,1024]{1,0:T(8,128)(2,1)S(1)} collective-permute-done((bf16[256,1024]{1,0:T(8,128)(2,1)S(1)}, bf16[256,1024]{1,0:T(8,128)(2,1)S(1)}, u32[]{:S(2)}, u32[]{:S(2)}) %collective-permute-start.17) | collective-permute-done | bytes 524320 | tf_op jit(solution)/shard_map/slot34/ppermute | solution.py:301
  66.5 1.3 %collective-permute-start.18 = (bf16[64,1024]{1,0:T(8,128)(2,1)S(1)}, bf16[64,1024]{1,0:T(8,128)(2,1)S(1)}, u32[]{:S(2)}, u32[]{:S(2)}) collective-permute-start(bf16[64,1024]{1,0:T(8,128)(2,1)S(1)} %get-tuple-element.45), channel_id=1, source_target_pairs={{4,0},{8,4},{12,8},{0,12},{5,1},{9,5},{13,9},{1,13},{6,2},{10,6},{... | collective-permute-start | bytes 393224 | tf_op jit(solution)/shard_map/slot3/ppermute | solution.py:303
  67.9 0.7 collective-permute-done.16.refs_13_
  68.6 3.4 %collective-permute-done.18.refs_14_ = bf16[64,1024]{1,0:T(8,128)(2,1)S(1)} collective-permute-done((bf16[64,1024]{1,0:T(8,128)(2,1)S(1)}, bf16[64,1024]{1,0:T(8,128)(2,1)S(1)}, u32[]{:S(2)}, u32[]{:S(2)}) %collective-permute-start.18) | collective-permute-done | bytes 131104 | tf_op jit(solution)/shard_map/slot3/ppermute | solution.py:303
  72.0 1.3 %collective-permute-done.19.other = bf16[256,256]{1,0:T(8,128)(2,1)S(1)} collective-permute-done((bf16[256,256]{1,0:T(8,128)(2,1)S(1)}, bf16[256,256]{1,0:T(8,128)(2,1)S(1)}, u32[]{:S(2)}, u32[]{:S(2)}) %collective-permute-start.19) | collective-permute-done | bytes 131104 | tf_op jit(solution)/shard_map/ppermute | solution.py:112
  73.4 3.1 %middle.1 = (bf16[256,1024]{1,0:T(8,128)(2,1)S(1)}, f32[256,256]{1,0:T(8,128)S(1)}, f32[256,256]{1,0:T(8,128)S(1)}) custom-call(s32[3]{0:T(128)S(1)} %pad_add_fusion.flags, bf16[128,1024]{1,0:T(8,128)(2,1)} %get-tuple-element.43.g_own, bf16[128,1024]{1,0:T(8,128)(2,1)} %copy-done.12, bf16[256,256]{1,0:T(8,128)(2,1)S(1)} %add_convert_fusion.2.mine, ...), custom_call_target="tpu_custom_call" | custom-call | tf_op jit(solution)/shard_map/middle/pallas_call | solution.py:265
  76.5 0.2 collective-permute-start.20
  76.7 0.5 fusion.1
  77.3 0.4 collective-permute-start.30
  77.7 0.7 copy-done.23
  78.5 1.6 %collective-permute-start.21 = (bf16[256,256]{1,0:T(8,128)(2,1)S(1)}, bf16[256,256]{1,0:T(8,128)(2,1)S(1)}, u32[]{:S(2)}, u32[]{:S(2)}) collective-permute-start(bf16[256,256]{1,0:T(8,128)(2,1)S(1)} %add_convert_fusion.1), channel_id=1, source_target_pairs={{0,18},{18,0},{2,16},{16,2},{1,19},{19,1},{3,17},{17,3},{4,22},{22... | collective-permute-start | bytes 393224 | tf_op jit(solution)/shard_map/ppermute | solution.py:107
  80.1 1.5 %collective-permute-start.22 = (bf16[256,256]{1,0:T(8,128)(2,1)S(1)}, bf16[256,256]{1,0:T(8,128)(2,1)S(1)}, u32[]{:S(2)}, u32[]{:S(2)}) collective-permute-start(bf16[256,256]{1,0:T(8,128)(2,1)S(1)} %add_convert_fusion.1), channel_id=1, source_target_pairs={{0,2},{2,0},{1,3},{3,1},{4,6},{6,4},{5,7},{7,5},{8,10},{10,8},{9,1... | collective-permute-start | bytes 393224 | tf_op jit(solution)/shard_map/ppermute | solution.py:107
  81.6 0.5 collective-permute-start.23
  82.1 0.6 collective-permute-start.24
  82.6 3.2 %collective-permute-done.21 = bf16[256,256]{1,0:T(8,128)(2,1)S(1)} collective-permute-done((bf16[256,256]{1,0:T(8,128)(2,1)S(1)}, bf16[256,256]{1,0:T(8,128)(2,1)S(1)}, u32[]{:S(2)}, u32[]{:S(2)}) %collective-permute-start.21) | collective-permute-done | bytes 131104 | tf_op jit(solution)/shard_map/ppermute | solution.py:107
  85.8 2.5 %collective-permute-start.25 = (bf16[64,1024]{1,0:T(8,128)(2,1)S(1)}, bf16[64,1024]{1,0:T(8,128)(2,1)S(1)}, u32[]{:S(2)}, u32[]{:S(2)}) collective-permute-start(bf16[64,1024]{1,0:T(8,128)(2,1)S(1)} %get-tuple-element.31), channel_id=1, source_target_pairs={{4,0},{8,4},{12,8},{0,12},{5,1},{9,5},{13,9},{1,13},{6,2},{10,6},{... | collective-permute-start | bytes 393224 | tf_op jit(solution)/shard_map/slot4/ppermute | solution.py:306
  88.5 1.5 %collective-permute-done.24.refs_3_ = bf16[64,1024]{1,0:T(8,128)(2,1)S(1)} collective-permute-done((bf16[64,1024]{1,0:T(8,128)(2,1)S(1)}, bf16[64,1024]{1,0:T(8,128)(2,1)S(1)}, u32[]{:S(2)}, u32[]{:S(2)}) %collective-permute-start.24) | collective-permute-done | bytes 131104 | tf_op jit(solution)/shard_map/slot4/ppermute | solution.py:306
  89.9 1.5 %collective-permute-done.25.refs_4_ = bf16[64,1024]{1,0:T(8,128)(2,1)S(1)} collective-permute-done((bf16[64,1024]{1,0:T(8,128)(2,1)S(1)}, bf16[64,1024]{1,0:T(8,128)(2,1)S(1)}, u32[]{:S(2)}, u32[]{:S(2)}) %collective-permute-start.25) | collective-permute-done | bytes 131104 | tf_op jit(solution)/shard_map/slot4/ppermute | solution.py:306
  92.2 0.6 collective-permute-done.26.other
  92.8 2.5 %last.1 = (bf16[128,1024]{1,0:T(8,128)(2,1)S(1)}, bf16[128,1024]{1,0:T(8,128)(2,1)S(1)}, bf16[128,1024]{1,0:T(8,128)(2,1)S(1)}, bf16[128,1024]{1,0:T(8,128)(2,1)S(1)}) custom-call(s32[3]{0:T(128)S(1)} %pad_add_fusion.flags, bf16[256,1024]{1,0:T(8,128)(2,1)} %copy-done.1, bf16[256,256]{1,0:T(8,128)(2,1)S(1)} %add_convert_fusion.mine, ...), custom_call_target="tpu_custom_call" | custom-call | tf_op jit(solution)/shard_map/last/pallas_call | solution.py:265
  95.3 0.5 collective-permute-start.28
  95.8 1.6 %collective-permute-start.27 = (bf16[128,1024]{1,0:T(8,128)(2,1)S(1)}, bf16[128,1024]{1,0:T(8,128)(2,1)S(1)}, u32[]{:S(2)}, u32[]{:S(2)}) collective-permute-start(bf16[128,1024]{1,0:T(8,128)(2,1)S(1)} %get-tuple-element.34), channel_id=1, source_target_pairs={{0,16},{16,0},{1,17},{17,1},{2,18},{18,2},{3,19},{19,3},{4,20},{20... | collective-permute-start | bytes 786440 | tf_op jit(solution)/shard_map/ppermute | solution.py:333
  97.4 0.2 fusion.4
  97.6 0.3 fusion
  97.9 0.1 convert_element_type.64.refs_0_
  98.0 1.5 %collective-permute-start.29 = (bf16[128,1024]{1,0:T(8,128)(2,1)S(1)}, bf16[128,1024]{1,0:T(8,128)(2,1)S(1)}, u32[]{:S(2)}, u32[]{:S(2)}) collective-permute-start(bf16[128,1024]{1,0:T(8,128)(2,1)S(1)} %get-tuple-element.36), channel_id=1, source_target_pairs={{0,18},{18,0},{2,16},{16,2},{1,19},{19,1},{3,17},{17,3},{4,22},{22... | collective-permute-start | bytes 786440 | tf_op jit(solution)/shard_map/ppermute | solution.py:331
  99.5 0.1 broadcast_in_dim.32
  99.7 4.9 %collective-permute-done.28 = bf16[128,1024]{1,0:T(8,128)(2,1)S(1)} collective-permute-done((bf16[128,1024]{1,0:T(8,128)(2,1)S(1)}, bf16[128,1024]{1,0:T(8,128)(2,1)S(1)}, u32[]{:S(2)}, u32[]{:S(2)}) %collective-permute-start.28) | collective-permute-done | bytes 262176 | tf_op jit(solution)/shard_map/ppermute | solution.py:332
  104.5 0.6 collective-permute-start.31
  105.1 3.3 %collective-permute-start.32 = (bf16[4,4096]{1,0:T(4,128)(2,1)S(1)}, bf16[4,4096]{1,0:T(4,128)(2,1)S(1)}, u32[]{:S(2)}, u32[]{:S(2)}) collective-permute-start(bf16[4,4096]{1,0:T(4,128)(2,1)S(1)} %convert_element_type.64.refs_0_), channel_id=1, source_target_pairs={{4,0},{8,4},{12,8},{0,12},{5,1},{9,5},{13,9},{1,13},{6,2},{10,6},{... | collective-permute-start | bytes 98312 | tf_op jit(solution)/shard_map/ppermute | solution.py:354
  108.3 0.5 collective-permute-start.33
  108.9 1.4 %collective-permute-done.29 = bf16[128,1024]{1,0:T(8,128)(2,1)S(1)} collective-permute-done((bf16[128,1024]{1,0:T(8,128)(2,1)S(1)}, bf16[128,1024]{1,0:T(8,128)(2,1)S(1)}, u32[]{:S(2)}, u32[]{:S(2)}) %collective-permute-start.29) | collective-permute-done | bytes 262176 | tf_op jit(solution)/shard_map/ppermute | solution.py:331
  110.4 2.8 %collective-permute-done.33.refs_3_ = bf16[4,4096]{1,0:T(4,128)(2,1)S(1)} collective-permute-done((bf16[4,4096]{1,0:T(4,128)(2,1)S(1)}, bf16[4,4096]{1,0:T(4,128)(2,1)S(1)}, u32[]{:S(2)}, u32[]{:S(2)}) %collective-permute-start.33) | collective-permute-done | bytes 32800 | tf_op jit(solution)/shard_map/ppermute | solution.py:354
  113.2 2.0 %scores.1 = f32[1,16]{1,0:T(1,128)} custom-call(f32[1]{0:T(128)S(6)} %mul.57.shift, bf16[4,4096]{1,0:T(4,128)(2,1)S(1)} %convert_element_type.64.refs_0_, bf16[4,4096]{1,0:T(4,128)(2,1)S(1)} %collective-permute-done.31.refs_1_, bf16[4,4096]{1,0:T(4,128)(2,1)S(1)} %collective-permute-done.32.refs_2_, bf16[4,4096]{1,0:T(4,128)(2,1)S(1)} %collective-permute-done.33.refs_3_), custom_call_target="tpu_custom_call" | custom-call | tf_op jit(solution)/shard_map/scores/pallas_call | solution.py:252
  (89 shorter events, 1.2 us)
Async XLA Ops:
  0.6 76.1 %copy-start = (bf16[1,128,4096]{2,1,0:T(8,128)(2,1)S(1)}, bf16[1,128,4096]{2,1,0:T(8,128)(2,1)}, u32[]{:S(2)}) copy-start(bf16[1,128,4096]{2,1,0:T(8,128)(2,1)} %param.8) | copy-start | bytes 3145732
  1.8 8.5 %copy-start.5 = (bf16[128,1024]{1,0:T(8,128)(2,1)}, bf16[128,1024]{1,0:T(8,128)(2,1)S(1)}, u32[]{:S(2)}) copy-start(bf16[128,1024]{1,0:T(8,128)(2,1)S(1)} %get-tuple-element.41.refs_0_) | copy-start | bytes 786436
  1.8 9.3 %collective-permute-start.5 = (bf16[128,1024]{1,0:T(8,128)(2,1)S(1)}, bf16[128,1024]{1,0:T(8,128)(2,1)S(1)}, u32[]{:S(2)}, u32[]{:S(2)}) collective-permute-start(bf16[128,1024]{1,0:T(8,128)(2,1)S(1)} %get-tuple-element.40), channel_id=1, source_target_pairs={{0,2},{2,0},{1,3},{3,1},{4,6},{6,4},{5,7},{7,5},{8,10},{10,8},{9,1... | collective-permute-start | bytes 786440 | tf_op jit(solution)/shard_map/ppermute | solution.py:291
  4.8 14.1 %collective-permute-start.1 = (bf16[128,1024]{1,0:T(8,128)(2,1)S(1)}, bf16[128,1024]{1,0:T(8,128)(2,1)S(1)}, u32[]{:S(2)}, u32[]{:S(2)}) collective-permute-start(bf16[128,1024]{1,0:T(8,128)(2,1)S(1)} %get-tuple-element.41.refs_0_), channel_id=1, source_target_pairs={{0,4},{4,8},{8,12},{12,0},{1,5},{5,9},{9,13},{13,1},{2,6},{6,10},{... | collective-permute-start | bytes 786440 | tf_op jit(solution)/shard_map/slot1/ppermute | solution.py:96
  6.4 15.5 %collective-permute-start.2 = (bf16[128,1024]{1,0:T(8,128)(2,1)S(1)}, bf16[128,1024]{1,0:T(8,128)(2,1)S(1)}, u32[]{:S(2)}, u32[]{:S(2)}) collective-permute-start(bf16[128,1024]{1,0:T(8,128)(2,1)S(1)} %get-tuple-element.41.refs_0_), channel_id=1, source_target_pairs={{4,0},{8,4},{12,8},{0,12},{5,1},{9,5},{13,9},{1,13},{6,2},{10,6},{... | collective-permute-start | bytes 786440 | tf_op jit(solution)/shard_map/slot1/ppermute | solution.py:96
  10.3 11.8 %collective-permute-start.11 = (bf16[128,1024]{1,0:T(8,128)(2,1)}, bf16[128,1024]{1,0:T(8,128)(2,1)S(1)}, u32[]{:S(2)}, u32[]{:S(2)}) collective-permute-start(bf16[128,1024]{1,0:T(8,128)(2,1)} %dynamic-slice_bitcast_fusion), channel_id=1, source_target_pairs={{0,2},{2,0},{1,3},{3,1},{4,6},{6,4},{5,7},{7,5},{8,10},{10,8},{9,1... | collective-permute-start | bytes 786440 | tf_op jit(solution)/shard_map/ppermute | solution.py:292
  12.2 6.7 %copy-start.6 = (bf16[128,1024]{1,0:T(8,128)(2,1)}, bf16[128,1024]{1,0:T(8,128)(2,1)S(1)}, u32[]{:S(2)}) copy-start(bf16[128,1024]{1,0:T(8,128)(2,1)S(1)} %get-tuple-element.38.refs_5_) | copy-start | bytes 786436
  12.2 15.0 %collective-permute-start.6 = (bf16[128,1024]{1,0:T(8,128)(2,1)S(1)}, bf16[128,1024]{1,0:T(8,128)(2,1)S(1)}, u32[]{:S(2)}, u32[]{:S(2)}) collective-permute-start(bf16[128,1024]{1,0:T(8,128)(2,1)S(1)} %get-tuple-element.38.refs_5_), channel_id=1, source_target_pairs={{0,4},{4,8},{8,12},{12,0},{1,5},{5,9},{9,13},{13,1},{2,6},{6,10},{... | collective-permute-start | bytes 786440 | tf_op jit(solution)/shard_map/slot2/ppermute | solution.py:96
  15.0 17.9 %collective-permute-start.7 = (bf16[128,1024]{1,0:T(8,128)(2,1)S(1)}, bf16[128,1024]{1,0:T(8,128)(2,1)S(1)}, u32[]{:S(2)}, u32[]{:S(2)}) collective-permute-start(bf16[128,1024]{1,0:T(8,128)(2,1)S(1)} %get-tuple-element.38.refs_5_), channel_id=1, source_target_pairs={{4,0},{8,4},{12,8},{0,12},{5,1},{9,5},{13,9},{1,13},{6,2},{10,6},{... | collective-permute-start | bytes 786440 | tf_op jit(solution)/shard_map/slot2/ppermute | solution.py:96
  18.9 3.3 %copy-start.7 = (bf16[128,1024]{1,0:T(8,128)(2,1)}, bf16[128,1024]{1,0:T(8,128)(2,1)S(1)}, u32[]{:S(2)}) copy-start(bf16[128,1024]{1,0:T(8,128)(2,1)S(1)} %collective-permute-done.1.refs_1_) | copy-start | bytes 786436
  18.9 18.1 %collective-permute-start = (bf16[128,1024]{1,0:T(8,128)(2,1)S(1)}, bf16[128,1024]{1,0:T(8,128)(2,1)S(1)}, u32[]{:S(2)}, u32[]{:S(2)}) collective-permute-start(bf16[128,1024]{1,0:T(8,128)(2,1)S(1)} %get-tuple-element.42), channel_id=1, source_target_pairs={{0,16},{16,0},{1,17},{17,1},{2,18},{18,2},{3,19},{19,3},{4,20},{20... | collective-permute-start | bytes 786440 | tf_op jit(solution)/shard_map/ppermute | solution.py:294
  21.9 11.0 %copy-start.8 = (bf16[128,1024]{1,0:T(8,128)(2,1)}, bf16[128,1024]{1,0:T(8,128)(2,1)S(1)}, u32[]{:S(2)}) copy-start(bf16[128,1024]{1,0:T(8,128)(2,1)S(1)} %collective-permute-done.2.refs_2_) | copy-start | bytes 786436
  21.9 15.3 %collective-permute-start.3 = (bf16[64,1024]{1,0:T(8,128)(2,1)S(1)}, bf16[64,1024]{1,0:T(8,128)(2,1)S(1)}, u32[]{:S(2)}, u32[]{:S(2)}) collective-permute-start(bf16[64,1024]{1,0:T(8,128)(2,1)S(1)} %slice.52), channel_id=1, source_target_pairs={{0,4},{4,8},{8,12},{12,0},{1,5},{5,9},{9,13},{13,1},{2,6},{6,10},{... | collective-permute-start | bytes 393224 | tf_op jit(solution)/shard_map/slot1/ppermute | solution.py:97
  22.2 16.4 %collective-permute-start.4 = (bf16[64,1024]{1,0:T(8,128)(2,1)S(1)}, bf16[64,1024]{1,0:T(8,128)(2,1)S(1)}, u32[]{:S(2)}, u32[]{:S(2)}) collective-permute-start(bf16[64,1024]{1,0:T(8,128)(2,1)S(1)} %slice.53), channel_id=1, source_target_pairs={{4,0},{8,4},{12,8},{0,12},{5,1},{9,5},{13,9},{1,13},{6,2},{10,6},{... | collective-permute-start | bytes 393224 | tf_op jit(solution)/shard_map/slot1/ppermute | solution.py:97
  27.2 6.3 %copy-start.9 = (bf16[128,1024]{1,0:T(8,128)(2,1)}, bf16[128,1024]{1,0:T(8,128)(2,1)S(1)}, u32[]{:S(2)}) copy-start(bf16[128,1024]{1,0:T(8,128)(2,1)S(1)} %collective-permute-done.6.refs_6_) | copy-start | bytes 786436
  32.9 0.7 copy-start.10
  32.9 8.3 %collective-permute-start.8 = (bf16[64,1024]{1,0:T(8,128)(2,1)S(1)}, bf16[64,1024]{1,0:T(8,128)(2,1)S(1)}, u32[]{:S(2)}, u32[]{:S(2)}) collective-permute-start(bf16[64,1024]{1,0:T(8,128)(2,1)S(1)} %slice.54), channel_id=1, source_target_pairs={{0,4},{4,8},{8,12},{12,0},{1,5},{5,9},{9,13},{13,1},{2,6},{6,10},{... | collective-permute-start | bytes 393224 | tf_op jit(solution)/shard_map/slot2/ppermute | solution.py:97
  33.6 9.1 %collective-permute-start.9 = (bf16[64,1024]{1,0:T(8,128)(2,1)S(1)}, bf16[64,1024]{1,0:T(8,128)(2,1)S(1)}, u32[]{:S(2)}, u32[]{:S(2)}) collective-permute-start(bf16[64,1024]{1,0:T(8,128)(2,1)S(1)} %slice.55), channel_id=1, source_target_pairs={{4,0},{8,4},{12,8},{0,12},{5,1},{9,5},{13,9},{1,13},{6,2},{10,6},{... | collective-permute-start | bytes 393224 | tf_op jit(solution)/shard_map/slot2/ppermute | solution.py:97
  37.0 8.9 %copy-start.2 = (bf16[256,1024]{1,0:T(8,128)(2,1)}, bf16[256,1024]{1,0:T(8,128)(2,1)S(1)}, u32[]{:S(2)}) copy-start(bf16[256,1024]{1,0:T(8,128)(2,1)S(1)} %pad_maximum_fusion.refs_10_.refs_0_) | copy-start | bytes 1572868
  37.0 5.7 %copy-start.12 = (bf16[128,1024]{1,0:T(8,128)(2,1)}, bf16[128,1024]{1,0:T(8,128)(2,1)S(1)}, u32[]{:S(2)}) copy-start(bf16[128,1024]{1,0:T(8,128)(2,1)S(1)} %collective-permute-done.g_other) | copy-start | bytes 786436
  37.1 18.2 %collective-permute-start.12 = (bf16[256,1024]{1,0:T(8,128)(2,1)S(1)}, bf16[256,1024]{1,0:T(8,128)(2,1)S(1)}, u32[]{:S(2)}, u32[]{:S(2)}) collective-permute-start(bf16[256,1024]{1,0:T(8,128)(2,1)S(1)} %pad_maximum_fusion.refs_10_.refs_0_), channel_id=1, source_target_pairs={{0,4},{4,8},{8,12},{12,0},{1,5},{5,9},{9,13},{13,1},{2,6},{6,10},{... | collective-permute-start | bytes 1572872 | tf_op jit(solution)/shard_map/slot34/ppermute | solution.py:301
  37.2 5.5 %copy-start.14 = (bf16[64,1024]{1,0:T(8,128)(2,1)}, bf16[64,1024]{1,0:T(8,128)(2,1)S(1)}, u32[]{:S(2)}) copy-start(bf16[64,1024]{1,0:T(8,128)(2,1)S(1)} %collective-permute-done.3.refs_3_) | copy-start | bytes 393220
  38.6 4.2 %copy-start.15 = (bf16[64,1024]{1,0:T(8,128)(2,1)}, bf16[64,1024]{1,0:T(8,128)(2,1)S(1)}, u32[]{:S(2)}) copy-start(bf16[64,1024]{1,0:T(8,128)(2,1)S(1)} %collective-permute-done.4.refs_4_) | copy-start | bytes 393220
  41.2 1.5 %copy-start.16 = (bf16[64,1024]{1,0:T(8,128)(2,1)}, bf16[64,1024]{1,0:T(8,128)(2,1)S(1)}, u32[]{:S(2)}) copy-start(bf16[64,1024]{1,0:T(8,128)(2,1)S(1)} %collective-permute-done.8.refs_8_) | copy-start | bytes 393220
  42.7 0.7 copy-start.17
  45.9 2.6 %collective-permute-start.10 = (f32[256,256]{1,0:T(8,128)S(1)}, f32[256,256]{1,0:T(8,128)S(1)}, u32[]{:S(2)}, u32[]{:S(2)}) collective-permute-start(f32[256,256]{1,0:T(8,128)S(1)} %get-tuple-element.21), channel_id=1, source_target_pairs={{0,1},{1,0},{2,3},{3,2},{4,5},{5,4},{6,7},{7,6},{8,9},{9,8},{10,11... | collective-permute-start | bytes 786440 | tf_op jit(solution)/shard_map/ppermute | solution.py:106
  46.0 20.5 %collective-permute-start.17 = (bf16[256,1024]{1,0:T(8,128)(2,1)S(1)}, bf16[256,1024]{1,0:T(8,128)(2,1)S(1)}, u32[]{:S(2)}, u32[]{:S(2)}) collective-permute-start(bf16[256,1024]{1,0:T(8,128)(2,1)S(1)} %pad_maximum_fusion.refs_10_.refs_0_), channel_id=1, source_target_pairs={{4,0},{8,4},{12,8},{0,12},{5,1},{9,5},{13,9},{1,13},{6,2},{10,6},{... | collective-permute-start | bytes 1572872 | tf_op jit(solution)/shard_map/slot34/ppermute | solution.py:301
  55.3 11.3 %copy-start.3 = (bf16[256,1024]{1,0:T(8,128)(2,1)}, bf16[256,1024]{1,0:T(8,128)(2,1)S(1)}, u32[]{:S(2)}) copy-start(bf16[256,1024]{1,0:T(8,128)(2,1)S(1)} %collective-permute-done.12.refs_11_.refs_1_) | copy-start | bytes 1572868
  55.3 12.5 %collective-permute-start.13 = (bf16[256,256]{1,0:T(8,128)(2,1)S(1)}, bf16[256,256]{1,0:T(8,128)(2,1)S(1)}, u32[]{:S(2)}, u32[]{:S(2)}) collective-permute-start(bf16[256,256]{1,0:T(8,128)(2,1)S(1)} %add_convert_fusion.3), channel_id=1, source_target_pairs={{0,18},{18,0},{2,16},{16,2},{1,19},{19,1},{3,17},{17,3},{4,22},{22... | collective-permute-start | bytes 393224 | tf_op jit(solution)/shard_map/ppermute | solution.py:107
  56.8 11.0 %collective-permute-start.14 = (bf16[256,256]{1,0:T(8,128)(2,1)S(1)}, bf16[256,256]{1,0:T(8,128)(2,1)S(1)}, u32[]{:S(2)}, u32[]{:S(2)}) collective-permute-start(bf16[256,256]{1,0:T(8,128)(2,1)S(1)} %add_convert_fusion.3), channel_id=1, source_target_pairs={{0,2},{2,0},{1,3},{3,1},{4,6},{6,4},{5,7},{7,5},{8,10},{10,8},{9,1... | collective-permute-start | bytes 393224 | tf_op jit(solution)/shard_map/ppermute | solution.py:107
  58.3 9.5 %collective-permute-start.15 = (bf16[256,256]{1,0:T(8,128)(2,1)S(1)}, bf16[256,256]{1,0:T(8,128)(2,1)S(1)}, u32[]{:S(2)}, u32[]{:S(2)}) collective-permute-start(bf16[256,256]{1,0:T(8,128)(2,1)S(1)} %add_convert_fusion.3), channel_id=1, source_target_pairs={{0,16},{16,0},{1,17},{17,1},{2,18},{18,2},{3,19},{19,3},{4,20},{20... | collective-permute-start | bytes 393224 | tf_op jit(solution)/shard_map/ppermute | solution.py:107
  58.8 9.8 %collective-permute-start.16 = (bf16[64,1024]{1,0:T(8,128)(2,1)S(1)}, bf16[64,1024]{1,0:T(8,128)(2,1)S(1)}, u32[]{:S(2)}, u32[]{:S(2)}) collective-permute-start(bf16[64,1024]{1,0:T(8,128)(2,1)S(1)} %get-tuple-element.47), channel_id=1, source_target_pairs={{0,4},{4,8},{8,12},{12,0},{1,5},{5,9},{9,13},{13,1},{2,6},{6,10},{... | collective-permute-start | bytes 393224 | tf_op jit(solution)/shard_map/slot3/ppermute | solution.py:303
  66.5 1.4 %copy-start.4 = (bf16[256,1024]{1,0:T(8,128)(2,1)}, bf16[256,1024]{1,0:T(8,128)(2,1)S(1)}, u32[]{:S(2)}) copy-start(bf16[256,1024]{1,0:T(8,128)(2,1)S(1)} %collective-permute-done.17.refs_12_.refs_2_) | copy-start | bytes 1572868
  66.5 5.5 %collective-permute-start.18 = (bf16[64,1024]{1,0:T(8,128)(2,1)S(1)}, bf16[64,1024]{1,0:T(8,128)(2,1)S(1)}, u32[]{:S(2)}, u32[]{:S(2)}) collective-permute-start(bf16[64,1024]{1,0:T(8,128)(2,1)S(1)} %get-tuple-element.45), channel_id=1, source_target_pairs={{4,0},{8,4},{12,8},{0,12},{5,1},{9,5},{13,9},{1,13},{6,2},{10,6},{... | collective-permute-start | bytes 393224 | tf_op jit(solution)/shard_map/slot3/ppermute | solution.py:303
  67.9 8.8 %copy-start.13 = (bf16[1,64,4096]{2,1,0:T(8,128)(2,1)S(1)}, bf16[1,64,4096]{2,1,0:T(8,128)(2,1)}, u32[]{:S(2)}) copy-start(bf16[1,64,4096]{2,1,0:T(8,128)(2,1)} %param.12) | copy-start | bytes 1572868
  68.6 4.8 %copy-start.20 = (bf16[64,1024]{1,0:T(8,128)(2,1)}, bf16[64,1024]{1,0:T(8,128)(2,1)S(1)}, u32[]{:S(2)}) copy-start(bf16[64,1024]{1,0:T(8,128)(2,1)S(1)} %collective-permute-done.16.refs_13_) | copy-start | bytes 393220
  72.0 1.4 %copy-start.21 = (bf16[64,1024]{1,0:T(8,128)(2,1)}, bf16[64,1024]{1,0:T(8,128)(2,1)S(1)}, u32[]{:S(2)}) copy-start(bf16[64,1024]{1,0:T(8,128)(2,1)S(1)} %collective-permute-done.18.refs_14_) | copy-start | bytes 393220
  72.0 1.3 %collective-permute-start.19 = (bf16[256,256]{1,0:T(8,128)(2,1)S(1)}, bf16[256,256]{1,0:T(8,128)(2,1)S(1)}, u32[]{:S(2)}, u32[]{:S(2)}) collective-permute-start(bf16[256,256]{1,0:T(8,128)(2,1)S(1)} %add_convert_fusion.2.mine), channel_id=1, source_target_pairs={{0,1},{1,0},{2,3},{3,2},{4,5},{5,4},{6,7},{7,6},{8,9},{9,8},{10,11... | collective-permute-start | bytes 393224 | tf_op jit(solution)/shard_map/ppermute | solution.py:112
  76.5 0.8 copy-start.1
  76.5 2.0 %collective-permute-start.20 = (f32[256,256]{1,0:T(8,128)S(1)}, f32[256,256]{1,0:T(8,128)S(1)}, u32[]{:S(2)}, u32[]{:S(2)}) collective-permute-start(f32[256,256]{1,0:T(8,128)S(1)} %get-tuple-element.29), channel_id=1, source_target_pairs={{0,1},{1,0},{2,3},{3,2},{4,5},{5,4},{6,7},{7,6},{8,9},{9,8},{10,11... | collective-permute-start | bytes 786440 | tf_op jit(solution)/shard_map/ppermute | solution.py:106
  77.3 20.3 %collective-permute-start.30 = (f32[128,64]{0,1:T(8,128)S(1)}, f32[128,64]{0,1:T(8,128)S(1)}, u32[]{:S(2)}, u32[]{:S(2)}) collective-permute-start(f32[128,64]{0,1:T(8,128)S(1)} %fusion.1), channel_id=1, source_target_pairs={{0,1},{1,0},{2,3},{3,2},{4,5},{5,4},{6,7},{7,6},{8,9},{9,8},{10,11... | collective-permute-start | bytes 98312 | tf_op jit(solution)/shard_map/ppermute | solution.py:351
  77.7 0.7 copy-start.23
  78.5 7.3 %collective-permute-start.21 = (bf16[256,256]{1,0:T(8,128)(2,1)S(1)}, bf16[256,256]{1,0:T(8,128)(2,1)S(1)}, u32[]{:S(2)}, u32[]{:S(2)}) collective-permute-start(bf16[256,256]{1,0:T(8,128)(2,1)S(1)} %add_convert_fusion.1), channel_id=1, source_target_pairs={{0,18},{18,0},{2,16},{16,2},{1,19},{19,1},{3,17},{17,3},{4,22},{22... | collective-permute-start | bytes 393224 | tf_op jit(solution)/shard_map/ppermute | solution.py:107
  80.1 8.3 %collective-permute-start.22 = (bf16[256,256]{1,0:T(8,128)(2,1)S(1)}, bf16[256,256]{1,0:T(8,128)(2,1)S(1)}, u32[]{:S(2)}, u32[]{:S(2)}) collective-permute-start(bf16[256,256]{1,0:T(8,128)(2,1)S(1)} %add_convert_fusion.1), channel_id=1, source_target_pairs={{0,2},{2,0},{1,3},{3,1},{4,6},{6,4},{5,7},{7,5},{8,10},{10,8},{9,1... | collective-permute-start | bytes 393224 | tf_op jit(solution)/shard_map/ppermute | solution.py:107
  81.6 6.8 %collective-permute-start.23 = (bf16[256,256]{1,0:T(8,128)(2,1)S(1)}, bf16[256,256]{1,0:T(8,128)(2,1)S(1)}, u32[]{:S(2)}, u32[]{:S(2)}) collective-permute-start(bf16[256,256]{1,0:T(8,128)(2,1)S(1)} %add_convert_fusion.1), channel_id=1, source_target_pairs={{0,16},{16,0},{1,17},{17,1},{2,18},{18,2},{3,19},{19,3},{4,20},{20... | collective-permute-start | bytes 393224 | tf_op jit(solution)/shard_map/ppermute | solution.py:107
  82.1 9.3 %copy-start.22 = (bf16[1,64,512]{2,1,0:T(8,128)(2,1)S(1)}, bf16[1,64,512]{2,1,0:T(8,128)(2,1)}, u32[]{:S(2)}) copy-start(bf16[1,64,512]{2,1,0:T(8,128)(2,1)} %param.13) | copy-start | bytes 196612
  82.1 7.8 %collective-permute-start.24 = (bf16[64,1024]{1,0:T(8,128)(2,1)S(1)}, bf16[64,1024]{1,0:T(8,128)(2,1)S(1)}, u32[]{:S(2)}, u32[]{:S(2)}) collective-permute-start(bf16[64,1024]{1,0:T(8,128)(2,1)S(1)} %get-tuple-element.30), channel_id=1, source_target_pairs={{0,4},{4,8},{8,12},{12,0},{1,5},{5,9},{9,13},{13,1},{2,6},{6,10},{... | collective-permute-start | bytes 393224 | tf_op jit(solution)/shard_map/slot4/ppermute | solution.py:306
  85.8 5.6 %collective-permute-start.25 = (bf16[64,1024]{1,0:T(8,128)(2,1)S(1)}, bf16[64,1024]{1,0:T(8,128)(2,1)S(1)}, u32[]{:S(2)}, u32[]{:S(2)}) collective-permute-start(bf16[64,1024]{1,0:T(8,128)(2,1)S(1)} %get-tuple-element.31), channel_id=1, source_target_pairs={{4,0},{8,4},{12,8},{0,12},{5,1},{9,5},{13,9},{1,13},{6,2},{10,6},{... | collective-permute-start | bytes 393224 | tf_op jit(solution)/shard_map/slot4/ppermute | solution.py:306
  89.9 2.2 %copy-start.18 = (bf16[64,1024]{1,0:T(8,128)(2,1)}, bf16[64,1024]{1,0:T(8,128)(2,1)S(1)}, u32[]{:S(2)}) copy-start(bf16[64,1024]{1,0:T(8,128)(2,1)S(1)} %collective-permute-done.24.refs_3_) | copy-start | bytes 393220
  91.4 0.8 copy-start.19
  91.4 1.3 %collective-permute-start.26 = (bf16[256,256]{1,0:T(8,128)(2,1)S(1)}, bf16[256,256]{1,0:T(8,128)(2,1)S(1)}, u32[]{:S(2)}, u32[]{:S(2)}) collective-permute-start(bf16[256,256]{1,0:T(8,128)(2,1)S(1)} %add_convert_fusion.mine), channel_id=1, source_target_pairs={{0,1},{1,0},{2,3},{3,2},{4,5},{5,4},{6,7},{7,6},{8,9},{9,8},{10,11... | collective-permute-start | bytes 393224 | tf_op jit(solution)/shard_map/ppermute | solution.py:112
  95.3 9.2 %collective-permute-start.28 = (bf16[128,1024]{1,0:T(8,128)(2,1)S(1)}, bf16[128,1024]{1,0:T(8,128)(2,1)S(1)}, u32[]{:S(2)}, u32[]{:S(2)}) collective-permute-start(bf16[128,1024]{1,0:T(8,128)(2,1)S(1)} %get-tuple-element.35), channel_id=1, source_target_pairs={{0,2},{2,0},{1,3},{3,1},{4,6},{6,4},{5,7},{7,5},{8,10},{10,8},{9,1... | collective-permute-start | bytes 786440 | tf_op jit(solution)/shard_map/ppermute | solution.py:332
  95.8 13.0 %collective-permute-start.27 = (bf16[128,1024]{1,0:T(8,128)(2,1)S(1)}, bf16[128,1024]{1,0:T(8,128)(2,1)S(1)}, u32[]{:S(2)}, u32[]{:S(2)}) collective-permute-start(bf16[128,1024]{1,0:T(8,128)(2,1)S(1)} %get-tuple-element.34), channel_id=1, source_target_pairs={{0,16},{16,0},{1,17},{17,1},{2,18},{18,2},{3,19},{19,3},{4,20},{20... | collective-permute-start | bytes 786440 | tf_op jit(solution)/shard_map/ppermute | solution.py:333
  98.0 12.3 %collective-permute-start.29 = (bf16[128,1024]{1,0:T(8,128)(2,1)S(1)}, bf16[128,1024]{1,0:T(8,128)(2,1)S(1)}, u32[]{:S(2)}, u32[]{:S(2)}) collective-permute-start(bf16[128,1024]{1,0:T(8,128)(2,1)S(1)} %get-tuple-element.36), channel_id=1, source_target_pairs={{0,18},{18,0},{2,16},{16,2},{1,19},{19,1},{3,17},{17,3},{4,22},{22... | collective-permute-start | bytes 786440 | tf_op jit(solution)/shard_map/ppermute | solution.py:331
  104.5 5.8 %collective-permute-start.31 = (bf16[4,4096]{1,0:T(4,128)(2,1)S(1)}, bf16[4,4096]{1,0:T(4,128)(2,1)S(1)}, u32[]{:S(2)}, u32[]{:S(2)}) collective-permute-start(bf16[4,4096]{1,0:T(4,128)(2,1)S(1)} %convert_element_type.64.refs_0_), channel_id=1, source_target_pairs={{0,4},{4,8},{8,12},{12,0},{1,5},{5,9},{9,13},{13,1},{2,6},{6,10},{... | collective-permute-start | bytes 98312 | tf_op jit(solution)/shard_map/ppermute | solution.py:354
  105.1 5.3 %collective-permute-start.32 = (bf16[4,4096]{1,0:T(4,128)(2,1)S(1)}, bf16[4,4096]{1,0:T(4,128)(2,1)S(1)}, u32[]{:S(2)}, u32[]{:S(2)}) collective-permute-start(bf16[4,4096]{1,0:T(4,128)(2,1)S(1)} %convert_element_type.64.refs_0_), channel_id=1, source_target_pairs={{4,0},{8,4},{12,8},{0,12},{5,1},{9,5},{13,9},{1,13},{6,2},{10,6},{... | collective-permute-start | bytes 98312 | tf_op jit(solution)/shard_map/ppermute | solution.py:354
  108.3 4.8 %collective-permute-start.33 = (bf16[4,4096]{1,0:T(4,128)(2,1)S(1)}, bf16[4,4096]{1,0:T(4,128)(2,1)S(1)}, u32[]{:S(2)}, u32[]{:S(2)}) collective-permute-start(bf16[4,4096]{1,0:T(4,128)(2,1)S(1)} %convert_element_type.64.refs_0_), channel_id=1, source_target_pairs={{0,8},{8,0},{4,12},{12,4},{1,9},{9,1},{5,13},{13,5},{2,10},{10,2},... | collective-permute-start | bytes 98312 | tf_op jit(solution)/shard_map/ppermute | solution.py:354
  110.3 4.8 %copy-start.11 = (bf16[1,128,4096]{2,1,0:T(8,128)(2,1)}, bf16[1,128,4096]{2,1,0:T(8,128)(2,1)S(1)}, u32[]{:S(2)}) copy-start(bf16[1,128,4096]{2,1,0:T(8,128)(2,1)S(1)} %bitcast_dynamic-update-slice_fusion) | copy-start | bytes 3145732

commit v4 on v3

--- a/solution.py
+++ b/solution.py
@@ -102,8 +102,8 @@
     return (axis, PAIR) if axis != "both" else (("group", "section"), ACROSS)
 
 
-def summed(keep, send, gate1, gate2):
-    own = after((keep + lax.ppermute(send, "mp", PAIR)).astype(BF16), *gate1)
+def summed(keep, send, sent_as, gate1, gate2):
+    own = after((keep + lax.ppermute(send, "mp", PAIR)).astype(sent_as), *gate1)
     others = [lax.ppermute(own, *plane(a)) for a in ("both", "section", "group")]
     total = own.astype(F32)
     for other in others:
@@ -293,7 +293,7 @@
     g_own = piece(cotangent, x, y)
     g_other = lax.ppermute(piece(cotangent, x, 1 - y), "group", PAIR)
     slot2 = gathered(jnp.where(last, u_keep, v_other), "slot2")
-    u_keep, v_other, u_other = after2((u_keep, v_other, u_other), *slot2[1:3])
+    u_keep, v_other, u_other = after2((u_keep, v_other, u_other), *slot2[1:3], *slot1[3:])
     h = n // 2
     third, fourth = jnp.where(last, v_other, u_other), jnp.where(last, u_other, u_keep)
     both = jnp.concatenate([third[:h], fourth[:h], third[h:], fourth[h:]], 0)
@@ -319,12 +319,12 @@
     keep, send = kernel_call(
         first_kernel, "first", [(half_part, False)] * 2, [wide, weight, part_of], 10, flags, g_own, g_other, *slot1, *slot2
     )
-    mine1, other1 = summed(keep, send, slot3[1:2], slot3[3:])
+    mine1, other1 = summed(keep, send, F32, slot3[1:2], slot3[3:])
     adjoint1, keep, send = kernel_call(
         middle_kernel, "middle", [(shape_of, False), (half_part, False), (half_part, False)],
         [wide, rank_of, weight, weight, part_of], 20, flags, g_own, g_other, mine1, other1, *slot1, *slot2, *slot3,
     )
-    mine0, other0 = summed(keep, send, (), slot4[3:])
+    mine0, other0 = summed(keep, send, BF16, (), slot4[3:])
     here, to_x, to_xy, to_y = kernel_call(
         last_kernel, "last", [(send_of, True)] * 4, [wide, rank_of, weight, wide], 15, flags, adjoint1, mine0, other0, *slot4
     )

time: 116 us -> 122 us (1.052)
  waiting for transfers between devices: 50.2 us -> 57 us
  starting transfers between devices: 43.9 us -> 42.5 us
    ppermute x2, waiting for transfers between devices: 2.64 us -> 22.4 us  [gathered(): lax.ppermute(below[:half], 'dp', UP)]
    ppermute x1, waiting for transfers between devices: 6.8 us -> 0.01 us  [spread(): lax.ppermute(both, 'dp', UP)]
    ppermute x6, waiting for transfers between devices: 3.2 us -> 9.98 us  [summed(): lax.ppermute(own, *plane(a))]
    ppermute x1, waiting for transfers between devices: 7.66 us -> 1.99 us  [spread(): lax.ppermute(both, 'dp', DOWN)]
    ppermute x4, waiting for transfers between devices: 8.48 us -> 3.9 us  [gathered(): below, above = (lax.ppermute(w, 'dp', UP), lax.ppermute(w, 'dp', DOWN))]
    ppermute x1, waiting for transfers between devices: 3.43 us -> 0.01 us  [spread(): lax.ppermute(above[n:n + h], 'dp', DOWN)]
    ppermute x2, starting transfers between devices: 6.91 us -> 4.49 us  [gathered(): lax.ppermute(above[half:], 'dp', DOWN)]
    ppermute x1, starting transfers between devices: 2.47 us -> 0.9 us  [spread(): lax.ppermute(both, 'dp', DOWN)]
  transfers between devices with their start and end apart: 34 -> 34, of which waited for: 19 -> 18; matrix products, arithmetic and copies ran while one was open for 6% -> 6% of each run, Pallas kernels for 4% -> 4%
where the time goes in v4:
time: 122 us
  waiting for transfers between devices  57 us (47%)
  starting transfers between devices  42.5 us (35%)
  Pallas kernels  10.2 us (8%)
  local copies, waits for them, and re-layouts  6.64 us (5%)
  other arithmetic  2.76 us (2%)
  between operations  1.77 us (1%)
    ppermute x2, waiting for transfers between devices, gathered(): lax.ppermute(below[:half], 'dp', UP)  22.4 us
    ppermute x6, waiting for transfers between devices, summed(): lax.ppermute(own, *plane(a))  9.98 us
    ppermute x4, starting transfers between devices, gathered(): below, above = (lax.ppermute(w, 'dp', UP), lax.ppermute(w, 'dp', DOWN))  8.76 us
    pallas_call x3, Pallas kernels, kernel_call(): pl.pallas_call(body, name=name, out_shape=[o for o, _ in outs], in_specs=...  8.13 us
    ppermute x6, starting transfers between devices, summed(): lax.ppermute(own, *plane(a))  7.11 us
    ppermute x1, waiting for transfers between devices, spread(): from_x = lax.ppermute(to_x, *plane('section'))  4.86 us
    ppermute x2, starting transfers between devices, gathered(): lax.ppermute(above[half:], 'dp', DOWN)  4.49 us
    ppermute x3, starting transfers between devices, spread(): lax.ppermute(rows, 'dp', p)  4.31 us
  transfers between devices with their start and end apart: 34, of which 18 were waited for; matrix products, arithmetic and copies ran while one was open for 6% of the time, Pallas kernels for 4%

profile of v4, /device:TPU:0, one launch (start us, length us, event | category | flops | bytes accessed | tf_op | source)
XLA Modules:
  0.0 121.8 jit_solution(15797136394952218728)
XLA Ops:
  0.7 1.2 dynamic-slice_bitcast_fusion.1
  1.8 3.0 %collective-permute-start.5 = (bf16[128,1024]{1,0:T(8,128)(2,1)S(1)}, bf16[128,1024]{1,0:T(8,128)(2,1)S(1)}, u32[]{:S(2)}, u32[]{:S(2)}) collective-permute-start(bf16[128,1024]{1,0:T(8,128)(2,1)S(1)} %get-tuple-element.40), channel_id=1, source_target_pairs={{0,2},{2,0},{1,3},{3,1},{4,6},{6,4},{5,7},{7,5},{8,10},{10,8},{9,1... | collective-permute-start | bytes 786440 | tf_op jit(solution)/shard_map/ppermute | solution.py:291
  4.8 1.6 %collective-permute-start.1 = (bf16[128,1024]{1,0:T(8,128)(2,1)S(1)}, bf16[128,1024]{1,0:T(8,128)(2,1)S(1)}, u32[]{:S(2)}, u32[]{:S(2)}) collective-permute-start(bf16[128,1024]{1,0:T(8,128)(2,1)S(1)} %get-tuple-element.41.refs_0_), channel_id=1, source_target_pairs={{0,4},{4,8},{8,12},{12,0},{1,5},{5,9},{9,13},{13,1},{2,6},{6,10},{... | collective-permute-start | bytes 786440 | tf_op jit(solution)/shard_map/slot1/ppermute | solution.py:96
  6.4 2.2 %collective-permute-start.2 = (bf16[128,1024]{1,0:T(8,128)(2,1)S(1)}, bf16[128,1024]{1,0:T(8,128)(2,1)S(1)}, u32[]{:S(2)}, u32[]{:S(2)}) collective-permute-start(bf16[128,1024]{1,0:T(8,128)(2,1)S(1)} %get-tuple-element.41.refs_0_), channel_id=1, source_target_pairs={{4,0},{8,4},{12,8},{0,12},{5,1},{9,5},{13,9},{1,13},{6,2},{10,6},{... | collective-permute-start | bytes 786440 | tf_op jit(solution)/shard_map/slot1/ppermute | solution.py:96
  8.7 1.0 dynamic-slice_bitcast_fusion
  9.6 0.4 collective-permute-start.11
  10.0 1.3 %collective-permute-done.5 = bf16[128,1024]{1,0:T(8,128)(2,1)S(1)} collective-permute-done((bf16[128,1024]{1,0:T(8,128)(2,1)S(1)}, bf16[128,1024]{1,0:T(8,128)(2,1)S(1)}, u32[]{:S(2)}, u32[]{:S(2)}) %collective-permute-start.5) | collective-permute-done | bytes 262176 | tf_op jit(solution)/shard_map/ppermute | solution.py:291
  11.3 1.0 broadcast_select_fusion.2
  12.3 2.8 %collective-permute-start.6 = (bf16[128,1024]{1,0:T(8,128)(2,1)S(1)}, bf16[128,1024]{1,0:T(8,128)(2,1)S(1)}, u32[]{:S(2)}, u32[]{:S(2)}) collective-permute-start(bf16[128,1024]{1,0:T(8,128)(2,1)S(1)} %get-tuple-element.38.refs_5_), channel_id=1, source_target_pairs={{0,4},{4,8},{8,12},{12,0},{1,5},{5,9},{9,13},{13,1},{2,6},{6,10},{... | collective-permute-start | bytes 786440 | tf_op jit(solution)/shard_map/slot2/ppermute | solution.py:96
  15.2 2.1 %collective-permute-start.7 = (bf16[128,1024]{1,0:T(8,128)(2,1)S(1)}, bf16[128,1024]{1,0:T(8,128)(2,1)S(1)}, u32[]{:S(2)}, u32[]{:S(2)}) collective-permute-start(bf16[128,1024]{1,0:T(8,128)(2,1)S(1)} %get-tuple-element.38.refs_5_), channel_id=1, source_target_pairs={{4,0},{8,4},{12,8},{0,12},{5,1},{9,5},{13,9},{1,13},{6,2},{10,6},{... | collective-permute-start | bytes 786440 | tf_op jit(solution)/shard_map/slot2/ppermute | solution.py:96
  17.3 0.7 slice.52
  18.0 3.9 %collective-permute-done.2.refs_2_ = bf16[128,1024]{1,0:T(8,128)(2,1)S(1)} collective-permute-done((bf16[128,1024]{1,0:T(8,128)(2,1)S(1)}, bf16[128,1024]{1,0:T(8,128)(2,1)S(1)}, u32[]{:S(2)}, u32[]{:S(2)}) %collective-permute-start.2) | collective-permute-done | bytes 262176 | tf_op jit(solution)/shard_map/slot1/ppermute | solution.py:96
  21.9 1.3 %collective-permute-start.4 = (bf16[64,1024]{1,0:T(8,128)(2,1)S(1)}, bf16[64,1024]{1,0:T(8,128)(2,1)S(1)}, u32[]{:S(2)}, u32[]{:S(2)}) collective-permute-start(bf16[64,1024]{1,0:T(8,128)(2,1)S(1)} %slice.53), channel_id=1, source_target_pairs={{4,0},{8,4},{12,8},{0,12},{5,1},{9,5},{13,9},{1,13},{6,2},{10,6},{... | collective-permute-start | bytes 393224 | tf_op jit(solution)/shard_map/slot1/ppermute | solution.py:97
  23.2 1.9 %constant_dynamic-slice_fusion = (bf16[128,1024]{1,0:T(8,128)(2,1)}, bf16[128,1024]{1,0:T(8,128)(2,1)}) fusion(bf16[128,4096]{1,0:T(8,128)(2,1)} %param.9, s32[]{:T(128)S(6)} %select_n.75, s32[]{:T(128)S(6)} %select_n.74), kind=kLoop, calls=%fused_computation.46 | loop fusion | bytes 1048584 | tf_op jit(solution)/shard_map/dynamic_slice | solution.py:283
  25.1 1.6 %collective-permute-start = (bf16[128,1024]{1,0:T(8,128)(2,1)}, bf16[128,1024]{1,0:T(8,128)(2,1)}, u32[]{:S(2)}, u32[]{:S(2)}) collective-permute-start(bf16[128,1024]{1,0:T(8,128)(2,1)} %get-tuple-element.42), channel_id=1, source_target_pairs={{0,16},{16,0},{1,17},{17,1},{2,18},{18,2},{3,19},{19,3},{4,20},{20... | collective-permute-start | bytes 786440 | tf_op jit(solution)/shard_map/ppermute | solution.py:294
  26.6 9.0 %collective-permute-done.3.refs_3_ = bf16[64,1024]{1,0:T(8,128)(2,1)S(1)} collective-permute-done((bf16[64,1024]{1,0:T(8,128)(2,1)}, bf16[64,1024]{1,0:T(8,128)(2,1)S(1)}, u32[]{:S(2)}, u32[]{:S(2)}) %collective-permute-start.3) | collective-permute-done | bytes 131104 | tf_op jit(solution)/shard_map/slot1/ppermute | solution.py:97
  35.6 0.8 collective-permute-done.4.refs_4_
  36.4 1.2 broadcast_select_fusion.1
  37.7 1.2 collective-permute-start.12
  38.9 0.7 collective-permute-start.8
  39.7 3.2 %collective-permute-start.9 = (bf16[64,1024]{1,0:T(8,128)(2,1)S(1)}, bf16[64,1024]{1,0:T(8,128)(2,1)S(1)}, u32[]{:S(2)}, u32[]{:S(2)}) collective-permute-start(bf16[64,1024]{1,0:T(8,128)(2,1)S(1)} %slice.55), channel_id=1, source_target_pairs={{4,0},{8,4},{12,8},{0,12},{5,1},{9,5},{13,9},{1,13},{6,2},{10,6},{... | collective-permute-start | bytes 393224 | tf_op jit(solution)/shard_map/slot2/ppermute | solution.py:97
  42.9 0.9 collective-permute-start.17
  43.9 13.4 %collective-permute-done.8.refs_8_ = bf16[64,1024]{1,0:T(8,128)(2,1)S(1)} collective-permute-done((bf16[64,1024]{1,0:T(8,128)(2,1)S(1)}, bf16[64,1024]{1,0:T(8,128)(2,1)S(1)}, u32[]{:S(2)}, u32[]{:S(2)}) %collective-permute-start.8) | collective-permute-done | bytes 131104 | tf_op jit(solution)/shard_map/slot2/ppermute | solution.py:97
  57.3 1.2 %collective-permute-done.9.refs_9_ = bf16[64,1024]{1,0:T(8,128)(2,1)S(1)} collective-permute-done((bf16[64,1024]{1,0:T(8,128)(2,1)S(1)}, bf16[64,1024]{1,0:T(8,128)(2,1)S(1)}, u32[]{:S(2)}, u32[]{:S(2)}) %collective-permute-start.9) | collective-permute-done | bytes 131104 | tf_op jit(solution)/shard_map/slot2/ppermute | solution.py:97
  58.6 0.7 copy-done.17
  59.2 2.5 %first.1 = (f32[256,256]{1,0:T(8,128)S(1)}, f32[256,256]{1,0:T(8,128)S(1)}) custom-call(s32[3]{0:T(128)S(1)} %pad_add_fusion.flags, bf16[128,1024]{1,0:T(8,128)(2,1)} %get-tuple-element.43.g_own, bf16[128,1024]{1,0:T(8,128)(2,1)} %collective-permute-done.g_other, bf16[128,1024]{1,0:T(8,128)(2,1)} %copy-done.5, bf16[128,1024]{1,0:T(8,128)(2,1)} %copy-done.7, ...), custom_call_target="tpu_custom_call" | custom-call | tf_op jit(solution)/shard_map/first/pallas_call | solution.py:265
  61.8 1.5 %collective-permute-done.10 = f32[256,256]{1,0:T(8,128)S(1)} collective-permute-done((f32[256,256]{1,0:T(8,128)S(1)}, f32[256,256]{1,0:T(8,128)S(1)}, u32[]{:S(2)}, u32[]{:S(2)}) %collective-permute-start.10) | collective-permute-done | bytes 262176 | tf_op jit(solution)/shard_map/ppermute | solution.py:106
  63.4 1.6 %collective-permute-start.13 = (f32[256,256]{1,0:T(8,128)S(1)}, f32[256,256]{1,0:T(8,128)S(1)}, u32[]{:S(2)}, u32[]{:S(2)}) collective-permute-start(f32[256,256]{1,0:T(8,128)S(1)} %add.94), channel_id=1, source_target_pairs={{0,18},{18,0},{2,16},{16,2},{1,19},{19,1},{3,17},{17,3},{4,22},{22... | collective-permute-start | bytes 786440 | tf_op jit(solution)/shard_map/ppermute | solution.py:107
  64.9 1.5 %collective-permute-start.14 = (f32[256,256]{1,0:T(8,128)S(1)}, f32[256,256]{1,0:T(8,128)S(1)}, u32[]{:S(2)}, u32[]{:S(2)}) collective-permute-start(f32[256,256]{1,0:T(8,128)S(1)} %add.94), channel_id=1, source_target_pairs={{0,2},{2,0},{1,3},{3,1},{4,6},{6,4},{5,7},{7,5},{8,10},{10,8},{9,1... | collective-permute-start | bytes 786440 | tf_op jit(solution)/shard_map/ppermute | solution.py:107
  66.4 0.5 collective-permute-start.15
  66.9 0.6 collective-permute-start.16
  67.5 2.0 %collective-permute-done.17.refs_12_.refs_2_ = bf16[256,1024]{1,0:T(8,128)(2,1)S(1)} collective-permute-done((bf16[256,1024]{1,0:T(8,128)(2,1)S(1)}, bf16[256,1024]{1,0:T(8,128)(2,1)S(1)}, u32[]{:S(2)}, u32[]{:S(2)}) %collective-permute-start.17) | collective-permute-done | bytes 524320 | tf_op jit(solution)/shard_map/slot34/ppermute | solution.py:301
  69.5 2.1 %collective-permute-start.18 = (bf16[64,1024]{1,0:T(8,128)(2,1)S(1)}, bf16[64,1024]{1,0:T(8,128)(2,1)S(1)}, u32[]{:S(2)}, u32[]{:S(2)}) collective-permute-start(bf16[64,1024]{1,0:T(8,128)(2,1)S(1)} %get-tuple-element.45), channel_id=1, source_target_pairs={{4,0},{8,4},{12,8},{0,12},{5,1},{9,5},{13,9},{1,13},{6,2},{10,6},{... | collective-permute-start | bytes 393224 | tf_op jit(solution)/shard_map/slot3/ppermute | solution.py:303
  71.7 1.9 %collective-permute-done.13 = f32[256,256]{1,0:T(8,128)S(1)} collective-permute-done((f32[256,256]{1,0:T(8,128)S(1)}, f32[256,256]{1,0:T(8,128)S(1)}, u32[]{:S(2)}, u32[]{:S(2)}) %collective-permute-start.13) | collective-permute-done | bytes 262176 | tf_op jit(solution)/shard_map/ppermute | solution.py:107
  73.5 4.9 %collective-permute-done.14 = f32[256,256]{1,0:T(8,128)S(1)} collective-permute-done((f32[256,256]{1,0:T(8,128)S(1)}, f32[256,256]{1,0:T(8,128)S(1)}, u32[]{:S(2)}, u32[]{:S(2)}) %collective-permute-start.14) | collective-permute-done | bytes 262176 | tf_op jit(solution)/shard_map/ppermute | solution.py:107
  78.6 1.3 %collective-permute-done.19.other = bf16[256,256]{1,0:T(8,128)(2,1)S(1)} collective-permute-done((bf16[256,256]{1,0:T(8,128)(2,1)S(1)}, bf16[256,256]{1,0:T(8,128)(2,1)S(1)}, u32[]{:S(2)}, u32[]{:S(2)}) %collective-permute-start.19) | collective-permute-done | bytes 131104 | tf_op jit(solution)/shard_map/ppermute | solution.py:112
  79.9 3.1 %middle.1 = (bf16[256,1024]{1,0:T(8,128)(2,1)S(1)}, f32[256,256]{1,0:T(8,128)S(1)}, f32[256,256]{1,0:T(8,128)S(1)}) custom-call(s32[3]{0:T(128)S(1)} %pad_add_fusion.flags, bf16[128,1024]{1,0:T(8,128)(2,1)} %get-tuple-element.43.g_own, bf16[128,1024]{1,0:T(8,128)(2,1)} %collective-permute-done.g_other, bf16[256,256]{1,0:T(8,128)(2,1)S(1)} %add_convert_fusion.2.mine, ...), custom_call_target="tpu_custom_call" | custom-call | tf_op jit(solution)/shard_map/middle/pallas_call | solution.py:265
  83.1 0.2 collective-permute-start.20
  83.3 0.5 fusion.1
  83.9 0.4 collective-permute-start.30
  84.2 0.7 copy-done.23
  85.1 1.4 %collective-permute-start.21 = (bf16[256,256]{1,0:T(8,128)(2,1)S(1)}, bf16[256,256]{1,0:T(8,128)(2,1)S(1)}, u32[]{:S(2)}, u32[]{:S(2)}) collective-permute-start(bf16[256,256]{1,0:T(8,128)(2,1)S(1)} %add_convert_fusion.1), channel_id=1, source_target_pairs={{0,18},{18,0},{2,16},{16,2},{1,19},{19,1},{3,17},{17,3},{4,22},{22... | collective-permute-start | bytes 393224 | tf_op jit(solution)/shard_map/ppermute | solution.py:107
  86.6 1.5 %collective-permute-start.22 = (bf16[256,256]{1,0:T(8,128)(2,1)S(1)}, bf16[256,256]{1,0:T(8,128)(2,1)S(1)}, u32[]{:S(2)}, u32[]{:S(2)}) collective-permute-start(bf16[256,256]{1,0:T(8,128)(2,1)S(1)} %add_convert_fusion.1), channel_id=1, source_target_pairs={{0,2},{2,0},{1,3},{3,1},{4,6},{6,4},{5,7},{7,5},{8,10},{10,8},{9,1... | collective-permute-start | bytes 393224 | tf_op jit(solution)/shard_map/ppermute | solution.py:107
  88.1 0.6 collective-permute-start.23
  88.7 0.5 collective-permute-start.24
  89.2 3.2 %collective-permute-done.21 = bf16[256,256]{1,0:T(8,128)(2,1)S(1)} collective-permute-done((bf16[256,256]{1,0:T(8,128)(2,1)S(1)}, bf16[256,256]{1,0:T(8,128)(2,1)S(1)}, u32[]{:S(2)}, u32[]{:S(2)}) %collective-permute-start.21) | collective-permute-done | bytes 131104 | tf_op jit(solution)/shard_map/ppermute | solution.py:107
  92.4 2.6 %collective-permute-start.25 = (bf16[64,1024]{1,0:T(8,128)(2,1)S(1)}, bf16[64,1024]{1,0:T(8,128)(2,1)S(1)}, u32[]{:S(2)}, u32[]{:S(2)}) collective-permute-start(bf16[64,1024]{1,0:T(8,128)(2,1)S(1)} %get-tuple-element.31), channel_id=1, source_target_pairs={{4,0},{8,4},{12,8},{0,12},{5,1},{9,5},{13,9},{1,13},{6,2},{10,6},{... | collective-permute-start | bytes 393224 | tf_op jit(solution)/shard_map/slot4/ppermute | solution.py:306
  95.1 0.8 collective-permute-done.24.refs_3_
  95.8 2.2 %collective-permute-done.25.refs_4_ = bf16[64,1024]{1,0:T(8,128)(2,1)S(1)} collective-permute-done((bf16[64,1024]{1,0:T(8,128)(2,1)S(1)}, bf16[64,1024]{1,0:T(8,128)(2,1)S(1)}, u32[]{:S(2)}, u32[]{:S(2)}) %collective-permute-start.25) | collective-permute-done | bytes 131104 | tf_op jit(solution)/shard_map/slot4/ppermute | solution.py:306
  98.8 0.6 collective-permute-done.26.other
  99.3 2.5 %last.1 = (bf16[128,1024]{1,0:T(8,128)(2,1)S(1)}, bf16[128,1024]{1,0:T(8,128)(2,1)S(1)}, bf16[128,1024]{1,0:T(8,128)(2,1)S(1)}, bf16[128,1024]{1,0:T(8,128)(2,1)S(1)}) custom-call(s32[3]{0:T(128)S(1)} %pad_add_fusion.flags, bf16[256,1024]{1,0:T(8,128)(2,1)} %copy-done.1, bf16[256,256]{1,0:T(8,128)(2,1)S(1)} %add_convert_fusion.mine, ...), custom_call_target="tpu_custom_call" | custom-call | tf_op jit(solution)/shard_map/last/pallas_call | solution.py:265
  101.9 0.6 collective-permute-start.28
  102.5 1.4 %collective-permute-start.27 = (bf16[128,1024]{1,0:T(8,128)(2,1)S(1)}, bf16[128,1024]{1,0:T(8,128)(2,1)S(1)}, u32[]{:S(2)}, u32[]{:S(2)}) collective-permute-start(bf16[128,1024]{1,0:T(8,128)(2,1)S(1)} %get-tuple-element.34), channel_id=1, source_target_pairs={{0,16},{16,0},{1,17},{17,1},{2,18},{18,2},{3,19},{19,3},{4,20},{20... | collective-permute-start | bytes 786440 | tf_op jit(solution)/shard_map/ppermute | solution.py:333
  103.9 0.2 fusion.4
  104.1 0.3 fusion
  104.4 0.1 convert_element_type.44.refs_0_
  104.5 1.6 %collective-permute-start.29 = (bf16[128,1024]{1,0:T(8,128)(2,1)S(1)}, bf16[128,1024]{1,0:T(8,128)(2,1)S(1)}, u32[]{:S(2)}, u32[]{:S(2)}) collective-permute-start(bf16[128,1024]{1,0:T(8,128)(2,1)S(1)} %get-tuple-element.36), channel_id=1, source_target_pairs={{0,18},{18,0},{2,16},{16,2},{1,19},{19,1},{3,17},{17,3},{4,22},{22... | collective-permute-start | bytes 786440 | tf_op jit(solution)/shard_map/ppermute | solution.py:331
  106.2 4.9 %collective-permute-done.28 = bf16[128,1024]{1,0:T(8,128)(2,1)S(1)} collective-permute-done((bf16[128,1024]{1,0:T(8,128)(2,1)S(1)}, bf16[128,1024]{1,0:T(8,128)(2,1)S(1)}, u32[]{:S(2)}, u32[]{:S(2)}) %collective-permute-start.28) | collective-permute-done | bytes 262176 | tf_op jit(solution)/shard_map/ppermute | solution.py:332
  111.1 0.7 collective-permute-start.31
  111.8 3.1 %collective-permute-start.32 = (bf16[4,4096]{1,0:T(4,128)(2,1)S(1)}, bf16[4,4096]{1,0:T(4,128)(2,1)S(1)}, u32[]{:S(2)}, u32[]{:S(2)}) collective-permute-start(bf16[4,4096]{1,0:T(4,128)(2,1)S(1)} %convert_element_type.44.refs_0_), channel_id=1, source_target_pairs={{4,0},{8,4},{12,8},{0,12},{5,1},{9,5},{13,9},{1,13},{6,2},{10,6},{... | collective-permute-start | bytes 98312 | tf_op jit(solution)/shard_map/ppermute | solution.py:354
  114.9 0.5 collective-permute-start.33
  115.5 1.3 %collective-permute-done.29 = bf16[128,1024]{1,0:T(8,128)(2,1)S(1)} collective-permute-done((bf16[128,1024]{1,0:T(8,128)(2,1)S(1)}, bf16[128,1024]{1,0:T(8,128)(2,1)S(1)}, u32[]{:S(2)}, u32[]{:S(2)}) %collective-permute-start.29) | collective-permute-done | bytes 262176 | tf_op jit(solution)/shard_map/ppermute | solution.py:331
  116.8 2.9 %collective-permute-done.33.refs_3_ = bf16[4,4096]{1,0:T(4,128)(2,1)S(1)} collective-permute-done((bf16[4,4096]{1,0:T(4,128)(2,1)S(1)}, bf16[4,4096]{1,0:T(4,128)(2,1)S(1)}, u32[]{:S(2)}, u32[]{:S(2)}) %collective-permute-start.33) | collective-permute-done | bytes 32800 | tf_op jit(solution)/shard_map/ppermute | solution.py:354
  119.7 2.0 %scores.1 = f32[1,16]{1,0:T(1,128)} custom-call(f32[1]{0:T(128)S(6)} %mul.57.shift, bf16[4,4096]{1,0:T(4,128)(2,1)S(1)} %convert_element_type.44.refs_0_, bf16[4,4096]{1,0:T(4,128)(2,1)S(1)} %collective-permute-done.31.refs_1_, bf16[4,4096]{1,0:T(4,128)(2,1)S(1)} %collective-permute-done.32.refs_2_, bf16[4,4096]{1,0:T(4,128)(2,1)S(1)} %collective-permute-done.33.refs_3_), custom_call_target="tpu_custom_call" | custom-call | tf_op jit(solution)/shard_map/scores/pallas_call | solution.py:252
  (89 shorter events, 1.2 us)
Async XLA Ops:
  0.6 82.7 %copy-start = (bf16[1,128,4096]{2,1,0:T(8,128)(2,1)S(1)}, bf16[1,128,4096]{2,1,0:T(8,128)(2,1)}, u32[]{:S(2)}) copy-start(bf16[1,128,4096]{2,1,0:T(8,128)(2,1)} %param.8) | copy-start | bytes 3145732
  1.8 7.8 %copy-start.5 = (bf16[128,1024]{1,0:T(8,128)(2,1)}, bf16[128,1024]{1,0:T(8,128)(2,1)S(1)}, u32[]{:S(2)}) copy-start(bf16[128,1024]{1,0:T(8,128)(2,1)S(1)} %get-tuple-element.41.refs_0_) | copy-start | bytes 786436
  1.8 9.5 %collective-permute-start.5 = (bf16[128,1024]{1,0:T(8,128)(2,1)S(1)}, bf16[128,1024]{1,0:T(8,128)(2,1)S(1)}, u32[]{:S(2)}, u32[]{:S(2)}) collective-permute-start(bf16[128,1024]{1,0:T(8,128)(2,1)S(1)} %get-tuple-element.40), channel_id=1, source_target_pairs={{0,2},{2,0},{1,3},{3,1},{4,6},{6,4},{5,7},{7,5},{8,10},{10,8},{9,1... | collective-permute-start | bytes 786440 | tf_op jit(solution)/shard_map/ppermute | solution.py:291
  4.8 12.5 %collective-permute-start.1 = (bf16[128,1024]{1,0:T(8,128)(2,1)S(1)}, bf16[128,1024]{1,0:T(8,128)(2,1)S(1)}, u32[]{:S(2)}, u32[]{:S(2)}) collective-permute-start(bf16[128,1024]{1,0:T(8,128)(2,1)S(1)} %get-tuple-element.41.refs_0_), channel_id=1, source_target_pairs={{0,4},{4,8},{8,12},{12,0},{1,5},{5,9},{9,13},{13,1},{2,6},{6,10},{... | collective-permute-start | bytes 786440 | tf_op jit(solution)/shard_map/slot1/ppermute | solution.py:96
  6.4 15.5 %collective-permute-start.2 = (bf16[128,1024]{1,0:T(8,128)(2,1)S(1)}, bf16[128,1024]{1,0:T(8,128)(2,1)S(1)}, u32[]{:S(2)}, u32[]{:S(2)}) collective-permute-start(bf16[128,1024]{1,0:T(8,128)(2,1)S(1)} %get-tuple-element.41.refs_0_), channel_id=1, source_target_pairs={{4,0},{8,4},{12,8},{0,12},{5,1},{9,5},{13,9},{1,13},{6,2},{10,6},{... | collective-permute-start | bytes 786440 | tf_op jit(solution)/shard_map/slot1/ppermute | solution.py:96
  9.6 15.5 %collective-permute-start.11 = (bf16[128,1024]{1,0:T(8,128)(2,1)S(1)}, bf16[128,1024]{1,0:T(8,128)(2,1)}, u32[]{:S(2)}, u32[]{:S(2)}) collective-permute-start(bf16[128,1024]{1,0:T(8,128)(2,1)S(1)} %dynamic-slice_bitcast_fusion), channel_id=1, source_target_pairs={{0,2},{2,0},{1,3},{3,1},{4,6},{6,4},{5,7},{7,5},{8,10},{10,8},{9,1... | collective-permute-start | bytes 786440 | tf_op jit(solution)/shard_map/ppermute | solution.py:292
  12.3 9.6 %copy-start.6 = (bf16[128,1024]{1,0:T(8,128)(2,1)}, bf16[128,1024]{1,0:T(8,128)(2,1)S(1)}, u32[]{:S(2)}) copy-start(bf16[128,1024]{1,0:T(8,128)(2,1)S(1)} %get-tuple-element.38.refs_5_) | copy-start | bytes 786436
  12.3 24.0 %collective-permute-start.6 = (bf16[128,1024]{1,0:T(8,128)(2,1)S(1)}, bf16[128,1024]{1,0:T(8,128)(2,1)S(1)}, u32[]{:S(2)}, u32[]{:S(2)}) collective-permute-start(bf16[128,1024]{1,0:T(8,128)(2,1)S(1)} %get-tuple-element.38.refs_5_), channel_id=1, source_target_pairs={{0,4},{4,8},{8,12},{12,0},{1,5},{5,9},{9,13},{13,1},{2,6},{6,10},{... | collective-permute-start | bytes 786440 | tf_op jit(solution)/shard_map/slot2/ppermute | solution.py:96
  15.2 21.2 %collective-permute-start.7 = (bf16[128,1024]{1,0:T(8,128)(2,1)S(1)}, bf16[128,1024]{1,0:T(8,128)(2,1)S(1)}, u32[]{:S(2)}, u32[]{:S(2)}) collective-permute-start(bf16[128,1024]{1,0:T(8,128)(2,1)S(1)} %get-tuple-element.38.refs_5_), channel_id=1, source_target_pairs={{4,0},{8,4},{12,8},{0,12},{5,1},{9,5},{13,9},{1,13},{6,2},{10,6},{... | collective-permute-start | bytes 786440 | tf_op jit(solution)/shard_map/slot2/ppermute | solution.py:96
  17.3 4.6 %copy-start.7 = (bf16[128,1024]{1,0:T(8,128)(2,1)}, bf16[128,1024]{1,0:T(8,128)(2,1)S(1)}, u32[]{:S(2)}) copy-start(bf16[128,1024]{1,0:T(8,128)(2,1)S(1)} %collective-permute-done.1.refs_1_) | copy-start | bytes 786436
  18.0 17.6 %collective-permute-start.3 = (bf16[64,1024]{1,0:T(8,128)(2,1)}, bf16[64,1024]{1,0:T(8,128)(2,1)S(1)}, u32[]{:S(2)}, u32[]{:S(2)}) collective-permute-start(bf16[64,1024]{1,0:T(8,128)(2,1)} %slice.52), channel_id=1, source_target_pairs={{0,4},{4,8},{8,12},{12,0},{1,5},{5,9},{9,13},{13,1},{2,6},{6,10},{... | collective-permute-start | bytes 393224 | tf_op jit(solution)/shard_map/slot1/ppermute | solution.py:97
  21.9 3.2 %copy-start.8 = (bf16[128,1024]{1,0:T(8,128)(2,1)}, bf16[128,1024]{1,0:T(8,128)(2,1)S(1)}, u32[]{:S(2)}) copy-start(bf16[128,1024]{1,0:T(8,128)(2,1)S(1)} %collective-permute-done.2.refs_2_) | copy-start | bytes 786436
  21.9 14.4 %collective-permute-start.4 = (bf16[64,1024]{1,0:T(8,128)(2,1)S(1)}, bf16[64,1024]{1,0:T(8,128)(2,1)S(1)}, u32[]{:S(2)}, u32[]{:S(2)}) collective-permute-start(bf16[64,1024]{1,0:T(8,128)(2,1)S(1)} %slice.53), channel_id=1, source_target_pairs={{4,0},{8,4},{12,8},{0,12},{5,1},{9,5},{13,9},{1,13},{6,2},{10,6},{... | collective-permute-start | bytes 393224 | tf_op jit(solution)/shard_map/slot1/ppermute | solution.py:97
  25.1 18.8 %collective-permute-start = (bf16[128,1024]{1,0:T(8,128)(2,1)}, bf16[128,1024]{1,0:T(8,128)(2,1)}, u32[]{:S(2)}, u32[]{:S(2)}) collective-permute-start(bf16[128,1024]{1,0:T(8,128)(2,1)} %get-tuple-element.42), channel_id=1, source_target_pairs={{0,16},{16,0},{1,17},{17,1},{2,18},{18,2},{3,19},{19,3},{4,20},{20... | collective-permute-start | bytes 786440 | tf_op jit(solution)/shard_map/ppermute | solution.py:294
  35.6 2.0 %copy-start.14 = (bf16[64,1024]{1,0:T(8,128)(2,1)}, bf16[64,1024]{1,0:T(8,128)(2,1)S(1)}, u32[]{:S(2)}) copy-start(bf16[64,1024]{1,0:T(8,128)(2,1)S(1)} %collective-permute-done.3.refs_3_) | copy-start | bytes 393220
  36.4 1.2 %copy-start.15 = (bf16[64,1024]{1,0:T(8,128)(2,1)}, bf16[64,1024]{1,0:T(8,128)(2,1)S(1)}, u32[]{:S(2)}) copy-start(bf16[64,1024]{1,0:T(8,128)(2,1)S(1)} %collective-permute-done.4.refs_4_) | copy-start | bytes 393220
  36.4 2.5 %copy-start.9 = (bf16[128,1024]{1,0:T(8,128)(2,1)}, bf16[128,1024]{1,0:T(8,128)(2,1)S(1)}, u32[]{:S(2)}) copy-start(bf16[128,1024]{1,0:T(8,128)(2,1)S(1)} %collective-permute-done.6.refs_6_) | copy-start | bytes 786436
  36.4 1.2 %copy-start.10 = (bf16[128,1024]{1,0:T(8,128)(2,1)}, bf16[128,1024]{1,0:T(8,128)(2,1)S(1)}, u32[]{:S(2)}) copy-start(bf16[128,1024]{1,0:T(8,128)(2,1)S(1)} %collective-permute-done.7.refs_7_) | copy-start | bytes 786436
  37.7 24.0 %copy-start.2 = (bf16[256,1024]{1,0:T(8,128)(2,1)}, bf16[256,1024]{1,0:T(8,128)(2,1)S(1)}, u32[]{:S(2)}) copy-start(bf16[256,1024]{1,0:T(8,128)(2,1)S(1)} %pad_maximum_fusion.refs_10_.refs_0_) | copy-start | bytes 1572868
  37.7 1.9 %copy-start.11 = (bf16[128,1024]{1,0:T(8,128)(2,1)S(1)}, bf16[128,1024]{1,0:T(8,128)(2,1)}, u32[]{:S(2)}) copy-start(bf16[128,1024]{1,0:T(8,128)(2,1)} %copy-done.10) | copy-start | bytes 786436
  37.7 25.6 %collective-permute-start.12 = (bf16[256,1024]{1,0:T(8,128)(2,1)S(1)}, bf16[256,1024]{1,0:T(8,128)(2,1)S(1)}, u32[]{:S(2)}, u32[]{:S(2)}) collective-permute-start(bf16[256,1024]{1,0:T(8,128)(2,1)S(1)} %pad_maximum_fusion.refs_10_.refs_0_), channel_id=1, source_target_pairs={{0,4},{4,8},{8,12},{12,0},{1,5},{5,9},{9,13},{13,1},{2,6},{6,10},{... | collective-permute-start | bytes 1572872 | tf_op jit(solution)/shard_map/slot34/ppermute | solution.py:301
  38.9 18.4 %collective-permute-start.8 = (bf16[64,1024]{1,0:T(8,128)(2,1)S(1)}, bf16[64,1024]{1,0:T(8,128)(2,1)S(1)}, u32[]{:S(2)}, u32[]{:S(2)}) collective-permute-start(bf16[64,1024]{1,0:T(8,128)(2,1)S(1)} %slice.54), channel_id=1, source_target_pairs={{0,4},{4,8},{8,12},{12,0},{1,5},{5,9},{9,13},{13,1},{2,6},{6,10},{... | collective-permute-start | bytes 393224 | tf_op jit(solution)/shard_map/slot2/ppermute | solution.py:97
  39.7 18.9 %collective-permute-start.9 = (bf16[64,1024]{1,0:T(8,128)(2,1)S(1)}, bf16[64,1024]{1,0:T(8,128)(2,1)S(1)}, u32[]{:S(2)}, u32[]{:S(2)}) collective-permute-start(bf16[64,1024]{1,0:T(8,128)(2,1)S(1)} %slice.55), channel_id=1, source_target_pairs={{4,0},{8,4},{12,8},{0,12},{5,1},{9,5},{13,9},{1,13},{6,2},{10,6},{... | collective-permute-start | bytes 393224 | tf_op jit(solution)/shard_map/slot2/ppermute | solution.py:97
  42.9 26.6 %collective-permute-start.17 = (bf16[256,1024]{1,0:T(8,128)(2,1)S(1)}, bf16[256,1024]{1,0:T(8,128)(2,1)S(1)}, u32[]{:S(2)}, u32[]{:S(2)}) collective-permute-start(bf16[256,1024]{1,0:T(8,128)(2,1)S(1)} %pad_maximum_fusion.refs_10_.refs_0_), channel_id=1, source_target_pairs={{4,0},{8,4},{12,8},{0,12},{5,1},{9,5},{13,9},{1,13},{6,2},{10,6},{... | collective-permute-start | bytes 1572872 | tf_op jit(solution)/shard_map/slot34/ppermute | solution.py:301
  57.3 1.3 %copy-start.16 = (bf16[64,1024]{1,0:T(8,128)(2,1)}, bf16[64,1024]{1,0:T(8,128)(2,1)S(1)}, u32[]{:S(2)}) copy-start(bf16[64,1024]{1,0:T(8,128)(2,1)S(1)} %collective-permute-done.8.refs_8_) | copy-start | bytes 393220
  58.6 0.7 copy-start.17
  61.7 1.6 %collective-permute-start.10 = (f32[256,256]{1,0:T(8,128)S(1)}, f32[256,256]{1,0:T(8,128)S(1)}, u32[]{:S(2)}, u32[]{:S(2)}) collective-permute-start(f32[256,256]{1,0:T(8,128)S(1)} %get-tuple-element.21), channel_id=1, source_target_pairs={{0,1},{1,0},{2,3},{3,2},{4,5},{5,4},{6,7},{7,6},{8,9},{9,8},{10,11... | collective-permute-start | bytes 786440 | tf_op jit(solution)/shard_map/ppermute | solution.py:106
  63.4 6.2 %copy-start.3 = (bf16[256,1024]{1,0:T(8,128)(2,1)}, bf16[256,1024]{1,0:T(8,128)(2,1)S(1)}, u32[]{:S(2)}) copy-start(bf16[256,1024]{1,0:T(8,128)(2,1)S(1)} %collective-permute-done.12.refs_11_.refs_1_) | copy-start | bytes 1572868
  63.4 10.2 %collective-permute-start.13 = (f32[256,256]{1,0:T(8,128)S(1)}, f32[256,256]{1,0:T(8,128)S(1)}, u32[]{:S(2)}, u32[]{:S(2)}) collective-permute-start(f32[256,256]{1,0:T(8,128)S(1)} %add.94), channel_id=1, source_target_pairs={{0,18},{18,0},{2,16},{16,2},{1,19},{19,1},{3,17},{17,3},{4,22},{22... | collective-permute-start | bytes 786440 | tf_op jit(solution)/shard_map/ppermute | solution.py:107
  64.9 13.5 %collective-permute-start.14 = (f32[256,256]{1,0:T(8,128)S(1)}, f32[256,256]{1,0:T(8,128)S(1)}, u32[]{:S(2)}, u32[]{:S(2)}) collective-permute-start(f32[256,256]{1,0:T(8,128)S(1)} %add.94), channel_id=1, source_target_pairs={{0,2},{2,0},{1,3},{3,1},{4,6},{6,4},{5,7},{7,5},{8,10},{10,8},{9,1... | collective-permute-start | bytes 786440 | tf_op jit(solution)/shard_map/ppermute | solution.py:107
  66.4 12.0 %collective-permute-start.15 = (f32[256,256]{1,0:T(8,128)S(1)}, f32[256,256]{1,0:T(8,128)S(1)}, u32[]{:S(2)}, u32[]{:S(2)}) collective-permute-start(f32[256,256]{1,0:T(8,128)S(1)} %add.94), channel_id=1, source_target_pairs={{0,16},{16,0},{1,17},{17,1},{2,18},{18,2},{3,19},{19,3},{4,20},{20... | collective-permute-start | bytes 786440 | tf_op jit(solution)/shard_map/ppermute | solution.py:107
  66.9 11.6 %collective-permute-start.16 = (bf16[64,1024]{1,0:T(8,128)(2,1)S(1)}, bf16[64,1024]{1,0:T(8,128)(2,1)S(1)}, u32[]{:S(2)}, u32[]{:S(2)}) collective-permute-start(bf16[64,1024]{1,0:T(8,128)(2,1)S(1)} %get-tuple-element.47), channel_id=1, source_target_pairs={{0,4},{4,8},{8,12},{12,0},{1,5},{5,9},{9,13},{13,1},{2,6},{6,10},{... | collective-permute-start | bytes 393224 | tf_op jit(solution)/shard_map/slot3/ppermute | solution.py:303
  69.5 9.0 %copy-start.4 = (bf16[256,1024]{1,0:T(8,128)(2,1)}, bf16[256,1024]{1,0:T(8,128)(2,1)S(1)}, u32[]{:S(2)}) copy-start(bf16[256,1024]{1,0:T(8,128)(2,1)S(1)} %collective-permute-done.17.refs_12_.refs_2_) | copy-start | bytes 1572868
  69.5 9.0 %collective-permute-start.18 = (bf16[64,1024]{1,0:T(8,128)(2,1)S(1)}, bf16[64,1024]{1,0:T(8,128)(2,1)S(1)}, u32[]{:S(2)}, u32[]{:S(2)}) collective-permute-start(bf16[64,1024]{1,0:T(8,128)(2,1)S(1)} %get-tuple-element.45), channel_id=1, source_target_pairs={{4,0},{8,4},{12,8},{0,12},{5,1},{9,5},{13,9},{1,13},{6,2},{10,6},{... | collective-permute-start | bytes 393224 | tf_op jit(solution)/shard_map/slot3/ppermute | solution.py:303
  78.5 4.8 %copy-start.13 = (bf16[1,64,4096]{2,1,0:T(8,128)(2,1)S(1)}, bf16[1,64,4096]{2,1,0:T(8,128)(2,1)}, u32[]{:S(2)}) copy-start(bf16[1,64,4096]{2,1,0:T(8,128)(2,1)} %param.12) | copy-start | bytes 1572868
  78.5 1.4 %copy-start.20 = (bf16[64,1024]{1,0:T(8,128)(2,1)}, bf16[64,1024]{1,0:T(8,128)(2,1)S(1)}, u32[]{:S(2)}) copy-start(bf16[64,1024]{1,0:T(8,128)(2,1)S(1)} %collective-permute-done.16.refs_13_) | copy-start | bytes 393220
  78.5 1.4 %copy-start.21 = (bf16[64,1024]{1,0:T(8,128)(2,1)}, bf16[64,1024]{1,0:T(8,128)(2,1)S(1)}, u32[]{:S(2)}) copy-start(bf16[64,1024]{1,0:T(8,128)(2,1)S(1)} %collective-permute-done.18.refs_14_) | copy-start | bytes 393220
  78.5 1.4 %collective-permute-start.19 = (bf16[256,256]{1,0:T(8,128)(2,1)S(1)}, bf16[256,256]{1,0:T(8,128)(2,1)S(1)}, u32[]{:S(2)}, u32[]{:S(2)}) collective-permute-start(bf16[256,256]{1,0:T(8,128)(2,1)S(1)} %add_convert_fusion.2.mine), channel_id=1, source_target_pairs={{0,1},{1,0},{2,3},{3,2},{4,5},{5,4},{6,7},{7,6},{8,9},{9,8},{10,11... | collective-permute-start | bytes 393224 | tf_op jit(solution)/shard_map/ppermute | solution.py:112
  83.1 0.8 copy-start.1
  83.1 2.0 %collective-permute-start.20 = (f32[256,256]{1,0:T(8,128)S(1)}, f32[256,256]{1,0:T(8,128)S(1)}, u32[]{:S(2)}, u32[]{:S(2)}) collective-permute-start(f32[256,256]{1,0:T(8,128)S(1)} %get-tuple-element.29), channel_id=1, source_target_pairs={{0,1},{1,0},{2,3},{3,2},{4,5},{5,4},{6,7},{7,6},{8,9},{9,8},{10,11... | collective-permute-start | bytes 786440 | tf_op jit(solution)/shard_map/ppermute | solution.py:106
  83.9 20.2 %collective-permute-start.30 = (f32[128,64]{0,1:T(8,128)S(1)}, f32[128,64]{0,1:T(8,128)S(1)}, u32[]{:S(2)}, u32[]{:S(2)}) collective-permute-start(f32[128,64]{0,1:T(8,128)S(1)} %fusion.1), channel_id=1, source_target_pairs={{0,1},{1,0},{2,3},{3,2},{4,5},{5,4},{6,7},{7,6},{8,9},{9,8},{10,11... | collective-permute-start | bytes 98312 | tf_op jit(solution)/shard_map/ppermute | solution.py:351
  84.2 0.7 copy-start.23
  85.1 7.3 %collective-permute-start.21 = (bf16[256,256]{1,0:T(8,128)(2,1)S(1)}, bf16[256,256]{1,0:T(8,128)(2,1)S(1)}, u32[]{:S(2)}, u32[]{:S(2)}) collective-permute-start(bf16[256,256]{1,0:T(8,128)(2,1)S(1)} %add_convert_fusion.1), channel_id=1, source_target_pairs={{0,18},{18,0},{2,16},{16,2},{1,19},{19,1},{3,17},{17,3},{4,22},{22... | collective-permute-start | bytes 393224 | tf_op jit(solution)/shard_map/ppermute | solution.py:107
  86.6 8.4 %collective-permute-start.22 = (bf16[256,256]{1,0:T(8,128)(2,1)S(1)}, bf16[256,256]{1,0:T(8,128)(2,1)S(1)}, u32[]{:S(2)}, u32[]{:S(2)}) collective-permute-start(bf16[256,256]{1,0:T(8,128)(2,1)S(1)} %add_convert_fusion.1), channel_id=1, source_target_pairs={{0,2},{2,0},{1,3},{3,1},{4,6},{6,4},{5,7},{7,5},{8,10},{10,8},{9,1... | collective-permute-start | bytes 393224 | tf_op jit(solution)/shard_map/ppermute | solution.py:107
  88.1 6.9 %collective-permute-start.23 = (bf16[256,256]{1,0:T(8,128)(2,1)S(1)}, bf16[256,256]{1,0:T(8,128)(2,1)S(1)}, u32[]{:S(2)}, u32[]{:S(2)}) collective-permute-start(bf16[256,256]{1,0:T(8,128)(2,1)S(1)} %add_convert_fusion.1), channel_id=1, source_target_pairs={{0,16},{16,0},{1,17},{17,1},{2,18},{18,2},{3,19},{19,3},{4,20},{20... | collective-permute-start | bytes 393224 | tf_op jit(solution)/shard_map/ppermute | solution.py:107
  88.7 9.3 %copy-start.22 = (bf16[1,64,512]{2,1,0:T(8,128)(2,1)S(1)}, bf16[1,64,512]{2,1,0:T(8,128)(2,1)}, u32[]{:S(2)}) copy-start(bf16[1,64,512]{2,1,0:T(8,128)(2,1)} %param.13) | copy-start | bytes 196612
  88.7 7.2 %collective-permute-start.24 = (bf16[64,1024]{1,0:T(8,128)(2,1)S(1)}, bf16[64,1024]{1,0:T(8,128)(2,1)S(1)}, u32[]{:S(2)}, u32[]{:S(2)}) collective-permute-start(bf16[64,1024]{1,0:T(8,128)(2,1)S(1)} %get-tuple-element.30), channel_id=1, source_target_pairs={{0,4},{4,8},{8,12},{12,0},{1,5},{5,9},{9,13},{13,1},{2,6},{6,10},{... | collective-permute-start | bytes 393224 | tf_op jit(solution)/shard_map/slot4/ppermute | solution.py:306
  92.4 5.6 %collective-permute-start.25 = (bf16[64,1024]{1,0:T(8,128)(2,1)S(1)}, bf16[64,1024]{1,0:T(8,128)(2,1)S(1)}, u32[]{:S(2)}, u32[]{:S(2)}) collective-permute-start(bf16[64,1024]{1,0:T(8,128)(2,1)S(1)} %get-tuple-element.31), channel_id=1, source_target_pairs={{4,0},{8,4},{12,8},{0,12},{5,1},{9,5},{13,9},{1,13},{6,2},{10,6},{... | collective-permute-start | bytes 393224 | tf_op jit(solution)/shard_map/slot4/ppermute | solution.py:306
  95.8 2.9 %copy-start.18 = (bf16[64,1024]{1,0:T(8,128)(2,1)}, bf16[64,1024]{1,0:T(8,128)(2,1)S(1)}, u32[]{:S(2)}) copy-start(bf16[64,1024]{1,0:T(8,128)(2,1)S(1)} %collective-permute-done.24.refs_3_) | copy-start | bytes 393220
  98.0 0.8 copy-start.19
  98.0 1.3 %collective-permute-start.26 = (bf16[256,256]{1,0:T(8,128)(2,1)S(1)}, bf16[256,256]{1,0:T(8,128)(2,1)S(1)}, u32[]{:S(2)}, u32[]{:S(2)}) collective-permute-start(bf16[256,256]{1,0:T(8,128)(2,1)S(1)} %add_convert_fusion.mine), channel_id=1, source_target_pairs={{0,1},{1,0},{2,3},{3,2},{4,5},{5,4},{6,7},{7,6},{8,9},{9,8},{10,11... | collective-permute-start | bytes 393224 | tf_op jit(solution)/shard_map/ppermute | solution.py:112
  101.9 9.2 %collective-permute-start.28 = (bf16[128,1024]{1,0:T(8,128)(2,1)S(1)}, bf16[128,1024]{1,0:T(8,128)(2,1)S(1)}, u32[]{:S(2)}, u32[]{:S(2)}) collective-permute-start(bf16[128,1024]{1,0:T(8,128)(2,1)S(1)} %get-tuple-element.35), channel_id=1, source_target_pairs={{0,2},{2,0},{1,3},{3,1},{4,6},{6,4},{5,7},{7,5},{8,10},{10,8},{9,1... | collective-permute-start | bytes 786440 | tf_op jit(solution)/shard_map/ppermute | solution.py:332
  102.5 12.9 %collective-permute-start.27 = (bf16[128,1024]{1,0:T(8,128)(2,1)S(1)}, bf16[128,1024]{1,0:T(8,128)(2,1)S(1)}, u32[]{:S(2)}, u32[]{:S(2)}) collective-permute-start(bf16[128,1024]{1,0:T(8,128)(2,1)S(1)} %get-tuple-element.34), channel_id=1, source_target_pairs={{0,16},{16,0},{1,17},{17,1},{2,18},{18,2},{3,19},{19,3},{4,20},{20... | collective-permute-start | bytes 786440 | tf_op jit(solution)/shard_map/ppermute | solution.py:333
  104.5 12.3 %collective-permute-start.29 = (bf16[128,1024]{1,0:T(8,128)(2,1)S(1)}, bf16[128,1024]{1,0:T(8,128)(2,1)S(1)}, u32[]{:S(2)}, u32[]{:S(2)}) collective-permute-start(bf16[128,1024]{1,0:T(8,128)(2,1)S(1)} %get-tuple-element.36), channel_id=1, source_target_pairs={{0,18},{18,0},{2,16},{16,2},{1,19},{19,1},{3,17},{17,3},{4,22},{22... | collective-permute-start | bytes 786440 | tf_op jit(solution)/shard_map/ppermute | solution.py:331
  111.1 5.7 %collective-permute-start.31 = (bf16[4,4096]{1,0:T(4,128)(2,1)S(1)}, bf16[4,4096]{1,0:T(4,128)(2,1)S(1)}, u32[]{:S(2)}, u32[]{:S(2)}) collective-permute-start(bf16[4,4096]{1,0:T(4,128)(2,1)S(1)} %convert_element_type.44.refs_0_), channel_id=1, source_target_pairs={{0,4},{4,8},{8,12},{12,0},{1,5},{5,9},{9,13},{13,1},{2,6},{6,10},{... | collective-permute-start | bytes 98312 | tf_op jit(solution)/shard_map/ppermute | solution.py:354
  111.8 5.0 %collective-permute-start.32 = (bf16[4,4096]{1,0:T(4,128)(2,1)S(1)}, bf16[4,4096]{1,0:T(4,128)(2,1)S(1)}, u32[]{:S(2)}, u32[]{:S(2)}) collective-permute-start(bf16[4,4096]{1,0:T(4,128)(2,1)S(1)} %convert_element_type.44.refs_0_), channel_id=1, source_target_pairs={{4,0},{8,4},{12,8},{0,12},{5,1},{9,5},{13,9},{1,13},{6,2},{10,6},{... | collective-permute-start | bytes 98312 | tf_op jit(solution)/shard_map/ppermute | solution.py:354
  114.9 4.8 %collective-permute-start.33 = (bf16[4,4096]{1,0:T(4,128)(2,1)S(1)}, bf16[4,4096]{1,0:T(4,128)(2,1)S(1)}, u32[]{:S(2)}, u32[]{:S(2)}) collective-permute-start(bf16[4,4096]{1,0:T(4,128)(2,1)S(1)} %convert_element_type.44.refs_0_), channel_id=1, source_target_pairs={{0,8},{8,0},{4,12},{12,4},{1,9},{9,1},{5,13},{13,5},{2,10},{10,2},... | collective-permute-start | bytes 98312 | tf_op jit(solution)/shard_map/ppermute | solution.py:354
  116.8 5.0 %copy-start.12 = (bf16[1,128,4096]{2,1,0:T(8,128)(2,1)}, bf16[1,128,4096]{2,1,0:T(8,128)(2,1)S(1)}, u32[]{:S(2)}) copy-start(bf16[1,128,4096]{2,1,0:T(8,128)(2,1)S(1)} %bitcast_dynamic-update-slice_fusion) | copy-start | bytes 3145732

commit v5 on v3

--- a/solution.py
+++ b/solution.py
@@ -351,7 +351,11 @@
     in_proj = in_part + lax.ppermute(in_part, "mp", PAIR)
     rows = own_rows(out_proj, in_proj, lengths[0])
     rows = after(rows, from_x)
-    blocks = [rows] + [lax.ppermute(rows, "dp", p) for p in (UP, DOWN, OPPOSITE)]
+    split = [(2 * a, 2 * b) for a, b in UP] + [(2 * a + 1, 2 * b + 1) for a, b in DOWN]
+    near = lax.ppermute(rows, ("dp", "mp"), split)
+    across = lax.ppermute(rows, "dp", OPPOSITE)
+    swapped = lax.ppermute(near, "mp", PAIR)
+    blocks = [rows, jnp.where(core == 0, near, swapped), jnp.where(core == 0, swapped, near), across]
     columns = rows.shape[1]
     scores = scores_by_kernel(blocks, damping * (columns * tok_rows / examples))[:, :examples]
     return (adjoint[None], scores)

time: 116 us -> 114 us (0.983)
  waiting for transfers between devices: 50.2 us -> 48.5 us
    ppermute x1, waiting for transfers between devices: 1.42 us -> 0.05 us  [spread(): from_xy = lax.ppermute(to_xy, *plane('both'))]
where the time goes in v5:
time: 114 us
  waiting for transfers between devices  48.5 us (43%)
  starting transfers between devices  43.9 us (39%)
  Pallas kernels  10.2 us (9%)
  local copies, waits for them, and re-layouts  6.62 us (6%)
  between operations  1.74 us (2%)
  other arithmetic  1.64 us (1%)
    ppermute x4, starting transfers between devices, gathered(): below, above = (lax.ppermute(w, 'dp', UP), lax.ppermute(w, 'dp', DOWN))  8.78 us
    ppermute x4, waiting for transfers between devices, gathered(): below, above = (lax.ppermute(w, 'dp', UP), lax.ppermute(w, 'dp', DOWN))  8.47 us
    pallas_call x3, Pallas kernels, kernel_call(): pl.pallas_call(body, name=name, out_shape=[o for o, _ in outs], in_specs=...  8.14 us
    ppermute x1, waiting for transfers between devices, spread(): lax.ppermute(both, 'dp', DOWN)  7.66 us
    ppermute x6, starting transfers between devices, summed(): lax.ppermute(own, *plane(a))  7.04 us
    ppermute x2, starting transfers between devices, gathered(): lax.ppermute(above[half:], 'dp', DOWN)  6.92 us
    ppermute x1, waiting for transfers between devices, spread(): lax.ppermute(both, 'dp', UP)  6.8 us
    ppermute x1, waiting for transfers between devices, spread(): from_x = lax.ppermute(to_x, *plane('section'))  4.87 us
  transfers between devices with their start and end apart: 34, of which 19 were waited for; matrix products, arithmetic and copies ran while one was open for 6% of the time, Pallas kernels for 4%

profile of v5, /device:TPU:0, one launch (start us, length us, event | category | flops | bytes accessed | tf_op | source)
XLA Modules:
  0.0 113.5 jit_solution(16854050477038266565)
XLA Ops:
  0.7 1.2 %dynamic-slice_bitcast_fusion.1 = (bf16[128,1024]{1,0:T(8,128)(2,1)S(1)}, bf16[128,1024]{1,0:T(8,128)(2,1)S(1)}) fusion(bf16[1,128,4096]{2,1,0:T(8,128)(2,1)} %param.11, s32[]{:T(128)S(6)} %select_n.89, s32[]{:T(128)S(6)} %select_n.86), kind=kLoop, calls=%fused_computation.15 | loop fusion | bytes 1048584 | tf_op jit(solution)/shard_map/dynamic_slice | solution.py:283
  1.8 3.0 %collective-permute-start.5 = (bf16[128,1024]{1,0:T(8,128)(2,1)S(1)}, bf16[128,1024]{1,0:T(8,128)(2,1)S(1)}, u32[]{:S(2)}, u32[]{:S(2)}) collective-permute-start(bf16[128,1024]{1,0:T(8,128)(2,1)S(1)} %get-tuple-element.40), channel_id=1, source_target_pairs={{0,2},{2,0},{1,3},{3,1},{4,6},{6,4},{5,7},{7,5},{8,10},{10,8},{9,1... | collective-permute-start | bytes 786440 | tf_op jit(solution)/shard_map/ppermute | solution.py:291
  4.8 1.6 %collective-permute-start.1 = (bf16[128,1024]{1,0:T(8,128)(2,1)S(1)}, bf16[128,1024]{1,0:T(8,128)(2,1)S(1)}, u32[]{:S(2)}, u32[]{:S(2)}) collective-permute-start(bf16[128,1024]{1,0:T(8,128)(2,1)S(1)} %get-tuple-element.41.refs_0_), channel_id=1, source_target_pairs={{0,4},{4,8},{8,12},{12,0},{1,5},{5,9},{9,13},{13,1},{2,6},{6,10},{... | collective-permute-start | bytes 786440 | tf_op jit(solution)/shard_map/slot1/ppermute | solution.py:96
  6.4 2.2 %collective-permute-start.2 = (bf16[128,1024]{1,0:T(8,128)(2,1)S(1)}, bf16[128,1024]{1,0:T(8,128)(2,1)S(1)}, u32[]{:S(2)}, u32[]{:S(2)}) collective-permute-start(bf16[128,1024]{1,0:T(8,128)(2,1)S(1)} %get-tuple-element.41.refs_0_), channel_id=1, source_target_pairs={{4,0},{8,4},{12,8},{0,12},{5,1},{9,5},{13,9},{1,13},{6,2},{10,6},{... | collective-permute-start | bytes 786440 | tf_op jit(solution)/shard_map/slot1/ppermute | solution.py:96
  8.7 1.7 %dynamic-slice_bitcast_fusion = bf16[128,1024]{1,0:T(8,128)(2,1)} fusion(bf16[1,128,4096]{2,1,0:T(8,128)(2,1)} %param.10, s32[]{:T(128)S(6)} %select_n.89), kind=kLoop, calls=%fused_computation.13 | loop fusion | bytes 524292 | tf_op jit(solution)/shard_map/dynamic_slice | solution.py:283
  10.3 0.3 collective-permute-start.11
  10.6 0.5 collective-permute-done.5
  11.1 1.0 broadcast_select_fusion.2
  12.2 2.9 %collective-permute-start.6 = (bf16[128,1024]{1,0:T(8,128)(2,1)S(1)}, bf16[128,1024]{1,0:T(8,128)(2,1)S(1)}, u32[]{:S(2)}, u32[]{:S(2)}) collective-permute-start(bf16[128,1024]{1,0:T(8,128)(2,1)S(1)} %get-tuple-element.38.refs_5_), channel_id=1, source_target_pairs={{0,4},{4,8},{8,12},{12,0},{1,5},{5,9},{9,13},{13,1},{2,6},{6,10},{... | collective-permute-start | bytes 786440 | tf_op jit(solution)/shard_map/slot2/ppermute | solution.py:96
  15.0 2.1 %collective-permute-start.7 = (bf16[128,1024]{1,0:T(8,128)(2,1)S(1)}, bf16[128,1024]{1,0:T(8,128)(2,1)S(1)}, u32[]{:S(2)}, u32[]{:S(2)}) collective-permute-start(bf16[128,1024]{1,0:T(8,128)(2,1)S(1)} %get-tuple-element.38.refs_5_), channel_id=1, source_target_pairs={{4,0},{8,4},{12,8},{0,12},{5,1},{9,5},{13,9},{1,13},{6,2},{10,6},{... | collective-permute-start | bytes 786440 | tf_op jit(solution)/shard_map/slot2/ppermute | solution.py:96
  17.1 1.8 %constant_dynamic-slice_fusion = (bf16[128,1024]{1,0:T(8,128)(2,1)S(1)}, bf16[128,1024]{1,0:T(8,128)(2,1)}) fusion(bf16[128,4096]{1,0:T(8,128)(2,1)} %param.9, s32[]{:T(128)S(6)} %select_n.87, s32[]{:T(128)S(6)} %select_n.86), kind=kLoop, calls=%fused_computation.49 | loop fusion | bytes 1048584 | tf_op jit(solution)/shard_map/dynamic_slice | solution.py:283
  18.9 1.6 %collective-permute-start = (bf16[128,1024]{1,0:T(8,128)(2,1)S(1)}, bf16[128,1024]{1,0:T(8,128)(2,1)S(1)}, u32[]{:S(2)}, u32[]{:S(2)}) collective-permute-start(bf16[128,1024]{1,0:T(8,128)(2,1)S(1)} %get-tuple-element.42), channel_id=1, source_target_pairs={{0,16},{16,0},{1,17},{17,1},{2,18},{18,2},{3,19},{19,3},{4,20},{20... | collective-permute-start | bytes 786440 | tf_op jit(solution)/shard_map/ppermute | solution.py:294
  20.5 1.4 %collective-permute-done.2.refs_2_ = bf16[128,1024]{1,0:T(8,128)(2,1)S(1)} collective-permute-done((bf16[128,1024]{1,0:T(8,128)(2,1)S(1)}, bf16[128,1024]{1,0:T(8,128)(2,1)S(1)}, u32[]{:S(2)}, u32[]{:S(2)}) %collective-permute-start.2) | collective-permute-done | bytes 262176 | tf_op jit(solution)/shard_map/slot1/ppermute | solution.py:96
  21.9 0.2 collective-permute-start.3
  22.2 3.6 %collective-permute-start.4 = (bf16[64,1024]{1,0:T(8,128)(2,1)S(1)}, bf16[64,1024]{1,0:T(8,128)(2,1)S(1)}, u32[]{:S(2)}, u32[]{:S(2)}) collective-permute-start(bf16[64,1024]{1,0:T(8,128)(2,1)S(1)} %slice.53), channel_id=1, source_target_pairs={{4,0},{8,4},{12,8},{0,12},{5,1},{9,5},{13,9},{1,13},{6,2},{10,6},{... | collective-permute-start | bytes 393224 | tf_op jit(solution)/shard_map/slot1/ppermute | solution.py:97
  25.8 1.4 %collective-permute-done.6.refs_6_ = bf16[128,1024]{1,0:T(8,128)(2,1)S(1)} collective-permute-done((bf16[128,1024]{1,0:T(8,128)(2,1)S(1)}, bf16[128,1024]{1,0:T(8,128)(2,1)S(1)}, u32[]{:S(2)}, u32[]{:S(2)}) %collective-permute-start.6) | collective-permute-done | bytes 262176 | tf_op jit(solution)/shard_map/slot2/ppermute | solution.py:96
  27.2 5.7 %collective-permute-done.7.refs_7_ = bf16[128,1024]{1,0:T(8,128)(2,1)S(1)} collective-permute-done((bf16[128,1024]{1,0:T(8,128)(2,1)S(1)}, bf16[128,1024]{1,0:T(8,128)(2,1)S(1)}, u32[]{:S(2)}, u32[]{:S(2)}) %collective-permute-start.7) | collective-permute-done | bytes 262176 | tf_op jit(solution)/shard_map/slot2/ppermute | solution.py:96
  32.9 0.5 collective-permute-start.8
  33.5 0.1 copy-done.10
  33.6 3.3 %collective-permute-start.9 = (bf16[64,1024]{1,0:T(8,128)(2,1)S(1)}, bf16[64,1024]{1,0:T(8,128)(2,1)S(1)}, u32[]{:S(2)}, u32[]{:S(2)}) collective-permute-start(bf16[64,1024]{1,0:T(8,128)(2,1)S(1)} %slice.55), channel_id=1, source_target_pairs={{4,0},{8,4},{12,8},{0,12},{5,1},{9,5},{13,9},{1,13},{6,2},{10,6},{... | collective-permute-start | bytes 393224 | tf_op jit(solution)/shard_map/slot2/ppermute | solution.py:97
  37.2 1.4 %collective-permute-done.4.refs_4_ = bf16[64,1024]{1,0:T(8,128)(2,1)S(1)} collective-permute-done((bf16[64,1024]{1,0:T(8,128)(2,1)S(1)}, bf16[64,1024]{1,0:T(8,128)(2,1)S(1)}, u32[]{:S(2)}, u32[]{:S(2)}) %collective-permute-start.4) | collective-permute-done | bytes 131104 | tf_op jit(solution)/shard_map/slot1/ppermute | solution.py:97
  38.6 2.6 %collective-permute-done.8.refs_8_ = bf16[64,1024]{1,0:T(8,128)(2,1)S(1)} collective-permute-done((bf16[64,1024]{1,0:T(8,128)(2,1)S(1)}, bf16[64,1024]{1,0:T(8,128)(2,1)S(1)}, u32[]{:S(2)}, u32[]{:S(2)}) %collective-permute-start.8) | collective-permute-done | bytes 131104 | tf_op jit(solution)/shard_map/slot2/ppermute | solution.py:97
  41.2 1.5 %collective-permute-done.9.refs_9_ = bf16[64,1024]{1,0:T(8,128)(2,1)S(1)} collective-permute-done((bf16[64,1024]{1,0:T(8,128)(2,1)S(1)}, bf16[64,1024]{1,0:T(8,128)(2,1)S(1)}, u32[]{:S(2)}, u32[]{:S(2)}) %collective-permute-start.9) | collective-permute-done | bytes 131104 | tf_op jit(solution)/shard_map/slot2/ppermute | solution.py:97
  42.8 0.6 copy-done.17
  43.4 2.5 %first.1 = (f32[256,256]{1,0:T(8,128)S(1)}, f32[256,256]{1,0:T(8,128)S(1)}) custom-call(s32[3]{0:T(128)S(1)} %pad_add_fusion.flags, bf16[128,1024]{1,0:T(8,128)(2,1)} %get-tuple-element.43.g_own, bf16[128,1024]{1,0:T(8,128)(2,1)} %copy-done.12, bf16[128,1024]{1,0:T(8,128)(2,1)} %copy-done.5, bf16[128,1024]{1,0:T(8,128)(2,1)} %copy-done.7, ...), custom_call_target="tpu_custom_call" | custom-call | tf_op jit(solution)/shard_map/first/pallas_call | solution.py:265
  46.0 2.5 %collective-permute-start.17 = (bf16[256,1024]{1,0:T(8,128)(2,1)S(1)}, bf16[256,1024]{1,0:T(8,128)(2,1)S(1)}, u32[]{:S(2)}, u32[]{:S(2)}) collective-permute-start(bf16[256,1024]{1,0:T(8,128)(2,1)S(1)} %pad_maximum_fusion.refs_10_.refs_0_), channel_id=1, source_target_pairs={{4,0},{8,4},{12,8},{0,12},{5,1},{9,5},{13,9},{1,13},{6,2},{10,6},{... | collective-permute-start | bytes 1572872 | tf_op jit(solution)/shard_map/slot34/ppermute | solution.py:301
  48.5 6.8 %collective-permute-done.12.refs_11_.refs_1_ = bf16[256,1024]{1,0:T(8,128)(2,1)S(1)} collective-permute-done((bf16[256,1024]{1,0:T(8,128)(2,1)S(1)}, bf16[256,1024]{1,0:T(8,128)(2,1)S(1)}, u32[]{:S(2)}, u32[]{:S(2)}) %collective-permute-start.12) | collective-permute-done | bytes 524320 | tf_op jit(solution)/shard_map/slot34/ppermute | solution.py:301
  55.3 1.5 %collective-permute-start.13 = (bf16[256,256]{1,0:T(8,128)(2,1)S(1)}, bf16[256,256]{1,0:T(8,128)(2,1)S(1)}, u32[]{:S(2)}, u32[]{:S(2)}) collective-permute-start(bf16[256,256]{1,0:T(8,128)(2,1)S(1)} %add_convert_fusion.3), channel_id=1, source_target_pairs={{0,18},{18,0},{2,16},{16,2},{1,19},{19,1},{3,17},{17,3},{4,22},{22... | collective-permute-start | bytes 393224 | tf_op jit(solution)/shard_map/ppermute | solution.py:107
  56.8 1.5 %collective-permute-start.14 = (bf16[256,256]{1,0:T(8,128)(2,1)S(1)}, bf16[256,256]{1,0:T(8,128)(2,1)S(1)}, u32[]{:S(2)}, u32[]{:S(2)}) collective-permute-start(bf16[256,256]{1,0:T(8,128)(2,1)S(1)} %add_convert_fusion.3), channel_id=1, source_target_pairs={{0,2},{2,0},{1,3},{3,1},{4,6},{6,4},{5,7},{7,5},{8,10},{10,8},{9,1... | collective-permute-start | bytes 393224 | tf_op jit(solution)/shard_map/ppermute | solution.py:107
  58.3 0.5 collective-permute-start.15
  58.8 7.7 %collective-permute-done.17.refs_12_.refs_2_ = bf16[256,1024]{1,0:T(8,128)(2,1)S(1)} collective-permute-done((bf16[256,1024]{1,0:T(8,128)(2,1)S(1)}, bf16[256,1024]{1,0:T(8,128)(2,1)S(1)}, u32[]{:S(2)}, u32[]{:S(2)}) %collective-permute-start.17) | collective-permute-done | bytes 524320 | tf_op jit(solution)/shard_map/slot34/ppermute | solution.py:301
  66.5 1.3 %collective-permute-start.18 = (bf16[64,1024]{1,0:T(8,128)(2,1)S(1)}, bf16[64,1024]{1,0:T(8,128)(2,1)S(1)}, u32[]{:S(2)}, u32[]{:S(2)}) collective-permute-start(bf16[64,1024]{1,0:T(8,128)(2,1)S(1)} %get-tuple-element.45), channel_id=1, source_target_pairs={{4,0},{8,4},{12,8},{0,12},{5,1},{9,5},{13,9},{1,13},{6,2},{10,6},{... | collective-permute-start | bytes 393224 | tf_op jit(solution)/shard_map/slot3/ppermute | solution.py:303
  67.9 0.7 collective-permute-done.16.refs_13_
  68.6 3.4 %collective-permute-done.18.refs_14_ = bf16[64,1024]{1,0:T(8,128)(2,1)S(1)} collective-permute-done((bf16[64,1024]{1,0:T(8,128)(2,1)S(1)}, bf16[64,1024]{1,0:T(8,128)(2,1)S(1)}, u32[]{:S(2)}, u32[]{:S(2)}) %collective-permute-start.18) | collective-permute-done | bytes 131104 | tf_op jit(solution)/shard_map/slot3/ppermute | solution.py:303
  72.0 1.3 %collective-permute-done.19.other = bf16[256,256]{1,0:T(8,128)(2,1)S(1)} collective-permute-done((bf16[256,256]{1,0:T(8,128)(2,1)S(1)}, bf16[256,256]{1,0:T(8,128)(2,1)S(1)}, u32[]{:S(2)}, u32[]{:S(2)}) %collective-permute-start.19) | collective-permute-done | bytes 131104 | tf_op jit(solution)/shard_map/ppermute | solution.py:112
  73.4 3.1 %middle.1 = (bf16[256,1024]{1,0:T(8,128)(2,1)S(1)}, f32[256,256]{1,0:T(8,128)S(1)}, f32[256,256]{1,0:T(8,128)S(1)}) custom-call(s32[3]{0:T(128)S(1)} %pad_add_fusion.flags, bf16[128,1024]{1,0:T(8,128)(2,1)} %get-tuple-element.43.g_own, bf16[128,1024]{1,0:T(8,128)(2,1)} %copy-done.12, bf16[256,256]{1,0:T(8,128)(2,1)S(1)} %add_convert_fusion.2.mine, ...), custom_call_target="tpu_custom_call" | custom-call | tf_op jit(solution)/shard_map/middle/pallas_call | solution.py:265
  76.5 0.2 collective-permute-start.20
  76.7 0.5 fusion.1
  77.3 0.4 collective-permute-start.30
  77.7 0.7 copy-done.23
  78.4 0.1 convert_reduce_fusion
  78.5 1.6 %collective-permute-start.21 = (bf16[256,256]{1,0:T(8,128)(2,1)S(1)}, bf16[256,256]{1,0:T(8,128)(2,1)S(1)}, u32[]{:S(2)}, u32[]{:S(2)}) collective-permute-start(bf16[256,256]{1,0:T(8,128)(2,1)S(1)} %add_convert_fusion.1), channel_id=1, source_target_pairs={{0,18},{18,0},{2,16},{16,2},{1,19},{19,1},{3,17},{17,3},{4,22},{22... | collective-permute-start | bytes 393224 | tf_op jit(solution)/shard_map/ppermute | solution.py:107
  80.1 1.5 %collective-permute-start.22 = (bf16[256,256]{1,0:T(8,128)(2,1)S(1)}, bf16[256,256]{1,0:T(8,128)(2,1)S(1)}, u32[]{:S(2)}, u32[]{:S(2)}) collective-permute-start(bf16[256,256]{1,0:T(8,128)(2,1)S(1)} %add_convert_fusion.1), channel_id=1, source_target_pairs={{0,2},{2,0},{1,3},{3,1},{4,6},{6,4},{5,7},{7,5},{8,10},{10,8},{9,1... | collective-permute-start | bytes 393224 | tf_op jit(solution)/shard_map/ppermute | solution.py:107
  81.6 0.5 collective-permute-start.23
  82.1 0.6 collective-permute-start.24
  82.6 3.2 %collective-permute-done.21 = bf16[256,256]{1,0:T(8,128)(2,1)S(1)} collective-permute-done((bf16[256,256]{1,0:T(8,128)(2,1)S(1)}, bf16[256,256]{1,0:T(8,128)(2,1)S(1)}, u32[]{:S(2)}, u32[]{:S(2)}) %collective-permute-start.21) | collective-permute-done | bytes 131104 | tf_op jit(solution)/shard_map/ppermute | solution.py:107
  85.8 2.5 %collective-permute-start.25 = (bf16[64,1024]{1,0:T(8,128)(2,1)S(1)}, bf16[64,1024]{1,0:T(8,128)(2,1)S(1)}, u32[]{:S(2)}, u32[]{:S(2)}) collective-permute-start(bf16[64,1024]{1,0:T(8,128)(2,1)S(1)} %get-tuple-element.31), channel_id=1, source_target_pairs={{4,0},{8,4},{12,8},{0,12},{5,1},{9,5},{13,9},{1,13},{6,2},{10,6},{... | collective-permute-start | bytes 393224 | tf_op jit(solution)/shard_map/slot4/ppermute | solution.py:306
  88.5 1.5 %collective-permute-done.24.refs_3_ = bf16[64,1024]{1,0:T(8,128)(2,1)S(1)} collective-permute-done((bf16[64,1024]{1,0:T(8,128)(2,1)S(1)}, bf16[64,1024]{1,0:T(8,128)(2,1)S(1)}, u32[]{:S(2)}, u32[]{:S(2)}) %collective-permute-start.24) | collective-permute-done | bytes 131104 | tf_op jit(solution)/shard_map/slot4/ppermute | solution.py:306
  89.9 1.5 %collective-permute-done.25.refs_4_ = bf16[64,1024]{1,0:T(8,128)(2,1)S(1)} collective-permute-done((bf16[64,1024]{1,0:T(8,128)(2,1)S(1)}, bf16[64,1024]{1,0:T(8,128)(2,1)S(1)}, u32[]{:S(2)}, u32[]{:S(2)}) %collective-permute-start.25) | collective-permute-done | bytes 131104 | tf_op jit(solution)/shard_map/slot4/ppermute | solution.py:306
  92.2 0.6 collective-permute-done.26.other
  92.8 2.5 %last.1 = (bf16[128,1024]{1,0:T(8,128)(2,1)S(1)}, bf16[128,1024]{1,0:T(8,128)(2,1)S(1)}, bf16[128,1024]{1,0:T(8,128)(2,1)S(1)}, bf16[128,1024]{1,0:T(8,128)(2,1)S(1)}) custom-call(s32[3]{0:T(128)S(1)} %pad_add_fusion.flags, bf16[256,1024]{1,0:T(8,128)(2,1)} %copy-done.1, bf16[256,256]{1,0:T(8,128)(2,1)S(1)} %add_convert_fusion.mine, ...), custom_call_target="tpu_custom_call" | custom-call | tf_op jit(solution)/shard_map/last/pallas_call | solution.py:265
  95.3 0.5 collective-permute-start.28
  95.8 1.6 %collective-permute-start.27 = (bf16[128,1024]{1,0:T(8,128)(2,1)S(1)}, bf16[128,1024]{1,0:T(8,128)(2,1)S(1)}, u32[]{:S(2)}, u32[]{:S(2)}) collective-permute-start(bf16[128,1024]{1,0:T(8,128)(2,1)S(1)} %get-tuple-element.34), channel_id=1, source_target_pairs={{0,16},{16,0},{1,17},{17,1},{2,18},{18,2},{3,19},{19,3},{4,20},{20... | collective-permute-start | bytes 786440 | tf_op jit(solution)/shard_map/ppermute | solution.py:333
  97.4 0.2 fusion.4
  97.6 0.3 fusion
  97.9 0.1 convert_element_type.64.refs_0_
  98.0 1.5 %collective-permute-start.29 = (bf16[128,1024]{1,0:T(8,128)(2,1)S(1)}, bf16[128,1024]{1,0:T(8,128)(2,1)S(1)}, u32[]{:S(2)}, u32[]{:S(2)}) collective-permute-start(bf16[128,1024]{1,0:T(8,128)(2,1)S(1)} %get-tuple-element.36), channel_id=1, source_target_pairs={{0,18},{18,0},{2,16},{16,2},{1,19},{19,1},{3,17},{17,3},{4,22},{22... | collective-permute-start | bytes 786440 | tf_op jit(solution)/shard_map/ppermute | solution.py:331
  99.5 0.1 broadcast_in_dim.32
  99.6 4.9 %collective-permute-done.28 = bf16[128,1024]{1,0:T(8,128)(2,1)S(1)} collective-permute-done((bf16[128,1024]{1,0:T(8,128)(2,1)S(1)}, bf16[128,1024]{1,0:T(8,128)(2,1)S(1)}, u32[]{:S(2)}, u32[]{:S(2)}) %collective-permute-start.28) | collective-permute-done | bytes 262176 | tf_op jit(solution)/shard_map/ppermute | solution.py:332
  104.5 0.6 collective-permute-start.31
  105.1 3.7 %collective-permute-start.33 = (bf16[4,4096]{1,0:T(4,128)(2,1)S(1)}, bf16[4,4096]{1,0:T(4,128)(2,1)S(1)}, u32[]{:S(2)}, u32[]{:S(2)}) collective-permute-start(bf16[4,4096]{1,0:T(4,128)(2,1)S(1)} %convert_element_type.64.refs_0_), channel_id=1, source_target_pairs={{0,8},{8,0},{4,12},{12,4},{1,9},{9,1},{5,13},{13,5},{2,10},{10,2},... | collective-permute-start | bytes 98312 | tf_op jit(solution)/shard_map/ppermute | solution.py:356
  108.9 1.4 %collective-permute-done.31 = bf16[4,4096]{1,0:T(4,128)(2,1)S(1)} collective-permute-done((bf16[4,4096]{1,0:T(4,128)(2,1)S(1)}, bf16[4,4096]{1,0:T(4,128)(2,1)S(1)}, u32[]{:S(2)}, u32[]{:S(2)}) %collective-permute-start.31) | collective-permute-done | bytes 32800 | tf_op jit(solution)/shard_map/ppermute | solution.py:355
  110.3 1.1 collective-permute-done.32
  111.5 2.0 %scores.1 = f32[1,16]{1,0:T(1,128)} custom-call(f32[1]{0:T(128)S(6)} %mul.57.shift, bf16[4,4096]{1,0:T(4,128)(2,1)S(1)} %convert_element_type.64.refs_0_, bf16[4,4096]{1,0:T(4,128)(2,1)S(1)} %get-tuple-element.55.refs_1_, bf16[4,4096]{1,0:T(4,128)(2,1)S(1)} %get-tuple-element.54.refs_2_, bf16[4,4096]{1,0:T(4,128)(2,1)S(1)} %collective-permute-done.33.refs_3_), custom_call_target="tpu_custom_call" | custom-call | tf_op jit(solution)/shard_map/scores/pallas_call | solution.py:252
  (90 shorter events, 1.2 us)
Async XLA Ops:
  0.6 76.1 %copy-start = (bf16[1,128,4096]{2,1,0:T(8,128)(2,1)S(1)}, bf16[1,128,4096]{2,1,0:T(8,128)(2,1)}, u32[]{:S(2)}) copy-start(bf16[1,128,4096]{2,1,0:T(8,128)(2,1)} %param.8) | copy-start | bytes 3145732
  1.8 8.5 %copy-start.5 = (bf16[128,1024]{1,0:T(8,128)(2,1)}, bf16[128,1024]{1,0:T(8,128)(2,1)S(1)}, u32[]{:S(2)}) copy-start(bf16[128,1024]{1,0:T(8,128)(2,1)S(1)} %get-tuple-element.41.refs_0_) | copy-start | bytes 786436
  1.8 9.3 %collective-permute-start.5 = (bf16[128,1024]{1,0:T(8,128)(2,1)S(1)}, bf16[128,1024]{1,0:T(8,128)(2,1)S(1)}, u32[]{:S(2)}, u32[]{:S(2)}) collective-permute-start(bf16[128,1024]{1,0:T(8,128)(2,1)S(1)} %get-tuple-element.40), channel_id=1, source_target_pairs={{0,2},{2,0},{1,3},{3,1},{4,6},{6,4},{5,7},{7,5},{8,10},{10,8},{9,1... | collective-permute-start | bytes 786440 | tf_op jit(solution)/shard_map/ppermute | solution.py:291
  4.8 14.1 %collective-permute-start.1 = (bf16[128,1024]{1,0:T(8,128)(2,1)S(1)}, bf16[128,1024]{1,0:T(8,128)(2,1)S(1)}, u32[]{:S(2)}, u32[]{:S(2)}) collective-permute-start(bf16[128,1024]{1,0:T(8,128)(2,1)S(1)} %get-tuple-element.41.refs_0_), channel_id=1, source_target_pairs={{0,4},{4,8},{8,12},{12,0},{1,5},{5,9},{9,13},{13,1},{2,6},{6,10},{... | collective-permute-start | bytes 786440 | tf_op jit(solution)/shard_map/slot1/ppermute | solution.py:96
  6.4 15.5 %collective-permute-start.2 = (bf16[128,1024]{1,0:T(8,128)(2,1)S(1)}, bf16[128,1024]{1,0:T(8,128)(2,1)S(1)}, u32[]{:S(2)}, u32[]{:S(2)}) collective-permute-start(bf16[128,1024]{1,0:T(8,128)(2,1)S(1)} %get-tuple-element.41.refs_0_), channel_id=1, source_target_pairs={{4,0},{8,4},{12,8},{0,12},{5,1},{9,5},{13,9},{1,13},{6,2},{10,6},{... | collective-permute-start | bytes 786440 | tf_op jit(solution)/shard_map/slot1/ppermute | solution.py:96
  10.3 11.8 %collective-permute-start.11 = (bf16[128,1024]{1,0:T(8,128)(2,1)}, bf16[128,1024]{1,0:T(8,128)(2,1)S(1)}, u32[]{:S(2)}, u32[]{:S(2)}) collective-permute-start(bf16[128,1024]{1,0:T(8,128)(2,1)} %dynamic-slice_bitcast_fusion), channel_id=1, source_target_pairs={{0,2},{2,0},{1,3},{3,1},{4,6},{6,4},{5,7},{7,5},{8,10},{10,8},{9,1... | collective-permute-start | bytes 786440 | tf_op jit(solution)/shard_map/ppermute | solution.py:292
  12.2 6.7 %copy-start.6 = (bf16[128,1024]{1,0:T(8,128)(2,1)}, bf16[128,1024]{1,0:T(8,128)(2,1)S(1)}, u32[]{:S(2)}) copy-start(bf16[128,1024]{1,0:T(8,128)(2,1)S(1)} %get-tuple-element.38.refs_5_) | copy-start | bytes 786436
  12.2 15.0 %collective-permute-start.6 = (bf16[128,1024]{1,0:T(8,128)(2,1)S(1)}, bf16[128,1024]{1,0:T(8,128)(2,1)S(1)}, u32[]{:S(2)}, u32[]{:S(2)}) collective-permute-start(bf16[128,1024]{1,0:T(8,128)(2,1)S(1)} %get-tuple-element.38.refs_5_), channel_id=1, source_target_pairs={{0,4},{4,8},{8,12},{12,0},{1,5},{5,9},{9,13},{13,1},{2,6},{6,10},{... | collective-permute-start | bytes 786440 | tf_op jit(solution)/shard_map/slot2/ppermute | solution.py:96
  15.0 17.9 %collective-permute-start.7 = (bf16[128,1024]{1,0:T(8,128)(2,1)S(1)}, bf16[128,1024]{1,0:T(8,128)(2,1)S(1)}, u32[]{:S(2)}, u32[]{:S(2)}) collective-permute-start(bf16[128,1024]{1,0:T(8,128)(2,1)S(1)} %get-tuple-element.38.refs_5_), channel_id=1, source_target_pairs={{4,0},{8,4},{12,8},{0,12},{5,1},{9,5},{13,9},{1,13},{6,2},{10,6},{... | collective-permute-start | bytes 786440 | tf_op jit(solution)/shard_map/slot2/ppermute | solution.py:96
  18.9 3.2 %copy-start.7 = (bf16[128,1024]{1,0:T(8,128)(2,1)}, bf16[128,1024]{1,0:T(8,128)(2,1)S(1)}, u32[]{:S(2)}) copy-start(bf16[128,1024]{1,0:T(8,128)(2,1)S(1)} %collective-permute-done.1.refs_1_) | copy-start | bytes 786436
  18.9 18.1 %collective-permute-start = (bf16[128,1024]{1,0:T(8,128)(2,1)S(1)}, bf16[128,1024]{1,0:T(8,128)(2,1)S(1)}, u32[]{:S(2)}, u32[]{:S(2)}) collective-permute-start(bf16[128,1024]{1,0:T(8,128)(2,1)S(1)} %get-tuple-element.42), channel_id=1, source_target_pairs={{0,16},{16,0},{1,17},{17,1},{2,18},{18,2},{3,19},{19,3},{4,20},{20... | collective-permute-start | bytes 786440 | tf_op jit(solution)/shard_map/ppermute | solution.py:294
  21.9 11.0 %copy-start.8 = (bf16[128,1024]{1,0:T(8,128)(2,1)}, bf16[128,1024]{1,0:T(8,128)(2,1)S(1)}, u32[]{:S(2)}) copy-start(bf16[128,1024]{1,0:T(8,128)(2,1)S(1)} %collective-permute-done.2.refs_2_) | copy-start | bytes 786436
  21.9 15.3 %collective-permute-start.3 = (bf16[64,1024]{1,0:T(8,128)(2,1)S(1)}, bf16[64,1024]{1,0:T(8,128)(2,1)S(1)}, u32[]{:S(2)}, u32[]{:S(2)}) collective-permute-start(bf16[64,1024]{1,0:T(8,128)(2,1)S(1)} %slice.52), channel_id=1, source_target_pairs={{0,4},{4,8},{8,12},{12,0},{1,5},{5,9},{9,13},{13,1},{2,6},{6,10},{... | collective-permute-start | bytes 393224 | tf_op jit(solution)/shard_map/slot1/ppermute | solution.py:97
  22.2 16.4 %collective-permute-start.4 = (bf16[64,1024]{1,0:T(8,128)(2,1)S(1)}, bf16[64,1024]{1,0:T(8,128)(2,1)S(1)}, u32[]{:S(2)}, u32[]{:S(2)}) collective-permute-start(bf16[64,1024]{1,0:T(8,128)(2,1)S(1)} %slice.53), channel_id=1, source_target_pairs={{4,0},{8,4},{12,8},{0,12},{5,1},{9,5},{13,9},{1,13},{6,2},{10,6},{... | collective-permute-start | bytes 393224 | tf_op jit(solution)/shard_map/slot1/ppermute | solution.py:97
  27.2 6.3 %copy-start.9 = (bf16[128,1024]{1,0:T(8,128)(2,1)}, bf16[128,1024]{1,0:T(8,128)(2,1)S(1)}, u32[]{:S(2)}) copy-start(bf16[128,1024]{1,0:T(8,128)(2,1)S(1)} %collective-permute-done.6.refs_6_) | copy-start | bytes 786436
  32.9 0.7 copy-start.10
  32.9 8.3 %collective-permute-start.8 = (bf16[64,1024]{1,0:T(8,128)(2,1)S(1)}, bf16[64,1024]{1,0:T(8,128)(2,1)S(1)}, u32[]{:S(2)}, u32[]{:S(2)}) collective-permute-start(bf16[64,1024]{1,0:T(8,128)(2,1)S(1)} %slice.54), channel_id=1, source_target_pairs={{0,4},{4,8},{8,12},{12,0},{1,5},{5,9},{9,13},{13,1},{2,6},{6,10},{... | collective-permute-start | bytes 393224 | tf_op jit(solution)/shard_map/slot2/ppermute | solution.py:97
  33.6 9.1 %collective-permute-start.9 = (bf16[64,1024]{1,0:T(8,128)(2,1)S(1)}, bf16[64,1024]{1,0:T(8,128)(2,1)S(1)}, u32[]{:S(2)}, u32[]{:S(2)}) collective-permute-start(bf16[64,1024]{1,0:T(8,128)(2,1)S(1)} %slice.55), channel_id=1, source_target_pairs={{4,0},{8,4},{12,8},{0,12},{5,1},{9,5},{13,9},{1,13},{6,2},{10,6},{... | collective-permute-start | bytes 393224 | tf_op jit(solution)/shard_map/slot2/ppermute | solution.py:97
  37.0 8.9 %copy-start.2 = (bf16[256,1024]{1,0:T(8,128)(2,1)}, bf16[256,1024]{1,0:T(8,128)(2,1)S(1)}, u32[]{:S(2)}) copy-start(bf16[256,1024]{1,0:T(8,128)(2,1)S(1)} %pad_maximum_fusion.refs_10_.refs_0_) | copy-start | bytes 1572868
  37.0 5.7 %copy-start.12 = (bf16[128,1024]{1,0:T(8,128)(2,1)}, bf16[128,1024]{1,0:T(8,128)(2,1)S(1)}, u32[]{:S(2)}) copy-start(bf16[128,1024]{1,0:T(8,128)(2,1)S(1)} %collective-permute-done.g_other) | copy-start | bytes 786436
  37.1 18.2 %collective-permute-start.12 = (bf16[256,1024]{1,0:T(8,128)(2,1)S(1)}, bf16[256,1024]{1,0:T(8,128)(2,1)S(1)}, u32[]{:S(2)}, u32[]{:S(2)}) collective-permute-start(bf16[256,1024]{1,0:T(8,128)(2,1)S(1)} %pad_maximum_fusion.refs_10_.refs_0_), channel_id=1, source_target_pairs={{0,4},{4,8},{8,12},{12,0},{1,5},{5,9},{9,13},{13,1},{2,6},{6,10},{... | collective-permute-start | bytes 1572872 | tf_op jit(solution)/shard_map/slot34/ppermute | solution.py:301
  37.2 5.5 %copy-start.14 = (bf16[64,1024]{1,0:T(8,128)(2,1)}, bf16[64,1024]{1,0:T(8,128)(2,1)S(1)}, u32[]{:S(2)}) copy-start(bf16[64,1024]{1,0:T(8,128)(2,1)S(1)} %collective-permute-done.3.refs_3_) | copy-start | bytes 393220
  38.6 4.2 %copy-start.15 = (bf16[64,1024]{1,0:T(8,128)(2,1)}, bf16[64,1024]{1,0:T(8,128)(2,1)S(1)}, u32[]{:S(2)}) copy-start(bf16[64,1024]{1,0:T(8,128)(2,1)S(1)} %collective-permute-done.4.refs_4_) | copy-start | bytes 393220
  41.2 1.5 %copy-start.16 = (bf16[64,1024]{1,0:T(8,128)(2,1)}, bf16[64,1024]{1,0:T(8,128)(2,1)S(1)}, u32[]{:S(2)}) copy-start(bf16[64,1024]{1,0:T(8,128)(2,1)S(1)} %collective-permute-done.8.refs_8_) | copy-start | bytes 393220
  42.7 0.7 copy-start.17
  45.9 2.6 %collective-permute-start.10 = (f32[256,256]{1,0:T(8,128)S(1)}, f32[256,256]{1,0:T(8,128)S(1)}, u32[]{:S(2)}, u32[]{:S(2)}) collective-permute-start(f32[256,256]{1,0:T(8,128)S(1)} %get-tuple-element.21), channel_id=1, source_target_pairs={{0,1},{1,0},{2,3},{3,2},{4,5},{5,4},{6,7},{7,6},{8,9},{9,8},{10,11... | collective-permute-start | bytes 786440 | tf_op jit(solution)/shard_map/ppermute | solution.py:106
  46.0 20.5 %collective-permute-start.17 = (bf16[256,1024]{1,0:T(8,128)(2,1)S(1)}, bf16[256,1024]{1,0:T(8,128)(2,1)S(1)}, u32[]{:S(2)}, u32[]{:S(2)}) collective-permute-start(bf16[256,1024]{1,0:T(8,128)(2,1)S(1)} %pad_maximum_fusion.refs_10_.refs_0_), channel_id=1, source_target_pairs={{4,0},{8,4},{12,8},{0,12},{5,1},{9,5},{13,9},{1,13},{6,2},{10,6},{... | collective-permute-start | bytes 1572872 | tf_op jit(solution)/shard_map/slot34/ppermute | solution.py:301
  55.3 11.3 %copy-start.3 = (bf16[256,1024]{1,0:T(8,128)(2,1)}, bf16[256,1024]{1,0:T(8,128)(2,1)S(1)}, u32[]{:S(2)}) copy-start(bf16[256,1024]{1,0:T(8,128)(2,1)S(1)} %collective-permute-done.12.refs_11_.refs_1_) | copy-start | bytes 1572868
  55.3 12.5 %collective-permute-start.13 = (bf16[256,256]{1,0:T(8,128)(2,1)S(1)}, bf16[256,256]{1,0:T(8,128)(2,1)S(1)}, u32[]{:S(2)}, u32[]{:S(2)}) collective-permute-start(bf16[256,256]{1,0:T(8,128)(2,1)S(1)} %add_convert_fusion.3), channel_id=1, source_target_pairs={{0,18},{18,0},{2,16},{16,2},{1,19},{19,1},{3,17},{17,3},{4,22},{22... | collective-permute-start | bytes 393224 | tf_op jit(solution)/shard_map/ppermute | solution.py:107
  56.8 11.0 %collective-permute-start.14 = (bf16[256,256]{1,0:T(8,128)(2,1)S(1)}, bf16[256,256]{1,0:T(8,128)(2,1)S(1)}, u32[]{:S(2)}, u32[]{:S(2)}) collective-permute-start(bf16[256,256]{1,0:T(8,128)(2,1)S(1)} %add_convert_fusion.3), channel_id=1, source_target_pairs={{0,2},{2,0},{1,3},{3,1},{4,6},{6,4},{5,7},{7,5},{8,10},{10,8},{9,1... | collective-permute-start | bytes 393224 | tf_op jit(solution)/shard_map/ppermute | solution.py:107
  58.3 9.5 %collective-permute-start.15 = (bf16[256,256]{1,0:T(8,128)(2,1)S(1)}, bf16[256,256]{1,0:T(8,128)(2,1)S(1)}, u32[]{:S(2)}, u32[]{:S(2)}) collective-permute-start(bf16[256,256]{1,0:T(8,128)(2,1)S(1)} %add_convert_fusion.3), channel_id=1, source_target_pairs={{0,16},{16,0},{1,17},{17,1},{2,18},{18,2},{3,19},{19,3},{4,20},{20... | collective-permute-start | bytes 393224 | tf_op jit(solution)/shard_map/ppermute | solution.py:107
  58.8 9.8 %collective-permute-start.16 = (bf16[64,1024]{1,0:T(8,128)(2,1)S(1)}, bf16[64,1024]{1,0:T(8,128)(2,1)S(1)}, u32[]{:S(2)}, u32[]{:S(2)}) collective-permute-start(bf16[64,1024]{1,0:T(8,128)(2,1)S(1)} %get-tuple-element.47), channel_id=1, source_target_pairs={{0,4},{4,8},{8,12},{12,0},{1,5},{5,9},{9,13},{13,1},{2,6},{6,10},{... | collective-permute-start | bytes 393224 | tf_op jit(solution)/shard_map/slot3/ppermute | solution.py:303
  66.5 1.4 %copy-start.4 = (bf16[256,1024]{1,0:T(8,128)(2,1)}, bf16[256,1024]{1,0:T(8,128)(2,1)S(1)}, u32[]{:S(2)}) copy-start(bf16[256,1024]{1,0:T(8,128)(2,1)S(1)} %collective-permute-done.17.refs_12_.refs_2_) | copy-start | bytes 1572868
  66.5 5.5 %collective-permute-start.18 = (bf16[64,1024]{1,0:T(8,128)(2,1)S(1)}, bf16[64,1024]{1,0:T(8,128)(2,1)S(1)}, u32[]{:S(2)}, u32[]{:S(2)}) collective-permute-start(bf16[64,1024]{1,0:T(8,128)(2,1)S(1)} %get-tuple-element.45), channel_id=1, source_target_pairs={{4,0},{8,4},{12,8},{0,12},{5,1},{9,5},{13,9},{1,13},{6,2},{10,6},{... | collective-permute-start | bytes 393224 | tf_op jit(solution)/shard_map/slot3/ppermute | solution.py:303
  67.9 8.8 %copy-start.13 = (bf16[1,64,4096]{2,1,0:T(8,128)(2,1)S(1)}, bf16[1,64,4096]{2,1,0:T(8,128)(2,1)}, u32[]{:S(2)}) copy-start(bf16[1,64,4096]{2,1,0:T(8,128)(2,1)} %param.12) | copy-start | bytes 1572868
  68.6 4.8 %copy-start.20 = (bf16[64,1024]{1,0:T(8,128)(2,1)}, bf16[64,1024]{1,0:T(8,128)(2,1)S(1)}, u32[]{:S(2)}) copy-start(bf16[64,1024]{1,0:T(8,128)(2,1)S(1)} %collective-permute-done.16.refs_13_) | copy-start | bytes 393220
  72.0 1.4 %copy-start.21 = (bf16[64,1024]{1,0:T(8,128)(2,1)}, bf16[64,1024]{1,0:T(8,128)(2,1)S(1)}, u32[]{:S(2)}) copy-start(bf16[64,1024]{1,0:T(8,128)(2,1)S(1)} %collective-permute-done.18.refs_14_) | copy-start | bytes 393220
  72.0 1.3 %collective-permute-start.19 = (bf16[256,256]{1,0:T(8,128)(2,1)S(1)}, bf16[256,256]{1,0:T(8,128)(2,1)S(1)}, u32[]{:S(2)}, u32[]{:S(2)}) collective-permute-start(bf16[256,256]{1,0:T(8,128)(2,1)S(1)} %add_convert_fusion.2.mine), channel_id=1, source_target_pairs={{0,1},{1,0},{2,3},{3,2},{4,5},{5,4},{6,7},{7,6},{8,9},{9,8},{10,11... | collective-permute-start | bytes 393224 | tf_op jit(solution)/shard_map/ppermute | solution.py:112
  76.5 0.8 copy-start.1
  76.5 2.0 %collective-permute-start.20 = (f32[256,256]{1,0:T(8,128)S(1)}, f32[256,256]{1,0:T(8,128)S(1)}, u32[]{:S(2)}, u32[]{:S(2)}) collective-permute-start(f32[256,256]{1,0:T(8,128)S(1)} %get-tuple-element.29), channel_id=1, source_target_pairs={{0,1},{1,0},{2,3},{3,2},{4,5},{5,4},{6,7},{7,6},{8,9},{9,8},{10,11... | collective-permute-start | bytes 786440 | tf_op jit(solution)/shard_map/ppermute | solution.py:106
  77.3 20.3 %collective-permute-start.30 = (f32[128,64]{0,1:T(8,128)S(1)}, f32[128,64]{0,1:T(8,128)S(1)}, u32[]{:S(2)}, u32[]{:S(2)}) collective-permute-start(f32[128,64]{0,1:T(8,128)S(1)} %fusion.1), channel_id=1, source_target_pairs={{0,1},{1,0},{2,3},{3,2},{4,5},{5,4},{6,7},{7,6},{8,9},{9,8},{10,11... | collective-permute-start | bytes 98312 | tf_op jit(solution)/shard_map/ppermute | solution.py:351
  77.7 0.7 copy-start.23
  78.5 7.3 %collective-permute-start.21 = (bf16[256,256]{1,0:T(8,128)(2,1)S(1)}, bf16[256,256]{1,0:T(8,128)(2,1)S(1)}, u32[]{:S(2)}, u32[]{:S(2)}) collective-permute-start(bf16[256,256]{1,0:T(8,128)(2,1)S(1)} %add_convert_fusion.1), channel_id=1, source_target_pairs={{0,18},{18,0},{2,16},{16,2},{1,19},{19,1},{3,17},{17,3},{4,22},{22... | collective-permute-start | bytes 393224 | tf_op jit(solution)/shard_map/ppermute | solution.py:107
  80.1 8.3 %collective-permute-start.22 = (bf16[256,256]{1,0:T(8,128)(2,1)S(1)}, bf16[256,256]{1,0:T(8,128)(2,1)S(1)}, u32[]{:S(2)}, u32[]{:S(2)}) collective-permute-start(bf16[256,256]{1,0:T(8,128)(2,1)S(1)} %add_convert_fusion.1), channel_id=1, source_target_pairs={{0,2},{2,0},{1,3},{3,1},{4,6},{6,4},{5,7},{7,5},{8,10},{10,8},{9,1... | collective-permute-start | bytes 393224 | tf_op jit(solution)/shard_map/ppermute | solution.py:107
  81.6 6.8 %collective-permute-start.23 = (bf16[256,256]{1,0:T(8,128)(2,1)S(1)}, bf16[256,256]{1,0:T(8,128)(2,1)S(1)}, u32[]{:S(2)}, u32[]{:S(2)}) collective-permute-start(bf16[256,256]{1,0:T(8,128)(2,1)S(1)} %add_convert_fusion.1), channel_id=1, source_target_pairs={{0,16},{16,0},{1,17},{17,1},{2,18},{18,2},{3,19},{19,3},{4,20},{20... | collective-permute-start | bytes 393224 | tf_op jit(solution)/shard_map/ppermute | solution.py:107
  82.1 9.3 %copy-start.22 = (bf16[1,64,512]{2,1,0:T(8,128)(2,1)S(1)}, bf16[1,64,512]{2,1,0:T(8,128)(2,1)}, u32[]{:S(2)}) copy-start(bf16[1,64,512]{2,1,0:T(8,128)(2,1)} %param.13) | copy-start | bytes 196612
  82.1 7.8 %collective-permute-start.24 = (bf16[64,1024]{1,0:T(8,128)(2,1)S(1)}, bf16[64,1024]{1,0:T(8,128)(2,1)S(1)}, u32[]{:S(2)}, u32[]{:S(2)}) collective-permute-start(bf16[64,1024]{1,0:T(8,128)(2,1)S(1)} %get-tuple-element.30), channel_id=1, source_target_pairs={{0,4},{4,8},{8,12},{12,0},{1,5},{5,9},{9,13},{13,1},{2,6},{6,10},{... | collective-permute-start | bytes 393224 | tf_op jit(solution)/shard_map/slot4/ppermute | solution.py:306
  85.8 5.6 %collective-permute-start.25 = (bf16[64,1024]{1,0:T(8,128)(2,1)S(1)}, bf16[64,1024]{1,0:T(8,128)(2,1)S(1)}, u32[]{:S(2)}, u32[]{:S(2)}) collective-permute-start(bf16[64,1024]{1,0:T(8,128)(2,1)S(1)} %get-tuple-element.31), channel_id=1, source_target_pairs={{4,0},{8,4},{12,8},{0,12},{5,1},{9,5},{13,9},{1,13},{6,2},{10,6},{... | collective-permute-start | bytes 393224 | tf_op jit(solution)/shard_map/slot4/ppermute | solution.py:306
  89.9 2.2 %copy-start.18 = (bf16[64,1024]{1,0:T(8,128)(2,1)}, bf16[64,1024]{1,0:T(8,128)(2,1)S(1)}, u32[]{:S(2)}) copy-start(bf16[64,1024]{1,0:T(8,128)(2,1)S(1)} %collective-permute-done.24.refs_3_) | copy-start | bytes 393220
  91.4 0.8 copy-start.19
  91.4 1.3 %collective-permute-start.26 = (bf16[256,256]{1,0:T(8,128)(2,1)S(1)}, bf16[256,256]{1,0:T(8,128)(2,1)S(1)}, u32[]{:S(2)}, u32[]{:S(2)}) collective-permute-start(bf16[256,256]{1,0:T(8,128)(2,1)S(1)} %add_convert_fusion.mine), channel_id=1, source_target_pairs={{0,1},{1,0},{2,3},{3,2},{4,5},{5,4},{6,7},{7,6},{8,9},{9,8},{10,11... | collective-permute-start | bytes 393224 | tf_op jit(solution)/shard_map/ppermute | solution.py:112
  95.3 9.2 %collective-permute-start.28 = (bf16[128,1024]{1,0:T(8,128)(2,1)S(1)}, bf16[128,1024]{1,0:T(8,128)(2,1)S(1)}, u32[]{:S(2)}, u32[]{:S(2)}) collective-permute-start(bf16[128,1024]{1,0:T(8,128)(2,1)S(1)} %get-tuple-element.35), channel_id=1, source_target_pairs={{0,2},{2,0},{1,3},{3,1},{4,6},{6,4},{5,7},{7,5},{8,10},{10,8},{9,1... | collective-permute-start | bytes 786440 | tf_op jit(solution)/shard_map/ppermute | solution.py:332
  95.8 13.0 %collective-permute-start.27 = (bf16[128,1024]{1,0:T(8,128)(2,1)S(1)}, bf16[128,1024]{1,0:T(8,128)(2,1)S(1)}, u32[]{:S(2)}, u32[]{:S(2)}) collective-permute-start(bf16[128,1024]{1,0:T(8,128)(2,1)S(1)} %get-tuple-element.34), channel_id=1, source_target_pairs={{0,16},{16,0},{1,17},{17,1},{2,18},{18,2},{3,19},{19,3},{4,20},{20... | collective-permute-start | bytes 786440 | tf_op jit(solution)/shard_map/ppermute | solution.py:333
  98.0 12.3 %collective-permute-start.29 = (bf16[128,1024]{1,0:T(8,128)(2,1)S(1)}, bf16[128,1024]{1,0:T(8,128)(2,1)S(1)}, u32[]{:S(2)}, u32[]{:S(2)}) collective-permute-start(bf16[128,1024]{1,0:T(8,128)(2,1)S(1)} %get-tuple-element.36), channel_id=1, source_target_pairs={{0,18},{18,0},{2,16},{16,2},{1,19},{19,1},{3,17},{17,3},{4,22},{22... | collective-permute-start | bytes 786440 | tf_op jit(solution)/shard_map/ppermute | solution.py:331
  104.5 5.7 %collective-permute-start.31 = (bf16[4,4096]{1,0:T(4,128)(2,1)S(1)}, bf16[4,4096]{1,0:T(4,128)(2,1)S(1)}, u32[]{:S(2)}, u32[]{:S(2)}) collective-permute-start(bf16[4,4096]{1,0:T(4,128)(2,1)S(1)} %convert_element_type.64.refs_0_), channel_id=1, source_target_pairs={{0,4},{4,8},{8,12},{12,0},{5,1},{9,5},{13,9},{1,13},{2,6},{6,10},{... | collective-permute-start | bytes 98312 | tf_op jit(solution)/shard_map/ppermute | solution.py:355
  105.1 6.4 %collective-permute-start.33 = (bf16[4,4096]{1,0:T(4,128)(2,1)S(1)}, bf16[4,4096]{1,0:T(4,128)(2,1)S(1)}, u32[]{:S(2)}, u32[]{:S(2)}) collective-permute-start(bf16[4,4096]{1,0:T(4,128)(2,1)S(1)} %convert_element_type.64.refs_0_), channel_id=1, source_target_pairs={{0,8},{8,0},{4,12},{12,4},{1,9},{9,1},{5,13},{13,5},{2,10},{10,2},... | collective-permute-start | bytes 98312 | tf_op jit(solution)/shard_map/ppermute | solution.py:356
  110.2 1.2 %collective-permute-start.32 = (bf16[4,4096]{1,0:T(4,128)(2,1)S(1)}, bf16[4,4096]{1,0:T(4,128)(2,1)S(1)}, u32[]{:S(2)}, u32[]{:S(2)}) collective-permute-start(bf16[4,4096]{1,0:T(4,128)(2,1)S(1)} %collective-permute-done.31), channel_id=1, source_target_pairs={{0,1},{1,0},{2,3},{3,2},{4,5},{5,4},{6,7},{7,6},{8,9},{9,8},{10,11... | collective-permute-start | bytes 98312 | tf_op jit(solution)/shard_map/ppermute | solution.py:357
  110.3 3.2 %copy-start.11 = (bf16[1,128,4096]{2,1,0:T(8,128)(2,1)}, bf16[1,128,4096]{2,1,0:T(8,128)(2,1)S(1)}, u32[]{:S(2)}) copy-start(bf16[1,128,4096]{2,1,0:T(8,128)(2,1)S(1)} %bitcast_dynamic-update-slice_fusion) | copy-start | bytes 3145732
